TPU v7x, 128 devices: a whole 4x4x4 slice. The times are simulated.
128 devices in a mesh: view: 4 (over z), slab: 32 (over y, x, core).
Axes of the slice: x: 4, y: 4, z: 4, core: 2. Of those that a mesh axis runs over, the one named last changes fastest.
Arguments:
- estimate: float32 [1024, 128, 128], P('slab'), may hold values from 0.5 to 2
- recorded: float32 [8, 1024, 128, 128], P('view', 'slab'), may hold values from 0.5 to 2
- psf_taps: float32 [8, 3, 31], P('view'), may hold values from 0.02 to 1
- tile_map: int32 [8, 32, 32], P('view'), may hold values from 0 to 1023, as said below
Outputs:
- new_estimate: float32 [1024, 128, 128], P('slab')
Inputs may be any that keep to these rules, and one draw needn't show every extreme that they name: For each view, tile_map[v] is a bijection of the 1024 tiles. Each view slab a takes its 32 tiles from the world slabs thus: 2 tiles from world slab a itself, none from exactly one other, one from each of the rest.
All inputs are finite; a program needn't handle non-finite values.
Results may differ from a plain program's by a relative error of at most 0.0003.
Values sent between devices are 32-bit elements; how exact they have to be, the bound alone decides.
No kernel may reach another device: no remote copies, remote signals or barrier semaphores. Data moves between devices by JAX's collectives and lax.ppermute only.
A program may use at most 128 MiB of HBM per device.

v0:
```python
import jax
import jax.numpy as jnp
from jax import lax
from jax.sharding import PartitionSpec as P

CAP = 2


exact_mode = lax.Precision.HIGHEST


def padded_2(cells, sides, width):
    for axis, dim in sides:
        count = lax.axis_size(axis)
        ends = count - 1
        head = lax.slice_in_dim(cells, 0, width, axis=dim)
        tail = lax.slice_in_dim(cells, cells.shape[dim] - width, cells.shape[dim], axis=dim)
        cells = jnp.concatenate(
            [
                lax.ppermute(tail, axis, [(i, (i + 1) % count) for i in range(ends)]),
                cells,
                lax.ppermute(head, axis, [((i + 1) % count, i) for i in range(ends)]),
            ],
            axis=dim,
        )
    return cells


def combined_all(value, axis, join):
    pieces = lax.all_gather(value, axis)
    head = pieces[0]
    tail = pieces[1:]
    running, _ = lax.scan(lambda running, share: (join(running, share), None), head, tail)
    return running


def band_forward(weights, length):
    tap_count = weights.shape[1]
    half_width = tap_count // 2
    shape = (tap_count, length, length)
    tap_position = lax.broadcasted_iota(jnp.int32, shape, 0)
    source_position = lax.broadcasted_iota(jnp.int32, shape, 1)
    target_position = lax.broadcasted_iota(jnp.int32, shape, 2)
    hits = (source_position - target_position + half_width == tap_position).astype(jnp.float32)
    kernel = jnp.einsum("vt,tji->vji", weights, hits, precision=exact_mode)
    divisor = jnp.sum(kernel, axis=1)
    return kernel / divisor[:, None, :]


def depth_band(weights, depth_rows, adjoint):
    tap_count = weights.shape[1]
    half_width = tap_count // 2
    shape = (tap_count, depth_rows + 2 * half_width, depth_rows)
    tap_position = lax.broadcasted_iota(jnp.int32, shape, 0)
    padded_position = lax.broadcasted_iota(jnp.int32, shape, 1)
    target_position = lax.broadcasted_iota(jnp.int32, shape, 2)
    if adjoint:
        hits = target_position + 2 * half_width - padded_position == tap_position
    else:
        hits = padded_position - target_position == tap_position
    return jnp.einsum("vt,tki->vki", weights, hits.astype(jnp.float32), precision=exact_mode)


def depth_divisor(weights, depth_rows, own_slab, total_rows):
    tap_count = weights.shape[1]
    half_width = tap_count // 2
    row_numbers = own_slab * depth_rows + jnp.arange(depth_rows, dtype=jnp.int32)
    shifted = row_numbers[None, :] + jnp.arange(tap_count, dtype=jnp.int32)[:, None] - half_width
    inside = ((shifted >= 0) & (shifted < total_rows)).astype(jnp.float32)
    return jnp.einsum("vt,ti->vi", weights, inside, precision=exact_mode)


def pick_rows(arrays, indices):
    return jax.vmap(lambda table, chosen: table[chosen])(arrays, indices)


def multiply(first, second):
    return first * second


def local(estimate, recorded, psf_taps, tile_map):
    view_count = psf_taps.shape[0]
    tap_count = psf_taps.shape[2]
    half_width = tap_count // 2
    depth_rows, height_rows, width_rows = estimate.shape
    grid_size = lax.axis_size("slab")
    tile_rows = height_rows // grid_size
    own_slab = lax.axis_index("slab")
    weights = psf_taps / jnp.sum(psf_taps, axis=-1, keepdims=True)
    source_slab = tile_map // grid_size
    source_tile = tile_map % grid_size
    slab_range = jnp.arange(grid_size, dtype=jnp.int32)
    slot_range = jnp.arange(CAP, dtype=jnp.int32)
    same_source = (source_slab[..., None] == slab_range).astype(jnp.int32)
    earlier = jnp.cumsum(same_source, axis=2) - same_source
    slot_rank = jnp.sum(earlier * same_source, axis=3)
    own_source = lax.dynamic_index_in_dim(source_slab, own_slab, 1, keepdims=False)
    own_rank = lax.dynamic_index_in_dim(slot_rank, own_slab, 1, keepdims=False)
    world_tiles = estimate.reshape(depth_rows, grid_size, tile_rows, width_rows).transpose(
        1, 0, 2, 3
    )
    outgoing = (source_slab[:, :, None, :] == own_slab) & (
        slot_rank[:, :, None, :] == slot_range[None, None, :, None]
    )
    outgoing_count = outgoing.astype(jnp.int32)
    picked_tile = jnp.sum(outgoing_count * source_tile[:, :, None, :], axis=3)
    filled = jnp.sum(outgoing_count, axis=3).astype(jnp.float32)
    sending = world_tiles[picked_tile] * filled[..., None, None, None]
    arrived = lax.all_to_all(sending, "slab", split_axis=1, concat_axis=1, tiled=True)
    arrived_flat = arrived.reshape(view_count, grid_size * CAP, depth_rows, tile_rows, width_rows)
    view_tiles = pick_rows(arrived_flat, own_source * CAP + own_rank)
    viewed = view_tiles.transpose(0, 2, 1, 3, 4).reshape(
        view_count, depth_rows, height_rows, width_rows
    )
    total_rows = depth_rows * grid_size
    divisor = depth_divisor(weights[:, 0], depth_rows, own_slab, total_rows)
    height_band = band_forward(weights[:, 1], height_rows)
    width_band = band_forward(weights[:, 2], width_rows)
    padded = padded_2(viewed, (("slab", 1),), half_width)
    blurred = jnp.einsum(
        "vkyx,vki->viyx", padded, depth_band(weights[:, 0], depth_rows, False), precision=exact_mode
    )
    blurred = blurred / divisor[:, :, None, None]
    blurred = jnp.einsum("vzyx,vyk->vzkx", blurred, height_band, precision=exact_mode)
    blurred = jnp.einsum("vzyx,vxk->vzyk", blurred, width_band, precision=exact_mode)
    scaled = recorded / blurred / divisor[:, :, None, None]
    padded_ratio = padded_2(scaled, (("slab", 1),), half_width)
    adjoint_volume = jnp.einsum(
        "vkyx,vki->viyx",
        padded_ratio,
        depth_band(weights[:, 0], depth_rows, True),
        precision=exact_mode,
    )
    adjoint_volume = jnp.einsum("vzyx,vky->vzkx", adjoint_volume, height_band, precision=exact_mode)
    adjoint_volume = jnp.einsum("vzyx,vkx->vzyk", adjoint_volume, width_band, precision=exact_mode)
    back_tiles = adjoint_volume.reshape(
        view_count, depth_rows, grid_size, tile_rows, width_rows
    ).transpose(0, 2, 1, 3, 4)
    target_tiles = own_slab * grid_size + slab_range
    matches = (tile_map[:, None, :, :] == target_tiles[None, :, None, None]).astype(jnp.int32)
    from_slab = jnp.sum(matches * slab_range[None, None, :, None], axis=(2, 3))
    from_rank = jnp.sum(matches * slot_rank[:, None, :, :], axis=(2, 3))
    returning = (own_source[:, None, None, :] == slab_range[None, :, None, None]) & (
        own_rank[:, None, None, :] == slot_range[None, None, :, None]
    )
    returning_count = returning.astype(jnp.int32)
    chosen_tile = jnp.sum(returning_count * slab_range[None, None, None, :], axis=3)
    used_slots = jnp.sum(returning_count, axis=3).astype(jnp.float32)
    sending_back = pick_rows(back_tiles, chosen_tile.reshape(view_count, grid_size * CAP))
    sending_back = (
        sending_back.reshape(view_count, grid_size, CAP, depth_rows, tile_rows, width_rows)
        * used_slots[..., None, None, None]
    )
    returned = lax.all_to_all(sending_back, "slab", split_axis=1, concat_axis=1, tiled=True)
    returned_flat = returned.reshape(view_count, grid_size * CAP, depth_rows, tile_rows, width_rows)
    world_back = pick_rows(returned_flat, from_slab * CAP + from_rank)
    correction = world_back.transpose(0, 2, 1, 3, 4).reshape(
        view_count, depth_rows, height_rows, width_rows
    )
    local_product = jnp.prod(correction, axis=0)
    total_product = combined_all(local_product, "view", multiply)
    return estimate * total_product


def solution(mesh):
    in_specs = (
        P("slab", None, None),
        P("view", "slab", None, None),
        P("view", None, None),
        P("view", None, None),
    )
    out_specs = P("slab", None, None)
    return jax.shard_map(local, mesh=mesh, in_specs=in_specs, out_specs=out_specs, check_vma=False)
```

profile of v0, /device:TPU:1, one launch (start us, length us, event | category | flops | bytes accessed | tf_op | source)
XLA Modules:
  0.0 537.7 jit_solution(16190276397212863388)
XLA Ops:
  10.0 2.8 copy.124
  12.9 4.3 gather_fusion
  17.2 4.0 broadcast_multiply_fusion.1
  21.3 4.3 copy.134
  25.5 8.6 %all-to-all-start = ((f32[2,32,2,32,4,128]{5,3,4,2,0,1:T(8,128)}), f32[2,32,2,32,4,128]{5,3,4,2,0,1:T(8,128)}, u32[]{:S(2)}, u32[]{:S(2)}) async-start(f32[2,32,2,32,4,128]{5,3,4,2,0,1:T(8,128)} %copy.134), calls=%async_computation | async-start | bytes 16777216 | tf_op jit(solution)/shard_map/all_to_all | solution.py:109
  34.5 100.3 %all-to-all-done = f32[2,32,2,32,4,128]{5,3,4,2,0,1:T(8,128)} async-done(((f32[2,32,2,32,4,128]{5,3,4,2,0,1:T(8,128)}), f32[2,32,2,32,4,128]{5,3,4,2,0,1:T(8,128)}, u32[]{:S(2)}, u32[]{:S(2)}) %all-to-all-start) | async-done | bytes 8388640 | tf_op jit(solution)/shard_map/all_to_all | solution.py:109
  134.9 8.5 %copy.135 = f32[2,32,2,32,4,128]{5,3,4,2,1,0:T(8,128)} copy(f32[2,32,2,32,4,128]{5,3,4,2,0,1:T(8,128)} %all-to-all-done) | data formatting | bytes 16777216 | tf_op jit(solution)/shard_map/all_to_all | solution.py:109
  143.3 6.1 %gather_fusion.1 = f32[64,32,4,128]{3,1,2,0:T(8,128)} fusion(f32[2,64,32,4,128]{4,2,3,1,0:T(8,128)} %bitcast.80, s32[64]{0:T(128)S(1)} %reshape.181), kind=kCustom, calls=%fused_computation.1 | custom fusion | bytes 8389120 | tf_op jit(solution)/shard_map/vmap()/gather | solution.py:74
  156.9 7.8 %collective-permute-start.1 = (f32[2,15,128,128]{3,2,1,0:T(8,128)}, f32[2,15,128,128]{3,2,1,0:T(8,128)}, u32[]{:S(2)}, u32[]{:S(2)}) collective-permute-start(f32[2,15,128,128]{3,2,1,0:T(8,128)} %copy.137), channel_id=1, source_target_pairs={{1,0},{2,1},{3,2},{4,3},{5,4},{6,5},{7,6},{8,7},{9,8},{10,9},{11,1... | collective-permute-start | bytes 5898248 | tf_op jit(solution)/shard_map/ppermute | solution.py:22
  167.0 9.6 %collective-permute-done = f32[2,15,128,128]{3,2,1,0:T(8,128)} collective-permute-done((f32[2,15,128,128]{3,2,1,0:T(8,128)S(1)}, f32[2,15,128,128]{3,2,1,0:T(8,128)}, u32[]{:S(2)}, u32[]{:S(2)}) %collective-permute-start) | collective-permute-done | bytes 1966112 | tf_op jit(solution)/shard_map/ppermute | solution.py:20
  179.3 3.9 collective-permute-done.1
  185.8 5.5 %broadcast_divide_fusion = f32[2,32,128,128]{3,1,2,0:T(8,128)S(1)} fusion(f32[2,32]{1,0:T(2,128)S(1)} %fusion.56, f32[2,15,128,128]{3,1,2,0:T(8,128)S(1)} %copy.139, f32[2,32,128,128]{3,1,2,0:T(8,128)S(1)} %bitcast.83, f32[2,15,128,128]{3,1,2,0:T(8,128)S(1)} %copy.138, f32[2,62,32,1]{1,0,2,3:T(2,128)S(1)} %convolution_bitcast_fusion), kind=kOutput, calls=%fused_computation.32 | convolution fusion | flops 785252352 | bytes 12336896 | tf_op jit(solution)/shard_map/vkyx,vki->viyx/dot_general | solution.py:120
  191.3 6.3 %fusion.20 = f32[2,32,128,128]{3,2,1,0:T(8,128)S(1)} fusion(f32[2,32,128,128]{3,1,2,0:T(8,128)S(1)} %broadcast_divide_fusion, f32[2,128,128,1]{2,0,1,3:T(2,128)S(1)} %divide_bitcast_fusion.1), kind=kOutput, calls=%fused_computation.28 | convolution fusion | flops 1610612736 | bytes 8519680 | tf_op jit(solution)/shard_map/vzyx,vyk->vzkx/dot_general | solution.py:124
  197.7 10.4 %copy_divide_fusion = f32[2,32,128,128]{3,1,2,0:T(8,128)S(1)} fusion(f32[2,32,128,128]{3,2,1,0:T(8,128)S(1)} %copy-done.5, f32[2,32,128,128]{3,2,1,0:T(8,128)S(1)} %fusion.20, f32[2,32]{1,0:T(2,128)S(1)} %fusion.56, f32[2,128,128,1]{2,0,1,3:T(2,128)S(1)} %divide_bitcast_fusion), kind=kOutput, calls=%fused_computation.23 | convolution fusion | flops 1612709888 | bytes 12714240 | tf_op jit(solution)/shard_map/vzyx,vxk->vzyk/dot_general | solution.py:125
  214.3 3.7 collective-permute-start.3
  219.0 15.0 %collective-permute-done.2 = f32[2,15,128,128]{3,2,1,0:T(8,128)} collective-permute-done((f32[2,15,128,128]{3,2,1,0:T(8,128)S(1)}, f32[2,15,128,128]{3,2,1,0:T(8,128)}, u32[]{:S(2)}, u32[]{:S(2)}) %collective-permute-start.2) | collective-permute-done | bytes 1966112 | tf_op jit(solution)/shard_map/ppermute | solution.py:20
  236.7 3.9 collective-permute-done.3
  243.3 5.5 %fusion.6 = f32[2,32,128,128]{3,1,2,0:T(8,128)S(1)} fusion(f32[2,15,128,128]{3,1,2,0:T(8,128)S(1)} %copy.149, f32[2,32,128,128]{3,1,2,0:T(8,128)S(1)} %copy-done.1, f32[2,15,128,128]{3,1,2,0:T(8,128)S(1)} %copy.148, f32[2,62,32,1]{1,0,2,3:T(2,128)S(1)} %convolution_bitcast_fusion.1), kind=kOutput, calls=%fused_computation.11 | convolution fusion | flops 784203776 | bytes 12336640 | tf_op jit(solution)/shard_map/vkyx,vki->viyx/dot_general | solution.py:128
  248.7 6.5 %fusion.23 = f32[2,32,128,128]{3,2,1,0:T(8,128)S(1)} fusion(f32[2,32,128,128]{3,1,2,0:T(8,128)S(1)} %fusion.6, f32[2,128,128,1]{2,0,1,3:T(2,128)S(1)} %divide_bitcast_fusion.1), kind=kOutput, calls=%fused_computation.29 | convolution fusion | flops 1610612736 | bytes 8519680 | tf_op jit(solution)/shard_map/vzyx,vky->vzkx/dot_general | solution.py:134
  255.3 6.6 %fusion.14 = f32[2,32,128,128]{3,1,2,0:T(8,128)} fusion(f32[2,32,128,128]{3,2,1,0:T(8,128)S(1)} %fusion.23, f32[2,128,128,1]{2,0,1,3:T(2,128)S(1)} %divide_bitcast_fusion), kind=kOutput, calls=%fused_computation.19 | convolution fusion | flops 1610612736 | bytes 8519680 | tf_op jit(solution)/shard_map/vzyx,vkx->vzyk/dot_general | solution.py:135
  261.9 6.5 %gather_fusion.2 = f32[128,32,4,128]{3,1,2,0:T(8,128)} fusion(f32[2,32,32,4,128]{4,2,3,1,0:T(8,128)} %bitcast.77, s32[128]{0:T(128)S(1)} %reshape.187), kind=kCustom, calls=%fused_computation.2 | custom fusion | bytes 16778240 | tf_op jit(solution)/shard_map/vmap()/gather | solution.py:74
  268.4 7.2 %broadcast_multiply_fusion = f32[2,32,2,32,4,128]{5,3,4,2,1,0:T(8,128)} fusion(f32[2,32,2,32,4,128]{5,3,4,2,1,0:T(8,128)} %bitcast.79, f32[2,32,2]{2,1,0:T(8,128)S(1)} %copy.156), kind=kLoop, calls=%fused_computation.26 | loop fusion | flops 2097152 | bytes 16777728 | tf_op jit(solution)/shard_map/mul | solution.py:151
  275.6 14.9 %copy.157 = f32[2,32,2,32,4,128]{5,4,3,2,0,1:T(4,128)} copy(f32[2,32,2,32,4,128]{5,3,4,2,1,0:T(8,128)} %broadcast_multiply_fusion) | data formatting | bytes 16777216 | tf_op jit(solution)/shard_map/mul | solution.py:151
  290.5 14.2 %all-to-all-start.1 = ((f32[2,32,2,32,4,128]{5,4,3,2,0,1:T(4,128)}), f32[2,32,2,32,4,128]{5,4,3,2,0,1:T(4,128)}, u32[]{:S(2)}, u32[]{:S(2)}) async-start(f32[2,32,2,32,4,128]{5,4,3,2,0,1:T(4,128)} %copy.157), calls=%async_computation.1 | async-start | bytes 16777216 | tf_op jit(solution)/shard_map/all_to_all | solution.py:154
  305.4 99.9 %all-to-all-done.1 = f32[2,32,2,32,4,128]{5,4,3,2,0,1:T(4,128)} async-done(((f32[2,32,2,32,4,128]{5,4,3,2,0,1:T(4,128)}), f32[2,32,2,32,4,128]{5,4,3,2,0,1:T(4,128)}, u32[]{:S(2)}, u32[]{:S(2)}) %all-to-all-start.1) | async-done | bytes 8388640 | tf_op jit(solution)/shard_map/all_to_all | solution.py:154
  405.3 7.7 %copy.158 = f32[2,32,2,32,4,128]{5,3,4,2,1,0:T(8,128)} copy(f32[2,32,2,32,4,128]{5,4,3,2,0,1:T(4,128)} %all-to-all-done.1) | data formatting | bytes 16777216 | tf_op jit(solution)/shard_map/all_to_all | solution.py:154
  413.1 6.1 %gather_fusion.3 = f32[64,32,4,128]{3,1,2,0:T(8,128)} fusion(f32[2,64,32,4,128]{4,2,3,1,0:T(8,128)} %bitcast.81, s32[64]{0:T(128)S(1)} %reshape.193), kind=kCustom, calls=%fused_computation.3 | custom fusion | bytes 8389120 | tf_op jit(solution)/shard_map/vmap()/gather | solution.py:74
  419.2 2.9 reduce_prod.11
  426.7 86.3 %all-gather.2.cloned.1.call-done = f32[4,32,128,128]{3,2,1,0:T(8,128)} async-done(((f32[1,32,128,128]{3,2,1,0:T(8,128)}), f32[4,32,128,128]{3,2,1,0:T(8,128)}) %all-gather.2.cloned.1.call-update) | async-done | bytes 8388624 | tf_op jit(solution)/shard_map/all_gather | solution.py:30
  513.0 6.3 %slice.54 = f32[3,32,128,128]{3,2,1,0:T(8,128)} slice(f32[4,32,128,128]{3,2,1,0:T(8,128)} %all-gather.2.cloned.1.call-done), slice={[1:4], [0:32], [0:128], [0:128]} | slice | bytes 12582912 | tf_op jit(solution)/shard_map/slice | solution.py:32
  521.0 6.4 %while.10 = (s32[]{:T(128)}, f32[32,128,128]{2,1,0:T(8,128)S(1)}, f32[3,32,128,128]{3,2,1,0:T(8,128)}, s32[]{:T(128)}) while((s32[]{:T(128)}, f32[32,128,128]{2,1,0:T(8,128)S(1)}, f32[3,32,128,128]{3,2,1,0:T(8,128)}, s32[]{:T(128)}) %tuple.28), condition=%wide.region_13.14_spmd, body=%wide.region_12.13_spmd.sunk | while | flops 524290 | bytes 6291513 | solution.py:33
  527.5 3.2 mul.99
  (73 shorter events, 45.0 us)
Async XLA Ops:
  25.5 109.3 %all-to-all-start = ((f32[2,32,2,32,4,128]{5,3,4,2,0,1:T(8,128)}), f32[2,32,2,32,4,128]{5,3,4,2,0,1:T(8,128)}, u32[]{:S(2)}, u32[]{:S(2)}) async-start(f32[2,32,2,32,4,128]{5,3,4,2,0,1:T(8,128)} %copy.134), calls=%async_computation | async-start | bytes 16777216 | tf_op jit(solution)/shard_map/all_to_all | solution.py:109
  152.1 12.6 %copy-start.4 = (f32[2,3,31]{2,0,1:T(2,128)S(1)}, f32[2,3,31]{2,0,1:T(2,128)}, u32[]{:S(2)}) copy-start(f32[2,3,31]{2,0,1:T(2,128)} %param.8) | copy-start | bytes 2236
  152.7 23.9 %collective-permute-start = (f32[2,15,128,128]{3,2,1,0:T(8,128)S(1)}, f32[2,15,128,128]{3,2,1,0:T(8,128)}, u32[]{:S(2)}, u32[]{:S(2)}) collective-permute-start(f32[2,15,128,128]{3,2,1,0:T(8,128)S(1)} %copy.136), channel_id=1, source_target_pairs={{0,1},{1,2},{2,3},{3,4},{4,5},{5,6},{6,7},{7,8},{8,9},{9,10},{10,1... | collective-permute-start | bytes 5898248 | tf_op jit(solution)/shard_map/ppermute | solution.py:20
  156.9 26.3 %collective-permute-start.1 = (f32[2,15,128,128]{3,2,1,0:T(8,128)}, f32[2,15,128,128]{3,2,1,0:T(8,128)}, u32[]{:S(2)}, u32[]{:S(2)}) collective-permute-start(f32[2,15,128,128]{3,2,1,0:T(8,128)} %copy.137), channel_id=1, source_target_pairs={{1,0},{2,1},{3,2},{4,3},{5,4},{6,5},{7,6},{8,7},{9,8},{10,9},{11,1... | collective-permute-start | bytes 5898248 | tf_op jit(solution)/shard_map/ppermute | solution.py:22
  166.9 18.9 %copy-start.2 = (f32[64,32,4,128]{3,1,2,0:T(8,128)S(1)}, f32[64,32,4,128]{3,1,2,0:T(8,128)}, u32[]{:S(2)}) copy-start(f32[64,32,4,128]{3,1,2,0:T(8,128)} %gather_fusion.1) | copy-start | bytes 12582916
  191.3 6.3 %copy-start.5 = (f32[2,32,128,128]{3,2,1,0:T(8,128)S(1)}, f32[2,32,128,128]{3,2,1,0:T(8,128)}, u32[]{:S(2)}) copy-start(f32[2,32,128,128]{3,2,1,0:T(8,128)} %param.7) | copy-start | bytes 12582916
  208.0 1.9 copy-start
  210.5 23.5 %collective-permute-start.2 = (f32[2,15,128,128]{3,2,1,0:T(8,128)S(1)}, f32[2,15,128,128]{3,2,1,0:T(8,128)}, u32[]{:S(2)}, u32[]{:S(2)}) collective-permute-start(f32[2,15,128,128]{3,2,1,0:T(8,128)S(1)} %copy.146), channel_id=1, source_target_pairs={{0,1},{1,2},{2,3},{3,4},{4,5},{5,6},{6,7},{7,8},{8,9},{9,10},{10,1... | collective-permute-start | bytes 5898248 | tf_op jit(solution)/shard_map/ppermute | solution.py:20
  214.3 26.3 %collective-permute-start.3 = (f32[2,15,128,128]{3,2,1,0:T(8,128)}, f32[2,15,128,128]{3,2,1,0:T(8,128)}, u32[]{:S(2)}, u32[]{:S(2)}) collective-permute-start(f32[2,15,128,128]{3,2,1,0:T(8,128)} %copy.147), channel_id=1, source_target_pairs={{1,0},{2,1},{3,2},{4,3},{5,4},{6,5},{7,6},{8,7},{9,8},{10,9},{11,1... | collective-permute-start | bytes 5898248 | tf_op jit(solution)/shard_map/ppermute | solution.py:22
  218.6 24.6 %copy-start.1 = (f32[2,32,128,128]{3,1,2,0:T(8,128)S(1)}, f32[2,32,128,128]{3,1,2,0:T(8,128)}, u32[]{:S(2)}) copy-start(f32[2,32,128,128]{3,1,2,0:T(8,128)} %copy-done) | copy-start | bytes 12582916
  290.5 14.4 %copy-start.3 = (s32[2,32,32]{2,1,0:T(8,128)S(1)}, s32[2,32,32]{2,1,0:T(8,128)}, u32[]{:S(2)}) copy-start(s32[2,32,32]{2,1,0:T(8,128)} %param.9) | copy-start | bytes 24580
  290.5 114.9 %all-to-all-start.1 = ((f32[2,32,2,32,4,128]{5,4,3,2,0,1:T(4,128)}), f32[2,32,2,32,4,128]{5,4,3,2,0,1:T(4,128)}, u32[]{:S(2)}, u32[]{:S(2)}) async-start(f32[2,32,2,32,4,128]{5,4,3,2,0,1:T(4,128)} %copy.157), calls=%async_computation.1 | async-start | bytes 16777216 | tf_op jit(solution)/shard_map/all_to_all | solution.py:154
  304.6 208.3 %all-gather.2.cloned.1.call-start = ((), (), s32[]{:S(2)}) async-start(), calls=%async_computation.2 | async-start | bytes 10485760 | tf_op jit(solution)/shard_map/all_gather | solution.py:30
Sparse Core Ops, SparseCore 0:
  426.8 86.1 all-gather.1
where the time goes:
time: 545 us; the launch traced here: 538 us
  waiting for transfers between devices  319 us (59%)
  local copies, waits for them, and re-layouts  96 us (18%)
  matrix products  43.1 us (8%)
  starting transfers between devices  38.7 us (7%)
  other arithmetic  27.1 us (5%)
  between operations  13.9 us (3%)
    all_to_all x1, waiting for transfers between devices, local(): lax.all_to_all(sending, 'slab', split_axis=1, concat_axis=1, tiled=True)  100 us
    all_to_all x1, waiting for transfers between devices, local(): lax.all_to_all(sending_back, 'slab', split_axis=1, concat_axis=1, tiled=T...  99.9 us
    all_gather x1, waiting for transfers between devices, combined_all(): pieces = lax.all_gather(value, axis)  86.3 us
    ppermute x2, waiting for transfers between devices, padded_2(): lax.ppermute(tail, axis, [(i, (i + 1) % count) for i in range(ends)])  24.6 us
    gather x6, local copies, waits for them, and re-layouts, pick_rows(): return jax.vmap(lambda table, chosen: table[chosen])(arrays, indices)  19 us
    mul x1, local copies, waits for them, and re-layouts, local(): sending_back.reshape(view_count, grid_size, CAP, depth_rows, tile_rows, w...  14.9 us
    all_to_all x1, starting transfers between devices, local(): lax.all_to_all(sending_back, 'slab', split_axis=1, concat_axis=1, tiled=T...  14.2 us
    ppermute x2, starting transfers between devices, padded_2(): lax.ppermute(head, axis, [((i + 1) % count, i) for i in range(ends)])  11.5 us
  transfers between devices with their start and end apart: 7, of which 7 were waited for; matrix products, arithmetic and copies ran while one was open for 2% of the time, Pallas kernels for 0%

commit v1 on v0

v1 whole, which is shorter than its diff:
```python
import functools

import jax
import jax.numpy as jnp
from jax import lax
from jax.experimental import pallas as pl
from jax.experimental.pallas import tpu as pltpu
from jax.sharding import PartitionSpec as P

TAPS = 31
HALF = 15
ZD = 32
YT = 4
NX = 128
GRID = 32
NY = 128
PAD = 16
NPAD = ZD + 2 * PAD
TILE = YT * ZD
PLANES = 4
CHUNKS = ((0, 2), (2, 4))

F32 = jnp.float32
BF16 = jnp.bfloat16
VMEM = pl.BlockSpec(memory_space=pltpu.VMEM)
SMEM = pl.BlockSpec(memory_space=pltpu.SMEM)


def call(kernel, outs, name, scratch=(), flops=0, moved=0):
    def run(*operands):
        in_specs = [SMEM if jnp.issubdtype(o.dtype, jnp.integer) else VMEM for o in operands]
        return pl.pallas_call(
            kernel,
            out_shape=[jax.ShapeDtypeStruct(s, F32) for s in outs],
            in_specs=in_specs,
            out_specs=[VMEM] * len(outs),
            scratch_shapes=list(scratch),
            name=name,
            cost_estimate=pl.CostEstimate(flops=flops, bytes_accessed=moved, transcendentals=0),
            compiler_params=pltpu.CompilerParams(vmem_limit_bytes=48 << 20),
        )(*operands)

    return run


def halves(x):
    high = x.astype(BF16)
    low = (x - high.astype(F32)).astype(BF16)
    return high, low


def dot(a, b):
    return jnp.dot(a, b, preferred_element_type=F32)


def left_dot(matrix, x):
    high, low = halves(x)
    full = dot(matrix, jnp.concatenate([high, low], axis=0))
    rows = full.shape[0] // 2
    return full[:rows] + full[rows:]


def right_dot(x, matrix):
    high, low = halves(x)
    full = dot(jnp.concatenate([high, low], axis=1), matrix)
    return full[:, :NX] + full[:, NX:]


def pack_kernel(table, est, send, kept):
    def move(tile, ref, slot):
        for j in range(YT):
            ref[slot, pl.ds(j * ZD, ZD), :] = est[pl.ds(tile * YT + j, ZD, stride=NY), :]

    def step(slot, carry):
        move(table[slot], send, slot)
        return carry

    lax.fori_loop(0, GRID, step, 0)
    move(table[GRID], kept, 0)


def unpack_kernel(table, recv, kept, low, high):
    def put(source, c):
        for j in range(YT):
            at = pl.multiple_of((c * YT + j) * PAD, PAD)
            low[pl.ds(at, PAD), :] = source[pl.ds(j * ZD, PAD), :]
            high[pl.ds(at, PAD), :] = source[pl.ds(j * ZD + PAD, PAD), :]

    def step(c, carry):
        slot = table[c]

        @pl.when(slot < GRID)
        def _():
            put(recv.at[slot], c)

        @pl.when(slot == GRID)
        def _():
            put(kept.at[0], c)

        return carry

    lax.fori_loop(0, GRID, step, 0)


def padded_pair(parts, first, second):
    columns = []
    for y in (first, second):
        at = pl.multiple_of(y * PAD, PAD)
        columns.append(jnp.concatenate([p[pl.ds(at, PAD), :] for p in parts], axis=0))
    return jnp.concatenate(columns, axis=1)


def blur_kernel(top, low, high, bottom, rec, zmat, xmat, ymat, ymat_t, xmat_t, out_low, out_high, work):
    parts = (top, low, high, bottom)

    def forward(group, carry):
        rows = []
        for pair in range(2):
            y = group * 4 + pair * 2
            blurred = left_dot(zmat[...], padded_pair(parts, y, y + 1))
            rows += [blurred[:, :NX], blurred[:, NX:]]
        done = right_dot(jnp.concatenate(rows, axis=0), xmat[...])
        work[pl.ds(pl.multiple_of(group * 4 * ZD, 4 * ZD), 4 * ZD), :] = done
        return carry

    lax.fori_loop(0, NY // 4, forward, 0)

    for base, out in ((0, out_low), (PAD, out_high)):

        def backward(step, carry, base=base, out=out):
            zz = step * 2
            z = base + zz
            x = jnp.concatenate([work[pl.ds(z + i, NY, stride=ZD), :] for i in range(2)], axis=1)
            seen = jnp.concatenate(
                [rec[pl.ds(pl.multiple_of((z + i) * NY, NY), NY), :] for i in range(2)], axis=1
            )
            ratio = seen / left_dot(ymat[...], x)
            back = left_dot(ymat_t[...], ratio)
            back = right_dot(jnp.concatenate([back[:, :NX], back[:, NX:]], axis=0), xmat_t[...])
            for i in range(2):
                out[pl.ds(zz + i, NY, stride=PAD), :] = back[i * NY : (i + 1) * NY]
            return carry

        lax.fori_loop(0, PAD // 2, backward, 0)


def adjoint_kernel(first, last, table, top, low, high, bottom, zmat, send, kept):
    parts = (top, low, high, bottom)

    def move(c, ref, slot):
        for j in range(first, last, 2):
            y = c * YT + j
            done = left_dot(zmat[...], padded_pair(parts, y, y + 1))
            at = (j - first) * ZD
            ref[slot, pl.ds(at, ZD), :] = done[:, :NX]
            ref[slot, pl.ds(at + ZD, ZD), :] = done[:, NX:]

    def step(slot, carry):
        move(table[slot], send, slot)
        return carry

    lax.fori_loop(0, GRID, step, 0)
    move(table[GRID], kept, 0)


def product_kernel(table0, table1, recv0, recv1, kept0, kept1, out):
    def step(t, carry):
        s0 = table0[t]
        s1 = table1[t]
        out[t] = recv0[jnp.minimum(s0, GRID - 1)] * recv1[jnp.minimum(s1, GRID - 1)]

        @pl.when((s0 == GRID) & (s1 < GRID))
        def _():
            out[t] = kept0[0] * recv1[s1]

        @pl.when((s1 == GRID) & (s0 < GRID))
        def _():
            out[t] = recv0[s0] * kept1[0]

        @pl.when((s1 == GRID) & (s0 == GRID))
        def _():
            out[t] = kept0[0] * kept1[0]

        return carry

    lax.fori_loop(0, GRID, step, 0)


def quarter_kernel(arrived, out):
    out[...] = (arrived[0] * arrived[1]) * (arrived[2] * arrived[3])


def final_kernel(place, est, *refs):
    out = refs[-1]
    pieces = refs[:-1]
    quarter = GRID // PLANES
    for chunk, (first, last) in enumerate(CHUNKS):
        for hop in range(PLANES):
            piece = pieces[chunk * PLANES + hop]
            base = place[hop] * quarter

            def step(t, carry, piece=piece, base=base, first=first, last=last):
                for j in range(first, last):
                    rows = pl.ds((base + t) * YT + j, ZD, stride=NY)
                    out[rows, :] = est[rows, :] * piece[t, pl.ds((j - first) * ZD, ZD), :]
                return carry

            lax.fori_loop(0, quarter, step, 0)


def stacked(matrix, axis):
    high = lax.reduce_precision(matrix, 8, 7)
    low = matrix - high
    if axis == 0:
        both = jnp.concatenate([high, low], axis=-2)
        return jnp.concatenate([both, both], axis=-1).astype(BF16)
    both = jnp.concatenate([high, low], axis=-1)
    return jnp.concatenate([both, both], axis=-2).astype(BF16)


def band(weights, positions):
    taps = jnp.arange(TAPS, dtype=jnp.int32)[None, :, None, None]
    return jnp.sum(jnp.where(positions[None, None] == taps, weights[:, :, None, None], 0.0), axis=1)


def bands(psf_taps, own):
    weights = psf_taps / jnp.sum(psf_taps, axis=-1, keepdims=True)
    i = jnp.arange(NX, dtype=jnp.int32)
    plain = band(weights[:, 1:].reshape(-1, TAPS), i[:, None] - i[None, :] + HALF)
    plain = plain / jnp.sum(plain, axis=1, keepdims=True)
    plain = plain.reshape(-1, 2, NX, NX)
    turned = plain.transpose(0, 1, 3, 2)
    ymat, xmat = turned[:, 0], plain[:, 1]
    ymat_t, xmat_t = plain[:, 0], turned[:, 1]

    wz = weights[:, 0]
    rows = own * ZD + jnp.arange(NPAD, dtype=jnp.int32) - PAD
    reach = rows[None, :] + jnp.arange(TAPS, dtype=jnp.int32)[:, None] - HALF
    inside = (reach >= 0) & (reach < GRID * ZD)
    divisor = jnp.sum(jnp.where(inside[None], wz[:, :, None], 0.0), axis=1)
    divisor = jnp.where((rows >= 0) & (rows < GRID * ZD), divisor, 1.0)
    k = jnp.arange(NPAD, dtype=jnp.int32)[None, :]
    o = jnp.arange(ZD, dtype=jnp.int32)[:, None]
    zmat = band(wz, k - o - 1) / divisor[:, PAD : PAD + ZD, None]
    zmat_t = band(wz, o - k + 2 * PAD - 1) / divisor[:, None, :]
    return (
        stacked(zmat, 0),
        stacked(xmat, 1),
        stacked(ymat, 0),
        stacked(ymat_t, 0),
        stacked(xmat_t, 1),
        stacked(zmat_t, 0),
    )


def tables(tile_map, own):
    source = tile_map // GRID
    tile = tile_map % GRID
    c = jnp.arange(GRID, dtype=jnp.int32)
    slots = jnp.arange(GRID + 1, dtype=jnp.int32)
    own_source = lax.dynamic_index_in_dim(source, own, 1, keepdims=False)
    own_tile = lax.dynamic_index_in_dim(tile, own, 1, keepdims=False)
    mine = own_source == own
    earlier = mine[:, None, :] & (c[None, :] < c[:, None])[None]
    second = mine & jnp.any(earlier, axis=2)
    second_at = second[:, None, :] & (c == own)[None, :, None]
    outgoing = (source == own) & ~second_at
    pack = jnp.sum(jnp.where(outgoing, tile, 0), axis=2)
    last = jnp.sum(jnp.where(second, own_tile, 0), axis=1, keepdims=True)
    pack = jnp.concatenate([pack, last], axis=1)
    place = jnp.where(second, GRID, own_source)
    chosen = jnp.sum(jnp.where(place[:, None, :] == slots[None, :, None], c[None, None, :], 0), axis=2)
    value = jnp.where(second_at, GRID, c[None, :, None])
    wanted = (own * GRID + c)[None, :, None, None] == tile_map[:, None]
    arriving = jnp.sum(jnp.where(wanted, value[:, None], 0), axis=(2, 3))
    return pack, place, chosen, arriving


def shifted(value, axis, hop, ring):
    count = lax.axis_size(axis)
    pairs = [(i, (i + hop) % count) for i in range(count) if ring or 0 <= i + hop < count]
    return lax.ppermute(value, axis, pairs)


def local(estimate, recorded, psf_taps, tile_map):
    own = lax.axis_index("slab")
    plane = lax.axis_index("view")
    pack, place, chosen, arriving = tables(tile_map, own)
    mats = bands(psf_taps, own)
    est = estimate.reshape(ZD * NY, NX)
    rec = recorded.reshape(-1, ZD * NY, NX)
    views = rec.shape[0]
    buffer = (GRID, TILE, NX)
    strip = (NY * PAD, NX)
    big = TILE * NX * 4 * GRID

    sent = [
        call(pack_kernel, (buffer, (1, TILE, NX)), "pack", moved=2 * big)(pack[v], est)
        for v in range(views)
    ]
    returned = [[] for _ in CHUNKS]
    for v in range(views):
        send, kept = sent[v]
        recv = lax.all_to_all(send, "slab", 0, 0, tiled=True)
        low, high = call(unpack_kernel, (strip, strip), "unpack", moved=2 * big)(place[v], recv, kept)
        top = shifted(high, "slab", 1, False)
        bottom = shifted(low, "slab", -1, False)
        low, high = call(
            blur_kernel,
            (strip, strip),
            "blur",
            scratch=[pltpu.VMEM((NY * ZD, NX), F32)],
            flops=10 << 30,
            moved=4 * big,
        )(top, low, high, bottom, rec[v], *[m[v] for m in mats[:5]])
        top = shifted(high, "slab", 1, False)
        bottom = shifted(low, "slab", -1, False)
        for n, (first, last) in enumerate(CHUNKS):
            rows = (last - first) * ZD
            send, kept = call(
                functools.partial(adjoint_kernel, first, last),
                ((GRID, rows, NX), (1, rows, NX)),
                "adjoint",
                flops=1 << 30,
                moved=2 * big,
            )(chosen[v], top, low, high, bottom, mats[5][v])
            returned[n].append((send, kept))
    pieces = []
    for n, (first, last) in enumerate(CHUNKS):
        rows = (last - first) * ZD
        back = [lax.all_to_all(send, "slab", 0, 0, tiled=True) for send, _ in returned[n]]
        (product,) = call(product_kernel, ((GRID, rows, NX),), "product", moved=2 * big)(
            arriving[0], arriving[1], *back, *[kept for _, kept in returned[n]]
        )
        spread = lax.all_to_all(product, "view", 0, 0, tiled=True)
        quarter = GRID // PLANES
        (mine,) = call(quarter_kernel, ((quarter, rows, NX),), "quarter", moved=big)(
            spread.reshape(PLANES, quarter, rows, NX)
        )
        pieces += [mine] + [shifted(mine, "view", hop, True) for hop in range(1, PLANES)]
    where = (plane - jnp.arange(PLANES, dtype=jnp.int32)) % PLANES
    (out,) = call(final_kernel, ((ZD * NY, NX),), "final", moved=3 * big)(where, est, *pieces)
    return out.reshape(estimate.shape)


def solution(mesh):
    in_specs = (
        P("slab", None, None),
        P("view", "slab", None, None),
        P("view", None, None),
        P("view", None, None),
    )
    out_specs = P("slab", None, None)
    return jax.shard_map(local, mesh=mesh, in_specs=in_specs, out_specs=out_specs, check_vma=False)
```

time: 545 us -> 319 us (0.59)
  waiting for transfers between devices: 319 us -> 112 us
  Pallas kernels: 0 us -> 92.3 us
  local copies, waits for them, and re-layouts: 96 us -> 23.1 us
  matrix products: 43.1 us -> 0 us
  starting transfers between devices: 38.7 us -> 78 us
  other arithmetic: 27.1 us -> 9.5 us
  between operations: 13.9 us -> 0.77 us
    all_to_all x2 -> x8, waiting for transfers between devices: 200 us -> 93.7 us  [the longest x4 38.5 us: local(): lax.all_to_all(send, 'slab', 0, 0, tiled=True)]
    pallas_call x0 -> x15, Pallas kernels: none -> 92.3 us  [run(): pl.pallas_call(kernel, out_shape=[jax.ShapeDtypeStruct(s, F32) for s in o...]
    all_gather x1 -> x0, waiting for transfers between devices: 86.3 us -> none  [combined_all(): pieces = lax.all_gather(value, axis)]
    dot_general x11 -> x0, matrix products: 43.1 us -> none  [the longest x1 10.4 us: local(): jnp.einsum('vzyx,vxk->vzyk', blurred, width_band, precision=exact_mode)]
    all_to_all x2 -> x8, starting transfers between devices: 22.8 us -> 48.7 us  [the longest x4 24.5 us: local(): lax.all_to_all(send, 'slab', 0, 0, tiled=True)]
    gather x7 -> x0, local copies, waits for them, and re-layouts: 23.3 us -> none  [the longest x6 19 us: pick_rows(): return jax.vmap(lambda table, chosen: table[chosen])(arrays, indices)]
    mul x6 -> x0, other arithmetic: 20.8 us -> none  [the longest x1 7.22 us: local(): sending_back.reshape(view_count, grid_size, CAP, depth_rows, tile_rows, w...]
    mul x2 -> x0, local copies, waits for them, and re-layouts: 19.1 us -> none  [the longest x1 14.9 us: local(): sending_back.reshape(view_count, grid_size, CAP, depth_rows, tile_rows, w...]
  transfers between devices with their start and end apart: 7 -> 22, of which waited for: 7 -> 12; matrix products, arithmetic and copies ran while one was open for 2% -> 4% of each run, Pallas kernels for 0% -> 27%
where the time goes in v1:
time: 319 us; the launch traced here: 316 us
  waiting for transfers between devices  112 us (35%)
  Pallas kernels  92.3 us (29%)
  starting transfers between devices  78 us (24%)
  local copies, waits for them, and re-layouts  23.1 us (7%)
  other arithmetic  9.5 us (3%)
    pallas_call x15, Pallas kernels, run(): pl.pallas_call(kernel, out_shape=[jax.ShapeDtypeStruct(s, F32) for s in o...  92.3 us
    all_to_all x4, waiting for transfers between devices, local(): lax.all_to_all(send, 'slab', 0, 0, tiled=True)  38.5 us
    all_to_all x2, waiting for transfers between devices, local(): recv = lax.all_to_all(send, 'slab', 0, 0, tiled=True)  36.3 us
    ppermute x14, starting transfers between devices, shifted(): return lax.ppermute(value, axis, pairs)  29.3 us
    all_to_all x4, starting transfers between devices, local(): lax.all_to_all(send, 'slab', 0, 0, tiled=True)  24.5 us
    all_to_all x2, waiting for transfers between devices, local(): spread = lax.all_to_all(product, 'view', 0, 0, tiled=True)  18.9 us
    ppermute x14, waiting for transfers between devices, shifted(): return lax.ppermute(value, axis, pairs)  18.5 us
    unnamed x62, local copies, waits for them, and re-layouts  18.4 us
  transfers between devices with their start and end apart: 22, of which 12 were waited for; matrix products, arithmetic and copies ran while one was open for 4% of the time, Pallas kernels for 27%

profile of v1, /device:TPU:1, one launch (start us, length us, event | category | flops | bytes accessed | tf_op | source)
XLA Modules:
  0.0 315.9 jit_solution(6147330124542415870)
XLA Ops:
  7.9 8.8 %all-to-all-start = ((f32[32,128,128]{2,1,0:T(8,128)}), f32[32,128,128]{2,1,0:T(8,128)}, u32[]{:S(2)}, u32[]{:S(2)}) async-start(f32[32,128,128]{2,1,0:T(8,128)} %copy-done.13), calls=%async_computation | async-start | bytes 4194304 | tf_op jit(solution)/shard_map/all_to_all | solution.py:304
  23.6 21.8 %all-to-all-done.recv = f32[32,128,128]{2,1,0:T(8,128)} async-done(((f32[32,128,128]{2,1,0:T(8,128)}), f32[32,128,128]{2,1,0:T(8,128)}, u32[]{:S(2)}, u32[]{:S(2)}) %all-to-all-start) | async-done | bytes 2097184 | tf_op jit(solution)/shard_map/all_to_all | solution.py:304
  45.4 6.0 %all-to-all-start.2 = ((f32[32,128,128]{2,1,0:T(8,128)}), f32[32,128,128]{2,1,0:T(8,128)}, u32[]{:S(2)}, u32[]{:S(2)}) async-start(f32[32,128,128]{2,1,0:T(8,128)} %copy-done.12), calls=%async_computation.2 | async-start | bytes 4194304 | tf_op jit(solution)/shard_map/all_to_all | solution.py:304
  51.6 3.8 %unpack.2 = (f32[2048,128]{1,0:T(8,128)}, f32[2048,128]{1,0:T(8,128)}) custom-call(s32[32]{0:T(128)S(1)} %get-tuple-element.82.table, f32[32,128,128]{2,1,0:T(8,128)} %all-to-all-done.recv, f32[1,128,128]{2,1,0:T(8,128)S(1)} %get-tuple-element.26.kept), custom_call_target="tpu_custom_call" | custom-call | bytes 4194304 | tf_op jit(solution)/shard_map/unpack/pallas_call | solution.py:32
  55.4 3.5 %collective-permute-start = (f32[2048,128]{1,0:T(8,128)}, f32[2048,128]{1,0:T(8,128)}, u32[]{:S(2)}, u32[]{:S(2)}) collective-permute-start(f32[2048,128]{1,0:T(8,128)} %get-tuple-element.27.high), channel_id=1, source_target_pairs={{0,1},{1,2},{2,3},{3,4},{4,5},{5,6},{6,7},{7,8},{8,9},{9,10},{10,1... | collective-permute-start | bytes 3145736 | tf_op jit(solution)/shard_map/ppermute | solution.py:282
  65.5 14.6 %all-to-all-done.2.recv = f32[32,128,128]{2,1,0:T(8,128)} async-done(((f32[32,128,128]{2,1,0:T(8,128)}), f32[32,128,128]{2,1,0:T(8,128)}, u32[]{:S(2)}, u32[]{:S(2)}) %all-to-all-start.2) | async-done | bytes 2097184 | tf_op jit(solution)/shard_map/all_to_all | solution.py:304
  80.1 3.6 %unpack.3 = (f32[2048,128]{1,0:T(8,128)}, f32[2048,128]{1,0:T(8,128)}) custom-call(s32[32]{0:T(128)S(1)} %get-tuple-element.81.table, f32[32,128,128]{2,1,0:T(8,128)} %all-to-all-done.2.recv, f32[1,128,128]{2,1,0:T(8,128)S(1)} %get-tuple-element.33.kept), custom_call_target="tpu_custom_call" | custom-call | bytes 4194304 | tf_op jit(solution)/shard_map/unpack/pallas_call | solution.py:32
  83.7 3.0 collective-permute-start.4
  86.7 3.0 collective-permute-start.5
  94.8 22.4 %blur.2 = (f32[2048,128]{1,0:T(8,128)S(1)}, f32[2048,128]{1,0:T(8,128)S(1)}) custom-call(f32[2048,128]{1,0:T(8,128)} %collective-permute-done.top, f32[2048,128]{1,0:T(8,128)} %get-tuple-element.28.low, f32[2048,128]{1,0:T(8,128)} %get-tuple-element.27.high, f32[2048,128]{1,0:T(8,128)} %collective-permute-done.1.bottom, f32[4096,128]{1,0:T(8,128)} %bitcast.114, ...), custom_call_target="tpu_custom_call" | custom-call | flops 10737418240 | bytes 8388608 | tf_op jit(solution)/shard_map/blur/pallas_call | solution.py:32
  121.8 23.3 %blur.3 = (f32[2048,128]{1,0:T(8,128)}, f32[2048,128]{1,0:T(8,128)}) custom-call(f32[2048,128]{1,0:T(8,128)} %collective-permute-done.4.top, f32[2048,128]{1,0:T(8,128)} %get-tuple-element.35.low, f32[2048,128]{1,0:T(8,128)} %get-tuple-element.34.high, f32[2048,128]{1,0:T(8,128)} %collective-permute-done.5.bottom, f32[4096,128]{1,0:T(8,128)} %bitcast.113, ...), custom_call_target="tpu_custom_call" | custom-call | flops 10737418240 | bytes 8388608 | tf_op jit(solution)/shard_map/blur/pallas_call | solution.py:32
  145.1 3.6 %collective-permute-start.6 = (f32[2048,128]{1,0:T(8,128)}, f32[2048,128]{1,0:T(8,128)}, u32[]{:S(2)}, u32[]{:S(2)}) collective-permute-start(f32[2048,128]{1,0:T(8,128)} %get-tuple-element.36.high), channel_id=1, source_target_pairs={{0,1},{1,2},{2,3},{3,4},{4,5},{5,6},{6,7},{7,8},{8,9},{9,10},{10,1... | collective-permute-start | bytes 3145736 | tf_op jit(solution)/shard_map/ppermute | solution.py:282
  150.9 5.1 %adjoint.4 = (f32[32,64,128]{2,1,0:T(8,128)S(1)}, f32[1,64,128]{2,1,0:T(8,128)S(1)}) custom-call(s32[33]{0:T(128)S(1)} %copy-done.25, f32[2048,128]{1,0:T(8,128)S(1)} %collective-permute-done.2.top, f32[2048,128]{1,0:T(8,128)S(1)} %get-tuple-element.30.low, f32[2048,128]{1,0:T(8,128)S(1)} %get-tuple-element.29.high, ...), custom_call_target="tpu_custom_call" | custom-call | flops 1073741824 | bytes 4194304 | tf_op jit(solution)/shard_map/adjoint/pallas_call | solution.py:32
  157.0 11.3 %all-to-all-start.1 = ((f32[32,64,128]{2,1,0:T(8,128)}), f32[32,64,128]{2,1,0:T(8,128)}, u32[]{:S(2)}, u32[]{:S(2)}) async-start(f32[32,64,128]{2,1,0:T(8,128)} %copy-done.17), calls=%async_computation.1 | async-start | bytes 2097152 | tf_op jit(solution)/shard_map/all_to_all | solution.py:331
  168.4 6.8 %adjoint.5 = (f32[32,64,128]{2,1,0:T(8,128)S(1)}, f32[1,64,128]{2,1,0:T(8,128)S(1)}) custom-call(s32[33]{0:T(128)S(1)} %copy-done.24, f32[2048,128]{1,0:T(8,128)} %collective-permute-done.6.top, f32[2048,128]{1,0:T(8,128)} %get-tuple-element.37.low, f32[2048,128]{1,0:T(8,128)} %get-tuple-element.36.high, f32[2048,128]{1,0:T(8,128)} %collective-permute-done.7.bottom, ...), custom_call_target="tpu_custom_call" | custom-call | flops 1073741824 | bytes 4194304 | tf_op jit(solution)/shard_map/adjoint/pallas_call | solution.py:32
  176.1 9.3 %all-to-all-done.1.recv0 = f32[32,64,128]{2,1,0:T(8,128)} async-done(((f32[32,64,128]{2,1,0:T(8,128)}), f32[32,64,128]{2,1,0:T(8,128)}, u32[]{:S(2)}, u32[]{:S(2)}) %all-to-all-start.1) | async-done | bytes 1048608 | tf_op jit(solution)/shard_map/all_to_all | solution.py:331
  185.4 4.6 %all-to-all-start.3 = ((f32[32,64,128]{2,1,0:T(8,128)}), f32[32,64,128]{2,1,0:T(8,128)}, u32[]{:S(2)}, u32[]{:S(2)}) async-start(f32[32,64,128]{2,1,0:T(8,128)} %copy-done.16), calls=%async_computation.3 | async-start | bytes 2097152 | tf_op jit(solution)/shard_map/all_to_all | solution.py:331
  193.7 5.1 %adjoint.6 = (f32[32,64,128]{2,1,0:T(8,128)S(1)}, f32[1,64,128]{2,1,0:T(8,128)S(1)}) custom-call(s32[33]{0:T(128)S(1)} %copy-done.25, f32[2048,128]{1,0:T(8,128)S(1)} %copy-done.5, f32[2048,128]{1,0:T(8,128)S(1)} %get-tuple-element.30.low, f32[2048,128]{1,0:T(8,128)S(1)} %copy-done.3, f32[2048,128]{1,0:T(8,128)S(1)} %copy-done.7, ...), custom_call_target="tpu_custom_call" | custom-call | flops 1073741824 | bytes 4194304 | tf_op jit(solution)/shard_map/adjoint/pallas_call | solution.py:32
  199.9 7.4 %all-to-all-done.3.recv1 = f32[32,64,128]{2,1,0:T(8,128)} async-done(((f32[32,64,128]{2,1,0:T(8,128)}), f32[32,64,128]{2,1,0:T(8,128)}, u32[]{:S(2)}, u32[]{:S(2)}) %all-to-all-start.3) | async-done | bytes 1048608 | tf_op jit(solution)/shard_map/all_to_all | solution.py:331
  207.3 4.0 %all-to-all-start.5 = ((f32[32,64,128]{2,1,0:T(8,128)}), f32[32,64,128]{2,1,0:T(8,128)S(1)}, u32[]{:S(2)}, u32[]{:S(2)}) async-start(f32[32,64,128]{2,1,0:T(8,128)} %copy-done.15), calls=%async_computation.5 | async-start | bytes 2097152 | tf_op jit(solution)/shard_map/all_to_all | solution.py:331
  211.3 6.8 %adjoint.7 = (f32[32,64,128]{2,1,0:T(8,128)S(1)}, f32[1,64,128]{2,1,0:T(8,128)S(1)}) custom-call(s32[33]{0:T(128)S(1)} %copy-done.24, f32[2048,128]{1,0:T(8,128)} %collective-permute-done.6.top, f32[2048,128]{1,0:T(8,128)} %get-tuple-element.37.low, f32[2048,128]{1,0:T(8,128)} %get-tuple-element.36.high, f32[2048,128]{1,0:T(8,128)} %collective-permute-done.7.bottom, ...), custom_call_target="tpu_custom_call" | custom-call | flops 1073741824 | bytes 4194304 | tf_op jit(solution)/shard_map/adjoint/pallas_call | solution.py:32
  219.0 9.4 %all-to-all-done.5.recv0 = f32[32,64,128]{2,1,0:T(8,128)S(1)} async-done(((f32[32,64,128]{2,1,0:T(8,128)}), f32[32,64,128]{2,1,0:T(8,128)S(1)}, u32[]{:S(2)}, u32[]{:S(2)}) %all-to-all-start.5) | async-done | bytes 1048608 | tf_op jit(solution)/shard_map/all_to_all | solution.py:331
  228.4 4.6 %all-to-all-start.6 = ((f32[32,64,128]{2,1,0:T(8,128)}), f32[32,64,128]{2,1,0:T(8,128)}, u32[]{:S(2)}, u32[]{:S(2)}) async-start(f32[32,64,128]{2,1,0:T(8,128)} %copy-done.14), calls=%async_computation.6 | async-start | bytes 2097152 | tf_op jit(solution)/shard_map/all_to_all | solution.py:331
  237.9 12.4 %all-to-all-done.6.recv1 = f32[32,64,128]{2,1,0:T(8,128)} async-done(((f32[32,64,128]{2,1,0:T(8,128)}), f32[32,64,128]{2,1,0:T(8,128)}, u32[]{:S(2)}, u32[]{:S(2)}) %all-to-all-start.6) | async-done | bytes 1048608 | tf_op jit(solution)/shard_map/all_to_all | solution.py:331
  250.3 5.2 %all-to-all-start.4 = ((f32[32,64,128]{2,1,0:T(8,128)}), f32[32,64,128]{2,1,0:T(8,128)S(1)}, u32[]{:S(2)}, u32[]{:S(2)}) async-start(f32[32,64,128]{2,1,0:T(8,128)} %copy-done.11), calls=%async_computation.4 | async-start | bytes 2097152 | tf_op jit(solution)/shard_map/all_to_all | solution.py:335
  259.8 10.2 %all-to-all-done.4 = f32[32,64,128]{2,1,0:T(8,128)S(1)} async-done(((f32[32,64,128]{2,1,0:T(8,128)}), f32[32,64,128]{2,1,0:T(8,128)S(1)}, u32[]{:S(2)}, u32[]{:S(2)}) %all-to-all-start.4) | async-done | bytes 1048608 | tf_op jit(solution)/shard_map/all_to_all | solution.py:335
  270.0 4.2 %all-to-all-start.7 = ((f32[32,64,128]{2,1,0:T(8,128)}), f32[32,64,128]{2,1,0:T(8,128)}, u32[]{:S(2)}, u32[]{:S(2)}) async-start(f32[32,64,128]{2,1,0:T(8,128)} %copy-done.10), calls=%async_computation.7 | async-start | bytes 2097152 | tf_op jit(solution)/shard_map/all_to_all | solution.py:335
  279.4 8.6 %all-to-all-done.7 = f32[32,64,128]{2,1,0:T(8,128)} async-done(((f32[32,64,128]{2,1,0:T(8,128)}), f32[32,64,128]{2,1,0:T(8,128)}, u32[]{:S(2)}, u32[]{:S(2)}) %all-to-all-start.7) | async-done | bytes 1048608 | tf_op jit(solution)/shard_map/all_to_all | solution.py:335
  293.8 5.4 %collective-permute-done.9.refs_2_ = f32[8,64,128]{2,1,0:T(8,128)S(1)} collective-permute-done((f32[8,64,128]{2,1,0:T(8,128)S(1)}, f32[8,64,128]{2,1,0:T(8,128)S(1)}, u32[]{:S(2)}, u32[]{:S(2)}) %collective-permute-start.9) | collective-permute-done | bytes 262176 | tf_op jit(solution)/shard_map/ppermute | solution.py:282
  299.2 5.4 %collective-permute-done.11.refs_5_ = f32[8,64,128]{2,1,0:T(8,128)} collective-permute-done((f32[8,64,128]{2,1,0:T(8,128)S(1)}, f32[8,64,128]{2,1,0:T(8,128)}, u32[]{:S(2)}, u32[]{:S(2)}) %collective-permute-start.11) | collective-permute-done | bytes 262176 | tf_op jit(solution)/shard_map/ppermute | solution.py:282
  304.6 5.9 %collective-permute-done.12.refs_6_ = f32[8,64,128]{2,1,0:T(8,128)} collective-permute-done((f32[8,64,128]{2,1,0:T(8,128)S(1)}, f32[8,64,128]{2,1,0:T(8,128)}, u32[]{:S(2)}, u32[]{:S(2)}) %collective-permute-start.12) | collective-permute-done | bytes 262176 | tf_op jit(solution)/shard_map/ppermute | solution.py:282
  310.5 5.4 %final.1 = f32[4096,128]{1,0:T(8,128)} custom-call(s32[4]{0:T(128)S(1)} %and_select_fusion.3.place, f32[4096,128]{1,0:T(8,128)S(1)} %bitcast.111, f32[8,64,128]{2,1,0:T(8,128)S(1)} %quarter.2.refs_0_, f32[8,64,128]{2,1,0:T(8,128)S(1)} %collective-permute-done.8.refs_1_, f32[8,64,128]{2,1,0:T(8,128)S(1)} %collective-permute-done.9.refs_2_, ...), custom_call_target="tpu_custom_call" | custom-call | bytes 6291456 | tf_op jit(solution)/shard_map/final/pallas_call | solution.py:32
  (153 shorter events, 60.5 us)
Async XLA Ops:
  7.9 11.3 %copy-start.1 = (f32[32,128,128]{2,1,0:T(8,128)S(1)}, f32[32,128,128]{2,1,0:T(8,128)}, u32[]{:S(2)}) copy-start(f32[32,128,128]{2,1,0:T(8,128)} %param.4) | copy-start | bytes 6291460
  7.9 37.5 %all-to-all-start = ((f32[32,128,128]{2,1,0:T(8,128)}), f32[32,128,128]{2,1,0:T(8,128)}, u32[]{:S(2)}, u32[]{:S(2)}) async-start(f32[32,128,128]{2,1,0:T(8,128)} %copy-done.13), calls=%async_computation | async-start | bytes 4194304 | tf_op jit(solution)/shard_map/all_to_all | solution.py:304
  45.4 34.7 %all-to-all-start.2 = ((f32[32,128,128]{2,1,0:T(8,128)}), f32[32,128,128]{2,1,0:T(8,128)}, u32[]{:S(2)}, u32[]{:S(2)}) async-start(f32[32,128,128]{2,1,0:T(8,128)} %copy-done.12), calls=%async_computation.2 | async-start | bytes 4194304 | tf_op jit(solution)/shard_map/all_to_all | solution.py:304
  51.5 11.5 %copy-start.26 = (f32[2,32,128,128]{3,2,1,0:T(8,128)S(1)}, f32[2,32,128,128]{3,2,1,0:T(8,128)}, u32[]{:S(2)}) copy-start(f32[2,32,128,128]{3,2,1,0:T(8,128)} %param.5) | copy-start | bytes 12582916
  55.4 36.0 %collective-permute-start = (f32[2048,128]{1,0:T(8,128)}, f32[2048,128]{1,0:T(8,128)}, u32[]{:S(2)}, u32[]{:S(2)}) collective-permute-start(f32[2048,128]{1,0:T(8,128)} %get-tuple-element.27.high), channel_id=1, source_target_pairs={{0,1},{1,2},{2,3},{3,4},{4,5},{5,6},{6,7},{7,8},{8,9},{9,10},{10,1... | collective-permute-start | bytes 3145736 | tf_op jit(solution)/shard_map/ppermute | solution.py:282
  58.9 32.5 %collective-permute-start.1 = (f32[2048,128]{1,0:T(8,128)}, f32[2048,128]{1,0:T(8,128)}, u32[]{:S(2)}, u32[]{:S(2)}) collective-permute-start(f32[2048,128]{1,0:T(8,128)} %get-tuple-element.28.low), channel_id=1, source_target_pairs={{1,0},{2,1},{3,2},{4,3},{5,4},{6,5},{7,6},{8,7},{9,8},{10,9},{11,1... | collective-permute-start | bytes 3145736 | tf_op jit(solution)/shard_map/ppermute | solution.py:282
  83.7 38.1 %collective-permute-start.4 = (f32[2048,128]{1,0:T(8,128)}, f32[2048,128]{1,0:T(8,128)}, u32[]{:S(2)}, u32[]{:S(2)}) collective-permute-start(f32[2048,128]{1,0:T(8,128)} %get-tuple-element.34.high), channel_id=1, source_target_pairs={{0,1},{1,2},{2,3},{3,4},{4,5},{5,6},{6,7},{7,8},{8,9},{9,10},{10,1... | collective-permute-start | bytes 3145736 | tf_op jit(solution)/shard_map/ppermute | solution.py:282
  86.7 35.0 %collective-permute-start.5 = (f32[2048,128]{1,0:T(8,128)}, f32[2048,128]{1,0:T(8,128)}, u32[]{:S(2)}, u32[]{:S(2)}) collective-permute-start(f32[2048,128]{1,0:T(8,128)} %get-tuple-element.35.low), channel_id=1, source_target_pairs={{1,0},{2,1},{3,2},{4,3},{5,4},{6,5},{7,6},{8,7},{9,8},{10,9},{11,1... | collective-permute-start | bytes 3145736 | tf_op jit(solution)/shard_map/ppermute | solution.py:282
  94.8 26.9 %copy-start.19 = (bf16[256,256]{1,0:T(8,128)(2,1)S(1)}, bf16[256,256]{1,0:T(8,128)(2,1)}, u32[]{:S(2)}) copy-start(bf16[256,256]{1,0:T(8,128)(2,1)} %get-tuple-element.61.xmat_t) | copy-start | bytes 393220
  94.8 27.0 %copy-start.20 = (bf16[256,256]{1,0:T(8,128)(2,1)S(1)}, bf16[256,256]{1,0:T(8,128)(2,1)}, u32[]{:S(2)}) copy-start(bf16[256,256]{1,0:T(8,128)(2,1)} %get-tuple-element.91.ymat) | copy-start | bytes 393220
  117.2 33.6 %copy-start.2 = (f32[2048,128]{1,0:T(8,128)}, f32[2048,128]{1,0:T(8,128)S(1)}, u32[]{:S(2)}) copy-start(f32[2048,128]{1,0:T(8,128)S(1)} %get-tuple-element.29.high) | copy-start | bytes 3145732
  117.2 33.6 %collective-permute-start.2 = (f32[2048,128]{1,0:T(8,128)S(1)}, f32[2048,128]{1,0:T(8,128)S(1)}, u32[]{:S(2)}, u32[]{:S(2)}) collective-permute-start(f32[2048,128]{1,0:T(8,128)S(1)} %get-tuple-element.29.high), channel_id=1, source_target_pairs={{0,1},{1,2},{2,3},{3,4},{4,5},{5,6},{6,7},{7,8},{8,9},{9,10},{10,1... | collective-permute-start | bytes 3145736 | tf_op jit(solution)/shard_map/ppermute | solution.py:282
  119.8 31.0 %collective-permute-start.3 = (f32[2048,128]{1,0:T(8,128)S(1)}, f32[2048,128]{1,0:T(8,128)S(1)}, u32[]{:S(2)}, u32[]{:S(2)}) collective-permute-start(f32[2048,128]{1,0:T(8,128)S(1)} %get-tuple-element.30.low), channel_id=1, source_target_pairs={{1,0},{2,1},{3,2},{4,3},{5,4},{6,5},{7,6},{8,7},{9,8},{10,9},{11,1... | collective-permute-start | bytes 3145736 | tf_op jit(solution)/shard_map/ppermute | solution.py:282
  121.8 28.9 %copy-start.29 = (bf16[2,64,64]{2,1,0:T(8,128)(2,1)S(1)}, bf16[2,64,64]{2,1,0:T(8,128)(2,1)}, u32[]{:S(2)}) copy-start(bf16[2,64,64]{2,1,0:T(8,128)(2,1)} %maximum_convert_fusion.5) | copy-start | bytes 49156
  121.8 29.1 %copy-start.25 = (s32[33]{0:T(128)S(1)}, s32[33]{0:T(128)}, u32[]{:S(2)}) copy-start(s32[33]{0:T(128)} %get-tuple-element.84.table) | copy-start | bytes 400
  145.1 23.2 %collective-permute-start.6 = (f32[2048,128]{1,0:T(8,128)}, f32[2048,128]{1,0:T(8,128)}, u32[]{:S(2)}, u32[]{:S(2)}) collective-permute-start(f32[2048,128]{1,0:T(8,128)} %get-tuple-element.36.high), channel_id=1, source_target_pairs={{0,1},{1,2},{2,3},{3,4},{4,5},{5,6},{6,7},{7,8},{8,9},{9,10},{10,1... | collective-permute-start | bytes 3145736 | tf_op jit(solution)/shard_map/ppermute | solution.py:282
  148.8 19.6 %collective-permute-start.7 = (f32[2048,128]{1,0:T(8,128)}, f32[2048,128]{1,0:T(8,128)}, u32[]{:S(2)}, u32[]{:S(2)}) collective-permute-start(f32[2048,128]{1,0:T(8,128)} %get-tuple-element.37.low), channel_id=1, source_target_pairs={{1,0},{2,1},{3,2},{4,3},{5,4},{6,5},{7,6},{8,7},{9,8},{10,9},{11,1... | collective-permute-start | bytes 3145736 | tf_op jit(solution)/shard_map/ppermute | solution.py:282
  157.0 11.3 %copy-start.24 = (s32[33]{0:T(128)S(1)}, s32[33]{0:T(128)}, u32[]{:S(2)}) copy-start(s32[33]{0:T(128)} %get-tuple-element.83.table) | copy-start | bytes 400
  157.0 28.4 %all-to-all-start.1 = ((f32[32,64,128]{2,1,0:T(8,128)}), f32[32,64,128]{2,1,0:T(8,128)}, u32[]{:S(2)}, u32[]{:S(2)}) async-start(f32[32,64,128]{2,1,0:T(8,128)} %copy-done.17), calls=%async_computation.1 | async-start | bytes 2097152 | tf_op jit(solution)/shard_map/all_to_all | solution.py:331
  185.4 21.8 %all-to-all-start.3 = ((f32[32,64,128]{2,1,0:T(8,128)}), f32[32,64,128]{2,1,0:T(8,128)}, u32[]{:S(2)}, u32[]{:S(2)}) async-start(f32[32,64,128]{2,1,0:T(8,128)} %copy-done.16), calls=%async_computation.3 | async-start | bytes 2097152 | tf_op jit(solution)/shard_map/all_to_all | solution.py:331
  207.3 21.1 %all-to-all-start.5 = ((f32[32,64,128]{2,1,0:T(8,128)}), f32[32,64,128]{2,1,0:T(8,128)S(1)}, u32[]{:S(2)}, u32[]{:S(2)}) async-start(f32[32,64,128]{2,1,0:T(8,128)} %copy-done.15), calls=%async_computation.5 | async-start | bytes 2097152 | tf_op jit(solution)/shard_map/all_to_all | solution.py:331
  219.0 14.0 %copy-start.28 = (s32[2,32,32]{2,0,1:T(2,128)S(1)}, s32[2,32,32]{2,0,1:T(2,128)}, u32[]{:S(2)}) copy-start(s32[2,32,32]{2,0,1:T(2,128)} %get-tuple-element.85) | copy-start | bytes 24580
  219.0 14.1 %copy-start.27 = (s32[2,32,32]{2,1,0:T(8,128)S(1)}, s32[2,32,32]{2,1,0:T(8,128)}, u32[]{:S(2)}) copy-start(s32[2,32,32]{2,1,0:T(8,128)} %param.7) | copy-start | bytes 24580
  228.4 21.9 %all-to-all-start.6 = ((f32[32,64,128]{2,1,0:T(8,128)}), f32[32,64,128]{2,1,0:T(8,128)}, u32[]{:S(2)}, u32[]{:S(2)}) async-start(f32[32,64,128]{2,1,0:T(8,128)} %copy-done.14), calls=%async_computation.6 | async-start | bytes 2097152 | tf_op jit(solution)/shard_map/all_to_all | solution.py:331
  250.3 19.7 %all-to-all-start.4 = ((f32[32,64,128]{2,1,0:T(8,128)}), f32[32,64,128]{2,1,0:T(8,128)S(1)}, u32[]{:S(2)}, u32[]{:S(2)}) async-start(f32[32,64,128]{2,1,0:T(8,128)} %copy-done.11), calls=%async_computation.4 | async-start | bytes 2097152 | tf_op jit(solution)/shard_map/all_to_all | solution.py:335
  270.0 18.0 %all-to-all-start.7 = ((f32[32,64,128]{2,1,0:T(8,128)}), f32[32,64,128]{2,1,0:T(8,128)}, u32[]{:S(2)}, u32[]{:S(2)}) async-start(f32[32,64,128]{2,1,0:T(8,128)} %copy-done.10), calls=%async_computation.7 | async-start | bytes 2097152 | tf_op jit(solution)/shard_map/all_to_all | solution.py:335
  274.3 18.9 %collective-permute-start.8 = (f32[8,64,128]{2,1,0:T(8,128)S(1)}, f32[8,64,128]{2,1,0:T(8,128)S(1)}, u32[]{:S(2)}, u32[]{:S(2)}) collective-permute-start(f32[8,64,128]{2,1,0:T(8,128)S(1)} %quarter.2.refs_0_), channel_id=1, source_target_pairs={{0,32},{32,64},{64,96},{96,0},{1,33},{33,65},{65,97},{97,1},{2,34}... | collective-permute-start | bytes 786440 | tf_op jit(solution)/shard_map/ppermute | solution.py:282
  275.8 23.4 %collective-permute-start.9 = (f32[8,64,128]{2,1,0:T(8,128)S(1)}, f32[8,64,128]{2,1,0:T(8,128)S(1)}, u32[]{:S(2)}, u32[]{:S(2)}) collective-permute-start(f32[8,64,128]{2,1,0:T(8,128)S(1)} %quarter.2.refs_0_), channel_id=1, source_target_pairs={{0,64},{32,96},{64,0},{96,32},{1,65},{33,97},{65,1},{97,33},{2,66}... | collective-permute-start | bytes 786440 | tf_op jit(solution)/shard_map/ppermute | solution.py:282
  278.2 21.0 %collective-permute-start.10 = (f32[8,64,128]{2,1,0:T(8,128)S(1)}, f32[8,64,128]{2,1,0:T(8,128)S(1)}, u32[]{:S(2)}, u32[]{:S(2)}) collective-permute-start(f32[8,64,128]{2,1,0:T(8,128)S(1)} %quarter.2.refs_0_), channel_id=1, source_target_pairs={{0,96},{32,0},{64,32},{96,64},{1,97},{33,1},{65,33},{97,65},{2,98}... | collective-permute-start | bytes 786440 | tf_op jit(solution)/shard_map/ppermute | solution.py:282
  289.3 15.3 %collective-permute-start.11 = (f32[8,64,128]{2,1,0:T(8,128)S(1)}, f32[8,64,128]{2,1,0:T(8,128)}, u32[]{:S(2)}, u32[]{:S(2)}) collective-permute-start(f32[8,64,128]{2,1,0:T(8,128)S(1)} %quarter.3.refs_4_), channel_id=1, source_target_pairs={{0,32},{32,64},{64,96},{96,0},{1,33},{33,65},{65,97},{97,1},{2,34}... | collective-permute-start | bytes 786440 | tf_op jit(solution)/shard_map/ppermute | solution.py:282
  289.6 20.9 %collective-permute-start.12 = (f32[8,64,128]{2,1,0:T(8,128)S(1)}, f32[8,64,128]{2,1,0:T(8,128)}, u32[]{:S(2)}, u32[]{:S(2)}) collective-permute-start(f32[8,64,128]{2,1,0:T(8,128)S(1)} %quarter.3.refs_4_), channel_id=1, source_target_pairs={{0,64},{32,96},{64,0},{96,32},{1,65},{33,97},{65,1},{97,33},{2,66}... | collective-permute-start | bytes 786440 | tf_op jit(solution)/shard_map/ppermute | solution.py:282
  293.2 17.3 %collective-permute-start.13 = (f32[8,64,128]{2,1,0:T(8,128)S(1)}, f32[8,64,128]{2,1,0:T(8,128)}, u32[]{:S(2)}, u32[]{:S(2)}) collective-permute-start(f32[8,64,128]{2,1,0:T(8,128)S(1)} %quarter.3.refs_4_), channel_id=1, source_target_pairs={{0,96},{32,0},{64,32},{96,64},{1,97},{33,1},{65,33},{97,65},{2,98}... | collective-permute-start | bytes 786440 | tf_op jit(solution)/shard_map/ppermute | solution.py:282
  (21 other events, 46.1 us)

commit v2 on v1

v2 whole, which is shorter than its diff:
```python
import functools

import jax
import jax.numpy as jnp
from jax import lax
from jax.experimental import pallas as pl
from jax.experimental.pallas import tpu as pltpu
from jax.sharding import PartitionSpec as P


TAPS = 31
HALF = 15
ZD = 32
YT = 4
NX = 128
GRID = 32
NY = 128
PAD = 16
NPAD = ZD + 2 * PAD
PLANES = 4
STEPS = 4
ROWS = ZD // STEPS
PITCH = NY + 8
WORK = ZD + 8

F32 = jnp.float32
BF16 = jnp.bfloat16
VMEM = pl.BlockSpec(memory_space=pltpu.VMEM)
SMEM = pl.BlockSpec(memory_space=pltpu.SMEM)
ANY = pl.BlockSpec(memory_space=pl.ANY)


def call(kernel, operands, outs, ins=None, out_specs=None, grid=(), scratch=(), flops=0, moved=0, far=(), alias=None):
    ins = ins or {}
    in_specs = [
        ins.get(n, SMEM if jnp.issubdtype(o.dtype, jnp.integer) else VMEM) for n, o in enumerate(operands)
    ]
    return pl.pallas_call(
        kernel,
        out_shape=[pltpu.HBM(s, F32) if n in far else jax.ShapeDtypeStruct(s, F32) for n, s in enumerate(outs)],
        grid=grid,
        in_specs=in_specs,
        out_specs=out_specs or [VMEM] * len(outs),
        scratch_shapes=list(scratch),
        input_output_aliases=alias or {},
        cost_estimate=pl.CostEstimate(flops=flops, bytes_accessed=moved, transcendentals=0),
        compiler_params=pltpu.CompilerParams(vmem_limit_bytes=24 << 20),
    )(*operands)


def halves(x):
    high = x.astype(BF16)
    low = (x - high.astype(F32)).astype(BF16)
    return high, low


def dot(a, b):
    return jnp.dot(a, b, preferred_element_type=F32)


def left_dot(matrix, x):
    high, low = halves(x)
    full = dot(matrix, jnp.concatenate([high, low], axis=0))
    rows = full.shape[0] // 2
    return full[:rows] + full[rows:]


def right_dot(x, matrix):
    high, low = halves(x)
    full = dot(jnp.concatenate([high, low], axis=1), matrix)
    return full[:, :NX] + full[:, NX:]


def pack_kernel(table, last, est, send, kept0, kept1, turned):
    for z in range(ROWS):
        turned[pl.ds(z * PITCH, NY), :] = est[pl.ds(z * NY, NY), :]

    def rows(tile, j):
        return turned[pl.ds(tile * YT + j, ROWS, stride=PITCH), :]

    def step(slot, carry):
        for v in range(2):
            tile = table[v, slot]
            for j in range(YT):
                send[slot, v, j] = rows(tile, j)
        return carry

    lax.fori_loop(0, GRID, step, 0, unroll=4)
    for v, kept in enumerate((kept0, kept1)):
        for j in range(YT):
            kept[0, j] = rows(last[v], j)


def unpack_kernel(v, table, recv, kept, low, high, sems):
    def put(source, c):
        at = pl.ds(pl.multiple_of(c * YT, YT), YT)
        pltpu.make_async_copy(source.at[:, pl.ds(0, PAD), :], low.at[at], sems.at[0]).start()
        pltpu.make_async_copy(source.at[:, pl.ds(PAD, PAD), :], high.at[at], sems.at[1]).start()

    def step(c, carry):
        slot = table[v, c]

        @pl.when(slot < GRID)
        def _():
            put(recv.at[slot, v], c)

        @pl.when(slot == GRID)
        def _():
            put(kept.at[0], c)

        return carry

    lax.fori_loop(0, GRID, step, 0)
    pltpu.make_async_copy(low, low, sems.at[0]).wait()
    pltpu.make_async_copy(high, high, sems.at[1]).wait()


def padded_pair(parts, *pair):
    columns = [jnp.concatenate([p[y] for p in parts], axis=0) for y in pair]
    return jnp.concatenate(columns, axis=1)


def blur_kernel(v, top, low, high, bottom, rec, zmat, xmat, ymat, ymat_t, xmat_t, out_low, out_high, work, seen_rows, sem):
    zmat, xmat, ymat, ymat_t, xmat_t = (r.at[0] for r in (zmat, xmat, ymat, ymat_t, xmat_t))
    parts = (top, low, high, bottom)
    fetch = pltpu.make_async_copy(rec.at[v], seen_rows, sem)
    fetch.start()

    def forward(group, carry):
        rows = []
        for pair in range(2):
            y = group * 4 + pair * 2
            blurred = left_dot(zmat[...], padded_pair(parts, y, y + 1))
            rows += [blurred[:, :NX], blurred[:, NX:]]
        done = right_dot(jnp.concatenate(rows, axis=0), xmat[...])
        for i in range(4):
            at = pl.multiple_of((group * 4 + i) * WORK, 8)
            work[pl.ds(at, ZD), :] = done[i * ZD : (i + 1) * ZD]
        return carry

    lax.fori_loop(0, NY // 4, forward, 0, unroll=8)
    fetch.wait()

    for base, out in ((0, out_low), (PAD, out_high)):

        def backward(step, carry, base=base, out=out):
            zz = step * 2
            z = base + zz
            x = jnp.concatenate([work[pl.ds(z + i, NY, stride=WORK), :] for i in range(2)], axis=1)
            seen = jnp.concatenate(
                [seen_rows[pl.ds(pl.multiple_of((z + i) * NY, NY), NY), :] for i in range(2)], axis=1
            )
            ratio = seen / left_dot(ymat[...], x)
            back = left_dot(ymat_t[...], ratio)
            back = right_dot(jnp.concatenate([back[:, :NX], back[:, NX:]], axis=0), xmat_t[...])
            for i in range(2):
                out[pl.ds(zz + i, NY, stride=PAD), :] = back[i * NY : (i + 1) * NY]
            return carry

        lax.fori_loop(0, PAD // 2, backward, 0, unroll=8)


def adjoint_first_kernel(v, table, top, low, high, bottom, zmat, *refs):
    parts = (top, low, high, bottom)
    send, kept = refs[-2:]
    slots = send.shape[0]
    base = pl.program_id(0) * slots

    def move(c):
        done = left_dot(zmat[v], padded_pair(parts, c * YT, c * YT + 1))
        return done[:, :NX], done[:, NX:]

    def step(slot, carry):
        send[slot, 0, 0], send[slot, 0, 1] = move(table[v, base + slot])
        return carry

    lax.fori_loop(0, slots, step, 0, unroll=slots)

    @pl.when(pl.program_id(0) == 0)
    def _():
        kept[0], kept[1] = move(table[v, GRID])


def adjoint_last_kernel(v, table, plane, top, low, high, bottom, zmat, *refs):
    parts = (top, low, high, bottom)
    *outs, work = refs

    def step(slot, carry):
        y = table[v, slot] * YT + 2
        done = left_dot(zmat[v], padded_pair(parts, y, y + 1))
        work[slot, pl.ds(0, ZD), :] = done[:, :NX]
        work[slot, pl.ds(ZD, ZD), :] = done[:, NX:]
        return carry

    lax.fori_loop(0, GRID + 1, step, 0, unroll=11)
    for hop, out in enumerate(outs):
        quarter = lax.rem(plane[0] + hop, PLANES)
        out[...] = work[:, pl.ds(pl.multiple_of(quarter * PAD, PAD), PAD), :]


def gather_kernel(*refs):
    *parts, send, kept, sems = refs
    copies = []
    for n, part in enumerate(parts):
        at = (n // 2, n % 2)
        copies.append(pltpu.make_async_copy(part.at[pl.ds(0, GRID)], send.at[:, at[0], at[1]], sems.at[n]))
        copies[-1].start()
    for n, part in enumerate(parts):
        kept[n // 2, n % 2] = part[GRID]
    for copy in copies:
        copy.wait()


def product_first_kernel(table, plane, recv, kept0, kept1, *outs):
    quarter = GRID // PLANES
    for hop, out in enumerate(outs):
        base = lax.rem(plane[0] + hop, PLANES) * quarter

        def step(n, carry, out=out, base=base):
            factors = []
            for v, kept in enumerate((kept0, kept1)):
                slot = table[v, base + n]
                factors.append(jnp.where(slot == GRID, kept[...], recv[jnp.minimum(slot, GRID - 1), v]))
            out[n] = factors[0] * factors[1]
            return carry

        lax.fori_loop(0, quarter, step, 0, unroll=2)


def product_last_kernel(*refs):
    *tables, recv, kept, out = refs

    def step(t, carry):
        factors = []
        for n, table in enumerate(tables):
            for v in range(2):
                slot = table[v, t]
                factors.append(jnp.where(slot == GRID, kept[n, v], recv[jnp.minimum(slot, GRID - 1), n, v]))
        while len(factors) > 1:
            factors = [a * b for a, b in zip(factors[::2], factors[1::2])]
        out[t] = factors[0]
        return carry

    lax.fori_loop(0, GRID, step, 0, unroll=4)


def quarter_kernel(first, second, third, fourth, out):
    out[...] = (first[...] * second[...]) * (third[...] * fourth[...])


def final_kernel(place, est, *refs):
    *pieces, out, turned = refs
    quarter = GRID // PLANES
    at = pl.program_id(0)
    for hop in range(PLANES):
        piece = pieces[hop]
        base = place[hop] * quarter
        for t in range(quarter):
            for j in range(2):
                turned[pl.ds((base + t) * YT + j, ROWS, stride=PITCH), :] = piece[t, j]
    for hop in range(PLANES):
        piece = pieces[PLANES + hop]
        own = place[hop]

        @pl.when(own % 2 == at // 2)
        def _(piece=piece, own=own):
            rows = pl.ds(pl.multiple_of((at % 2) * ROWS, ROWS), ROWS)
            for t in range(GRID):
                turned[pl.ds(t * YT + 2 + own // 2, ROWS, stride=PITCH), :] = piece[t, rows]

    for z in range(ROWS):
        rows = pl.ds(z * NY, NY)
        out[rows, :] = est[rows, :] * turned[pl.ds(z * PITCH, NY), :]


def stacked(matrix, axis):
    high = lax.reduce_precision(matrix, 8, 7)
    low = matrix - high
    if axis == 0:
        both = jnp.concatenate([high, low], axis=-2)
        return jnp.concatenate([both, both], axis=-1).astype(BF16)
    both = jnp.concatenate([high, low], axis=-1)
    return jnp.concatenate([both, both], axis=-2).astype(BF16)


def band(weights, positions):
    taps = jnp.arange(TAPS, dtype=jnp.int32)[None, :, None, None]
    return jnp.sum(jnp.where(positions[None, None] == taps, weights[:, :, None, None], 0.0), axis=1)


def bands(psf_taps, own):
    weights = psf_taps / jnp.sum(psf_taps, axis=-1, keepdims=True)
    i = jnp.arange(NX, dtype=jnp.int32)
    plain = band(weights[:, 1:].reshape(-1, TAPS), i[:, None] - i[None, :] + HALF)
    plain = plain / jnp.sum(plain, axis=1, keepdims=True)
    plain = plain.reshape(-1, 2, NX, NX)
    turned = plain.transpose(0, 1, 3, 2)
    ymat, xmat = turned[:, 0], plain[:, 1]
    ymat_t, xmat_t = plain[:, 0], turned[:, 1]

    wz = weights[:, 0]
    rows = own * ZD + jnp.arange(NPAD, dtype=jnp.int32) - PAD
    reach = rows[None, :] + jnp.arange(TAPS, dtype=jnp.int32)[:, None] - HALF
    inside = (reach >= 0) & (reach < GRID * ZD)
    divisor = jnp.sum(jnp.where(inside[None], wz[:, :, None], 0.0), axis=1)
    divisor = jnp.where((rows >= 0) & (rows < GRID * ZD), divisor, 1.0)
    k = jnp.arange(NPAD, dtype=jnp.int32)[None, :]
    o = jnp.arange(ZD, dtype=jnp.int32)[:, None]
    zmat = band(wz, k - o - 1) / divisor[:, PAD : PAD + ZD, None]
    zmat_t = band(wz, o - k + 2 * PAD - 1) / divisor[:, None, :]
    return (
        stacked(zmat, 0),
        stacked(xmat, 1),
        stacked(ymat, 0),
        stacked(ymat_t, 0),
        stacked(xmat_t, 1),
        stacked(zmat_t, 0),
    )


def tables(tile_map, own):
    source = tile_map // GRID
    tile = tile_map % GRID
    c = jnp.arange(GRID, dtype=jnp.int32)
    slots = jnp.arange(GRID + 1, dtype=jnp.int32)
    key = c[None, None, :] * GRID + tile
    outgoing = source == own
    pack = jnp.min(jnp.where(outgoing, key, GRID * GRID - 1), axis=2) % GRID
    inner = outgoing & (c == own)[None, :, None]
    last_key = jnp.max(jnp.where(inner, key, 0), axis=(1, 2))
    last = last_key % GRID
    own_source = lax.dynamic_index_in_dim(source, own, 1, keepdims=False)
    second = c[None, :] == (last_key // GRID)[:, None]
    place = jnp.where(second, GRID, own_source)
    chosen = jnp.sum(jnp.where(place[:, None, :] == slots[None, :, None], c[None, None, :], 0), axis=2)
    second_at = second[:, None, :] & (c == own)[None, :, None]
    value = jnp.where(second_at, GRID, c[None, :, None])
    wanted = (own * GRID + c)[None, :, None, None] == tile_map[:, None]
    arriving = jnp.sum(jnp.where(wanted, value[:, None], 0), axis=(2, 3))
    return pack, last, place, chosen, arriving


def shifted(value, axis, hop, ring):
    count = lax.axis_size(axis)
    pairs = [(i, (i + hop) % count) for i in range(count) if ring or 0 <= i + hop < count]
    return lax.ppermute(value, axis, pairs)


def exchange(value, axis):
    return lax.all_to_all(value, axis, 0, 0, tiled=True)


def after(value, *others):
    return lax.optimization_barrier((value, *others))[0]


def local(estimate, recorded, psf_taps, tile_map):
    own = lax.axis_index("slab")
    plane = lax.axis_index("view")
    pack, last, place, chosen, arriving = tables(tile_map, own)
    mats = bands(psf_taps, own)
    est = estimate.reshape(ZD * NY, NX)
    far_est = pltpu.with_memory_space_constraint(est, pltpu.HBM)
    rec = recorded.reshape(-1, ZD * NY, NX)
    strip = (NY, PAD, NX)
    big = ZD * NY * NX * 4

    def unpacked(v, recv, kept):
        return call(
            functools.partial(unpack_kernel, v),
            (place, recv, kept),
            (strip, strip),
            ins={1: ANY, 2: ANY},
            scratch=[pltpu.SemaphoreType.DMA((2,))],
            moved=2 * big,
        )

    def padded(low, high):
        return shifted(high, "slab", 1, False), low, high, shifted(low, "slab", -1, False)

    def blurred(v, parts):
        low, high = call(
            functools.partial(blur_kernel, v),
            (*parts, far_rec, *mats[:5]),
            ((NY * PAD, NX), (NY * PAD, NX)),
            ins={4: ANY}
            | {5 + n: pl.BlockSpec((1, *m.shape[1:]), lambda s: (v, 0, 0)) for n, m in enumerate(mats[:5])},
            grid=(1,),
            scratch=[
                pltpu.VMEM((NY * WORK, NX), F32),
                pltpu.VMEM((ZD * NY, NX), F32),
                pltpu.SemaphoreType.DMA,
            ],
            flops=5 << 30,
            moved=4 * big,
        )
        return low.reshape(strip), high.reshape(strip)

    far_rec = pltpu.with_memory_space_constraint(rec, pltpu.HBM)
    views = rec.shape[0]
    steps = lambda *block: pl.BlockSpec(block, lambda s: (*[0] * (len(block) - 2), s, 0))
    send, *kept = call(
        pack_kernel,
        (pack, last, far_est),
        ((GRID, views, YT, ZD, NX), (1, YT, ZD, NX), (1, YT, ZD, NX)),
        ins={2: steps(ROWS * NY, NX)},
        out_specs=[
            steps(GRID, views, YT, ROWS, NX),
            steps(1, YT, ROWS, NX),
            steps(1, YT, ROWS, NX),
        ],
        grid=(STEPS,),
        scratch=[pltpu.VMEM((ROWS * PITCH, NX), F32)],
        moved=2 * big,
        far=(0, 1, 2),
    )
    recv = exchange(send, "slab")
    places = [arriving] + [shifted(arriving, "view", hop, True) for hop in range(1, PLANES)]
    recv, *rest = lax.optimization_barrier((recv, *mats, *places))
    mats, places = rest[: len(mats)], rest[len(mats) :]
    parts0 = padded(*unpacked(0, recv, kept[0]))
    recv = after(recv, parts0[1])
    parts1 = padded(*unpacked(1, recv, kept[1]))
    back0 = blurred(0, parts0)
    ready0 = padded(*back0)
    parts1 = lax.optimization_barrier((*parts1, *back0))[:4]
    back1 = blurred(1, parts1)
    ready1 = padded(*back1)
    half = (GRID, views, 2, ZD, NX)

    def adjoint_first(v, parts, buffer=None):
        operands = (chosen, *parts, mats[5])
        return call(
            functools.partial(adjoint_first_kernel, v),
            operands if buffer is None else (*operands, buffer),
            (half, (2, ZD, NX)),
            ins={6: ANY},
            out_specs=[
                pl.BlockSpec((GRID // STEPS, 1, 2, ZD, NX), lambda s: (s, v, 0, 0, 0)),
                pl.BlockSpec((2, ZD, NX), lambda s: (0, 0, 0)),
            ],
            grid=(STEPS,),
            flops=1 << 30,
            moved=2 * big,
            far=(0,),
            alias={} if buffer is None else {6: 0},
        )

    def adjoint_last(v, parts):
        return call(
            functools.partial(adjoint_last_kernel, v),
            (chosen, plane.reshape(1), *parts, mats[5]),
            ((GRID + 1, PAD, NX),) * PLANES,
            scratch=[pltpu.VMEM((GRID + 1, 2 * ZD, NX), F32)],
            flops=1 << 30,
            moved=2 * big,
        )

    def across(parts):
        return [shifted(p, "view", hop, True) for hop, p in enumerate(parts) if hop]

    last0 = adjoint_last(0, ready0)
    last0 = [last0[0], *across(last0)]
    send, kept0 = adjoint_first(0, ready0)
    send, kept1 = adjoint_first(1, ready1, send)
    recv = exchange(send, "slab")
    last1 = adjoint_last(1, ready1)
    last1 = [last1[0], *across(last1)]
    send, kept = call(
        gather_kernel,
        [part for pair in zip(last0, last1) for part in pair],
        ((GRID, PLANES, views, PAD, NX), (PLANES, views, PAD, NX)),
        out_specs=[ANY, VMEM],
        scratch=[pltpu.SemaphoreType.DMA((PLANES * views,))],
        moved=2 * big,
        far=(0,),
    )
    recv1 = exchange(after(send, recv), "slab")
    block = (GRID // PLANES, 2, ZD, NX)
    products = call(
        product_first_kernel, (arriving, plane.reshape(1), recv, kept0, kept1), (block,) * PLANES, moved=2 * big
    )
    arrived = across(products)
    (mine,) = call(quarter_kernel, (products[0], *arrived), (block,), moved=big)
    pieces = [mine] + [shifted(mine, "view", hop, True) for hop in range(1, PLANES)]
    (product,) = call(product_last_kernel, (*places, recv1, kept), ((GRID, PAD, NX),), moved=2 * big)
    pieces += [product] + [shifted(product, "view", hop, True) for hop in range(1, PLANES)]
    where = (plane - jnp.arange(PLANES, dtype=jnp.int32)) % PLANES
    blocks = {1: pl.BlockSpec((ROWS * NY, NX), lambda s: (s, 0))}
    for n in range(PLANES):
        blocks[2 + n] = pl.BlockSpec((*block[:2], ROWS, NX), lambda s: (0, 0, s, 0))
    (out,) = call(
        final_kernel,
        (where, est, *pieces),
        ((ZD * NY, NX),),
        ins=blocks,
        out_specs=[pl.BlockSpec((ROWS * NY, NX), lambda s: (s, 0))],
        grid=(STEPS,),
        scratch=[pltpu.VMEM((ROWS * PITCH, NX), F32)],
        moved=3 * big,
    )
    return out.reshape(estimate.shape)


def solution(mesh):
    in_specs = (
        P("slab", None, None),
        P("view", "slab", None, None),
        P("view", None, None),
        P("view", None, None),
    )
    out_specs = P("slab", None, None)

    return jax.shard_map(local, mesh=mesh, in_specs=in_specs, out_specs=out_specs, check_vma=False)
```

time: 319 us -> 250 us (0.78)
  Pallas kernels: 92.3 us -> 45.6 us
  local copies, waits for them, and re-layouts: 23.1 us -> 6.76 us
    pallas_call x15 -> x14, Pallas kernels: 92.3 us -> 45.6 us  [call(): pl.pallas_call(kernel, out_shape=[pltpu.HBM(s, F32) if n in far else jax....]
    all_to_all x8 -> x3, waiting for transfers between devices: 93.7 us -> 55.4 us  [exchange(): return lax.all_to_all(value, axis, 0, 0, tiled=True)]
    ppermute x14 -> x26, waiting for transfers between devices: 18.5 us -> 56.1 us  [shifted(): return lax.ppermute(value, axis, pairs)]
    all_to_all x8 -> x3, starting transfers between devices: 48.7 us -> 29.5 us  [exchange(): return lax.all_to_all(value, axis, 0, 0, tiled=True)]
    ppermute x14 -> x26, starting transfers between devices: 29.3 us -> 46.9 us  [shifted(): return lax.ppermute(value, axis, pairs)]
    unnamed x62 -> x40, local copies, waits for them, and re-layouts: 18.4 us -> 6.18 us
  transfers between devices with their start and end apart: 22 -> 29, of which waited for: 12 -> 17; matrix products, arithmetic and copies ran while one was open for 4% -> 2% of each run, Pallas kernels for 27% -> 15%
where the time goes in v2:
time: 250 us; the launch traced here: 249 us
  waiting for transfers between devices  112 us (45%)
  starting transfers between devices  76.4 us (31%)
  Pallas kernels  45.6 us (18%)
  other arithmetic  7.63 us (3%)
  local copies, waits for them, and re-layouts  6.76 us (3%)
    ppermute x26, waiting for transfers between devices, shifted(): return lax.ppermute(value, axis, pairs)  56.1 us
    all_to_all x3, waiting for transfers between devices, exchange(): return lax.all_to_all(value, axis, 0, 0, tiled=True)  55.4 us
    ppermute x26, starting transfers between devices, shifted(): return lax.ppermute(value, axis, pairs)  46.9 us
    pallas_call x14, Pallas kernels, call(): pl.pallas_call(kernel, out_shape=[pltpu.HBM(s, F32) if n in far else jax....  45.6 us
    all_to_all x3, starting transfers between devices, exchange(): return lax.all_to_all(value, axis, 0, 0, tiled=True)  29.5 us
    unnamed x40, local copies, waits for them, and re-layouts  6.18 us
  transfers between devices with their start and end apart: 29, of which 17 were waited for; matrix products, arithmetic and copies ran while one was open for 2% of the time, Pallas kernels for 15%

profile of v2, /device:TPU:1, one launch (start us, length us, event | category | flops | bytes accessed | tf_op | source)
XLA Modules:
  0.0 248.5 jit_solution(1463588487190712840)
XLA Ops:
  4.0 4.6 %collective-permute-start.2 = (s32[2,32]{1,0:T(2,128)S(1)}, s32[2,32]{1,0:T(2,128)S(1)}, u32[]{:S(2)}, u32[]{:S(2)}) collective-permute-start(s32[2,32]{1,0:T(2,128)S(1)} %select_reduce_fusion.2.table.refs_0_), channel_id=1, source_target_pairs={{0,96},{32,0},{64,32},{96,64},{1,97},{33,1},{65,33},{97,65},{2,98}... | collective-permute-start | bytes 776 | tf_op jit(solution)/shard_map/ppermute | solution.py:346
  9.4 4.9 %shard_map.46 = (f32[32,2,4,32,128]{4,3,2,1,0:T(8,128)}, f32[1,4,32,128]{3,2,1,0:T(8,128)}, f32[1,4,32,128]{3,2,1,0:T(8,128)}) custom-call(s32[2,32]{1,0:T(2,128)S(1)} %and_select_fusion.1.table, s32[2]{0:T(128)S(1)} %get-tuple-element.119.last, f32[4096,128]{1,0:T(8,128)} %bitcast.49), custom_call_target="tpu_custom_call" | custom-call | bytes 4194304 | tf_op jit(solution)/shard_map/pallas_call | solution.py:38
  14.3 8.8 %all-to-all-start = ((f32[32,2,4,32,128]{4,3,2,1,0:T(8,128)}), f32[32,2,4,32,128]{4,3,2,1,0:T(8,128)}, u32[]{:S(2)}, u32[]{:S(2)}) async-start(f32[32,2,4,32,128]{4,3,2,1,0:T(8,128)} %get-tuple-element.51), calls=%async_computation | async-start | bytes 8388608 | tf_op jit(solution)/shard_map/all_to_all | solution.py:350
  27.2 46.6 %all-to-all-done.recv = f32[32,2,4,32,128]{4,3,2,1,0:T(8,128)} async-done(((f32[32,2,4,32,128]{4,3,2,1,0:T(8,128)}), f32[32,2,4,32,128]{4,3,2,1,0:T(8,128)}, u32[]{:S(2)}, u32[]{:S(2)}) %all-to-all-start) | async-done | bytes 4194336 | tf_op jit(solution)/shard_map/all_to_all | solution.py:350
  73.8 3.1 %shard_map.47 = (f32[128,16,128]{2,1,0:T(8,128)S(1)}, f32[128,16,128]{2,1,0:T(8,128)}) custom-call(s32[2,32]{1,0:T(2,128)S(1)} %broadcast_select_fusion.1.table, f32[32,2,4,32,128]{4,3,2,1,0:T(8,128)} %all-to-all-done.recv, f32[1,4,32,128]{3,2,1,0:T(8,128)S(1)} %copy-done.16), custom_call_target="tpu_custom_call" | custom-call | bytes 4194304 | tf_op jit(solution)/shard_map/pallas_call | solution.py:38
  76.9 4.3 %collective-permute-start.5 = (f32[128,16,128]{2,1,0:T(8,128)}, f32[128,16,128]{2,1,0:T(8,128)}, u32[]{:S(2)}, u32[]{:S(2)}) collective-permute-start(f32[128,16,128]{2,1,0:T(8,128)} %get-tuple-element.59.high), channel_id=1, source_target_pairs={{0,1},{1,2},{2,3},{3,4},{4,5},{5,6},{6,7},{7,8},{8,9},{9,10},{10,1... | collective-permute-start | bytes 3145736 | tf_op jit(solution)/shard_map/ppermute | solution.py:346
  81.2 3.5 %collective-permute-start.6 = (f32[128,16,128]{2,1,0:T(8,128)S(1)}, f32[128,16,128]{2,1,0:T(8,128)}, u32[]{:S(2)}, u32[]{:S(2)}) collective-permute-start(f32[128,16,128]{2,1,0:T(8,128)S(1)} %get-tuple-element.54.low), channel_id=1, source_target_pairs={{1,0},{2,1},{3,2},{4,3},{5,4},{6,5},{7,6},{8,7},{9,8},{10,9},{11,1... | collective-permute-start | bytes 3145736 | tf_op jit(solution)/shard_map/ppermute | solution.py:346
  84.7 3.5 %shard_map.48 = (f32[128,16,128]{2,1,0:T(8,128)}, f32[128,16,128]{2,1,0:T(8,128)}) custom-call(s32[2,32]{1,0:T(2,128)S(1)} %broadcast_select_fusion.1.table, f32[32,2,4,32,128]{4,3,2,1,0:T(8,128)} %all-to-all-done.recv, f32[1,4,32,128]{3,2,1,0:T(8,128)S(1)} %copy-done.15), custom_call_target="tpu_custom_call" | custom-call | bytes 4194304 | tf_op jit(solution)/shard_map/pallas_call | solution.py:38
  90.3 3.2 %collective-permute-start.4 = (f32[128,16,128]{2,1,0:T(8,128)}, f32[128,16,128]{2,1,0:T(8,128)}, u32[]{:S(2)}, u32[]{:S(2)}) collective-permute-start(f32[128,16,128]{2,1,0:T(8,128)} %get-tuple-element.68.low), channel_id=1, source_target_pairs={{1,0},{2,1},{3,2},{4,3},{5,4},{6,5},{7,6},{8,7},{9,8},{10,9},{11,1... | collective-permute-start | bytes 3145736 | tf_op jit(solution)/shard_map/ppermute | solution.py:346
  93.8 3.6 %collective-permute-done.6.bottom = f32[128,16,128]{2,1,0:T(8,128)} collective-permute-done((f32[128,16,128]{2,1,0:T(8,128)S(1)}, f32[128,16,128]{2,1,0:T(8,128)}, u32[]{:S(2)}, u32[]{:S(2)}) %collective-permute-start.6) | collective-permute-done | bytes 1048608 | tf_op jit(solution)/shard_map/ppermute | solution.py:346
  98.6 9.0 %shard_map.49 = (f32[2048,128]{1,0:T(8,128)S(1)}, f32[2048,128]{1,0:T(8,128)S(1)}) custom-call(f32[128,16,128]{2,1,0:T(8,128)} %collective-permute-done.5.top, f32[128,16,128]{2,1,0:T(8,128)S(1)} %copy-done.18, f32[128,16,128]{2,1,0:T(8,128)} %get-tuple-element.59.high, f32[128,16,128]{2,1,0:T(8,128)} %collective-permute-done.6.bottom, ...), custom_call_target="tpu_custom_call" | custom-call | flops 5368709120 | bytes 8388608 | tf_op jit(solution)/shard_map/pallas_call | solution.py:38
  109.6 2.6 %collective-permute-start.10 = (f32[128,16,128]{2,1,0:T(8,128)S(1)}, f32[128,16,128]{2,1,0:T(8,128)S(1)}, u32[]{:S(2)}, u32[]{:S(2)}) collective-permute-start(f32[128,16,128]{2,1,0:T(8,128)S(1)} %bitcast.51), channel_id=1, source_target_pairs={{1,0},{2,1},{3,2},{4,3},{5,4},{6,5},{7,6},{8,7},{9,8},{10,9},{11,1... | collective-permute-start | bytes 3145736 | tf_op jit(solution)/shard_map/ppermute | solution.py:346
  112.2 9.3 %shard_map.50 = (f32[2048,128]{1,0:T(8,128)S(1)}, f32[2048,128]{1,0:T(8,128)S(1)}) custom-call(f32[128,16,128]{2,1,0:T(8,128)} %collective-permute-done.3.top, f32[128,16,128]{2,1,0:T(8,128)} %get-tuple-element.68.low, f32[128,16,128]{2,1,0:T(8,128)} %get-tuple-element.69.high, f32[128,16,128]{2,1,0:T(8,128)} %collective-permute-done.4.bottom, ...), custom_call_target="tpu_custom_call" | custom-call | flops 5368709120 | bytes 8388608 | tf_op jit(solution)/shard_map/pallas_call | solution.py:38
  123.5 3.6 %collective-permute-start.7 = (f32[128,16,128]{2,1,0:T(8,128)S(1)}, f32[128,16,128]{2,1,0:T(8,128)S(1)}, u32[]{:S(2)}, u32[]{:S(2)}) collective-permute-start(f32[128,16,128]{2,1,0:T(8,128)S(1)} %bitcast.60), channel_id=1, source_target_pairs={{0,1},{1,2},{2,3},{3,4},{4,5},{5,6},{6,7},{7,8},{8,9},{9,10},{10,1... | collective-permute-start | bytes 3145736 | tf_op jit(solution)/shard_map/ppermute | solution.py:346
  127.3 2.8 %shard_map.51 = (f32[32,2,2,32,128]{4,3,2,1,0:T(8,128)}, f32[2,32,128]{2,1,0:T(8,128)S(1)}) custom-call(s32[2,33]{1,0:T(2,128)S(1)} %select_reduce_fusion.6.table, f32[128,16,128]{2,1,0:T(8,128)S(1)} %collective-permute-done.9.top, f32[128,16,128]{2,1,0:T(8,128)S(1)} %bitcast.52, f32[128,16,128]{2,1,0:T(8,128)S(1)} %bitcast.55, ...), custom_call_target="tpu_custom_call" | custom-call | flops 1073741824 | bytes 4194304 | tf_op jit(solution)/shard_map/pallas_call | solution.py:38
  130.1 7.6 %collective-permute-done.8.bottom = f32[128,16,128]{2,1,0:T(8,128)S(1)} collective-permute-done((f32[128,16,128]{2,1,0:T(8,128)S(1)}, f32[128,16,128]{2,1,0:T(8,128)S(1)}, u32[]{:S(2)}, u32[]{:S(2)}) %collective-permute-start.8) | collective-permute-done | bytes 1048608 | tf_op jit(solution)/shard_map/ppermute | solution.py:346
  138.9 2.8 %shard_map.52 = (f32[32,2,2,32,128]{4,3,2,1,0:T(8,128)}, f32[2,32,128]{2,1,0:T(8,128)S(1)}) custom-call(s32[2,33]{1,0:T(2,128)S(1)} %select_reduce_fusion.6.table, f32[128,16,128]{2,1,0:T(8,128)S(1)} %collective-permute-done.7.top, f32[128,16,128]{2,1,0:T(8,128)S(1)} %bitcast.58, f32[128,16,128]{2,1,0:T(8,128)S(1)} %bitcast.61, ...), custom_call_target="tpu_custom_call", output_to_operand_aliasing={{0}: (6, {})} | custom-call | flops 1073741824 | bytes 4194304 | tf_op jit(solution)/shard_map/pallas_call | solution.py:38
  141.7 12.2 %all-to-all-start.1 = ((f32[32,2,2,32,128]{4,3,2,1,0:T(8,128)}), f32[32,2,2,32,128]{4,3,2,1,0:T(8,128)S(1)}, u32[]{:S(2)}, u32[]{:S(2)}) async-start(f32[32,2,2,32,128]{4,3,2,1,0:T(8,128)} %get-tuple-element.75), calls=%async_computation.1 | async-start | bytes 4194304 | tf_op jit(solution)/shard_map/all_to_all | solution.py:350
  169.8 5.6 %collective-permute-done.20.refs_5_ = f32[33,16,128]{2,1,0:T(8,128)S(1)} collective-permute-done((f32[33,16,128]{2,1,0:T(8,128)S(1)}, f32[33,16,128]{2,1,0:T(8,128)S(1)}, u32[]{:S(2)}, u32[]{:S(2)}) %collective-permute-start.20) | collective-permute-done | bytes 270368 | tf_op jit(solution)/shard_map/ppermute | solution.py:346
  175.6 5.8 %collective-permute-done.17.refs_2_ = f32[33,16,128]{2,1,0:T(8,128)S(1)} collective-permute-done((f32[33,16,128]{2,1,0:T(8,128)S(1)}, f32[33,16,128]{2,1,0:T(8,128)S(1)}, u32[]{:S(2)}, u32[]{:S(2)}) %collective-permute-start.17) | collective-permute-done | bytes 270368 | tf_op jit(solution)/shard_map/ppermute | solution.py:346
  181.4 5.5 %collective-permute-done.19.refs_4_ = f32[33,16,128]{2,1,0:T(8,128)S(1)} collective-permute-done((f32[33,16,128]{2,1,0:T(8,128)S(1)}, f32[33,16,128]{2,1,0:T(8,128)S(1)}, u32[]{:S(2)}, u32[]{:S(2)}) %collective-permute-start.19) | collective-permute-done | bytes 270368 | tf_op jit(solution)/shard_map/ppermute | solution.py:346
  188.5 8.4 %all-to-all-start.2 = ((f32[32,4,2,16,128]{4,3,2,1,0:T(8,128)}), f32[32,4,2,16,128]{4,3,2,1,0:T(8,128)}, u32[]{:S(2)}, u32[]{:S(2)}) async-start(f32[32,4,2,16,128]{4,3,2,1,0:T(8,128)} %get-tuple-element.95), calls=%async_computation.2 | async-start | bytes 4194304 | tf_op jit(solution)/shard_map/all_to_all | solution.py:350
  202.4 4.4 %collective-permute-done.11.second = f32[8,2,32,128]{3,2,1,0:T(8,128)S(1)} collective-permute-done((f32[8,2,32,128]{3,2,1,0:T(8,128)S(1)}, f32[8,2,32,128]{3,2,1,0:T(8,128)S(1)}, u32[]{:S(2)}, u32[]{:S(2)}) %collective-permute-start.11) | collective-permute-done | bytes 262176 | tf_op jit(solution)/shard_map/ppermute | solution.py:346
  206.8 6.4 %collective-permute-done.12.third = f32[8,2,32,128]{3,2,1,0:T(8,128)S(1)} collective-permute-done((f32[8,2,32,128]{3,2,1,0:T(8,128)S(1)}, f32[8,2,32,128]{3,2,1,0:T(8,128)S(1)}, u32[]{:S(2)}, u32[]{:S(2)}) %collective-permute-start.12) | collective-permute-done | bytes 262176 | tf_op jit(solution)/shard_map/ppermute | solution.py:346
  213.3 2.9 %collective-permute-start.16 = (f32[8,2,32,128]{3,2,1,0:T(8,128)S(1)}, f32[8,2,32,128]{3,2,1,0:T(8,128)S(1)}, u32[]{:S(2)}, u32[]{:S(2)}) collective-permute-start(f32[8,2,32,128]{3,2,1,0:T(8,128)S(1)} %shard_map.54.refs_0_), channel_id=1, source_target_pairs={{0,96},{32,0},{64,32},{96,64},{1,97},{33,1},{65,33},{97,65},{2,98}... | collective-permute-start | bytes 786440 | tf_op jit(solution)/shard_map/ppermute | solution.py:346
  216.9 8.8 %all-to-all-done.2.refs_4_ = f32[32,4,2,16,128]{4,3,2,1,0:T(8,128)} async-done(((f32[32,4,2,16,128]{4,3,2,1,0:T(8,128)}), f32[32,4,2,16,128]{4,3,2,1,0:T(8,128)}, u32[]{:S(2)}, u32[]{:S(2)}) %all-to-all-start.2) | async-done | bytes 2097184 | tf_op jit(solution)/shard_map/all_to_all | solution.py:350
  225.7 2.3 shard_map.58.refs_4_
  228.0 2.4 collective-permute-start.25
  231.6 3.4 %collective-permute-done.25.refs_7_ = f32[32,16,128]{2,1,0:T(8,128)S(1)} collective-permute-done((f32[32,16,128]{2,1,0:T(8,128)S(1)}, f32[32,16,128]{2,1,0:T(8,128)S(1)}, u32[]{:S(2)}, u32[]{:S(2)}) %collective-permute-start.25) | collective-permute-done | bytes 262176 | tf_op jit(solution)/shard_map/ppermute | solution.py:346
  235.0 2.9 %collective-permute-done.24.refs_6_ = f32[32,16,128]{2,1,0:T(8,128)S(1)} collective-permute-done((f32[32,16,128]{2,1,0:T(8,128)S(1)}, f32[32,16,128]{2,1,0:T(8,128)S(1)}, u32[]{:S(2)}, u32[]{:S(2)}) %collective-permute-start.24) | collective-permute-done | bytes 262176 | tf_op jit(solution)/shard_map/ppermute | solution.py:346
  237.9 7.8 %collective-permute-done.23.refs_5_ = f32[32,16,128]{2,1,0:T(8,128)S(1)} collective-permute-done((f32[32,16,128]{2,1,0:T(8,128)S(1)}, f32[32,16,128]{2,1,0:T(8,128)S(1)}, u32[]{:S(2)}, u32[]{:S(2)}) %collective-permute-start.23) | collective-permute-done | bytes 262176 | tf_op jit(solution)/shard_map/ppermute | solution.py:346
  245.7 2.8 %shard_map.59 = f32[4096,128]{1,0:T(8,128)} custom-call(s32[4]{0:T(128)S(1)} %and_select_fusion.3.place, f32[4096,128]{1,0:T(8,128)S(1)} %bitcast.50, f32[8,2,32,128]{3,2,1,0:T(8,128)S(1)} %shard_map.54.refs_0_, f32[8,2,32,128]{3,2,1,0:T(8,128)S(1)} %collective-permute-done.14.refs_1_, f32[8,2,32,128]{3,2,1,0:T(8,128)S(1)} %collective-permute-done.15.refs_2_, ...), custom_call_target="tpu_custom_call" | custom-call | bytes 6291456 | tf_op jit(solution)/shard_map/pallas_call | solution.py:38
  (133 shorter events, 42.3 us)
Async XLA Ops:
  4.0 23.1 %collective-permute-start.2 = (s32[2,32]{1,0:T(2,128)S(1)}, s32[2,32]{1,0:T(2,128)S(1)}, u32[]{:S(2)}, u32[]{:S(2)}) collective-permute-start(s32[2,32]{1,0:T(2,128)S(1)} %select_reduce_fusion.2.table.refs_0_), channel_id=1, source_target_pairs={{0,96},{32,0},{64,32},{96,64},{1,97},{33,1},{65,33},{97,65},{2,98}... | collective-permute-start | bytes 776 | tf_op jit(solution)/shard_map/ppermute | solution.py:346
  8.7 18.5 %collective-permute-start.1 = (s32[2,32]{1,0:T(2,128)S(1)}, s32[2,32]{1,0:T(2,128)S(1)}, u32[]{:S(2)}, u32[]{:S(2)}) collective-permute-start(s32[2,32]{1,0:T(2,128)S(1)} %select_reduce_fusion.2.table.refs_0_), channel_id=1, source_target_pairs={{0,64},{32,96},{64,0},{96,32},{1,65},{33,97},{65,1},{97,33},{2,66}... | collective-permute-start | bytes 776 | tf_op jit(solution)/shard_map/ppermute | solution.py:346
  8.7 18.5 %collective-permute-start = (s32[2,32]{1,0:T(2,128)S(1)}, s32[2,32]{1,0:T(2,128)S(1)}, u32[]{:S(2)}, u32[]{:S(2)}) collective-permute-start(s32[2,32]{1,0:T(2,128)S(1)} %select_reduce_fusion.2.table.refs_0_), channel_id=1, source_target_pairs={{0,32},{32,64},{64,96},{96,0},{1,33},{33,65},{65,97},{97,1},{2,34}... | collective-permute-start | bytes 776 | tf_op jit(solution)/shard_map/ppermute | solution.py:346
  14.3 59.5 %all-to-all-start = ((f32[32,2,4,32,128]{4,3,2,1,0:T(8,128)}), f32[32,2,4,32,128]{4,3,2,1,0:T(8,128)}, u32[]{:S(2)}, u32[]{:S(2)}) async-start(f32[32,2,4,32,128]{4,3,2,1,0:T(8,128)} %get-tuple-element.51), calls=%async_computation | async-start | bytes 8388608 | tf_op jit(solution)/shard_map/all_to_all | solution.py:350
  26.5 47.3 %copy-start.16 = (f32[1,4,32,128]{3,2,1,0:T(8,128)S(1)}, f32[1,4,32,128]{3,2,1,0:T(8,128)}, u32[]{:S(2)}) copy-start(f32[1,4,32,128]{3,2,1,0:T(8,128)} %get-tuple-element.53.kept) | copy-start | bytes 196612
  76.9 16.9 %collective-permute-start.5 = (f32[128,16,128]{2,1,0:T(8,128)}, f32[128,16,128]{2,1,0:T(8,128)}, u32[]{:S(2)}, u32[]{:S(2)}) collective-permute-start(f32[128,16,128]{2,1,0:T(8,128)} %get-tuple-element.59.high), channel_id=1, source_target_pairs={{0,1},{1,2},{2,3},{3,4},{4,5},{5,6},{6,7},{7,8},{8,9},{9,10},{10,1... | collective-permute-start | bytes 3145736 | tf_op jit(solution)/shard_map/ppermute | solution.py:346
  81.2 16.2 %collective-permute-start.6 = (f32[128,16,128]{2,1,0:T(8,128)S(1)}, f32[128,16,128]{2,1,0:T(8,128)}, u32[]{:S(2)}, u32[]{:S(2)}) collective-permute-start(f32[128,16,128]{2,1,0:T(8,128)S(1)} %get-tuple-element.54.low), channel_id=1, source_target_pairs={{1,0},{2,1},{3,2},{4,3},{5,4},{6,5},{7,6},{8,7},{9,8},{10,9},{11,1... | collective-permute-start | bytes 3145736 | tf_op jit(solution)/shard_map/ppermute | solution.py:346
  88.2 24.1 %collective-permute-start.3 = (f32[128,16,128]{2,1,0:T(8,128)}, f32[128,16,128]{2,1,0:T(8,128)}, u32[]{:S(2)}, u32[]{:S(2)}) collective-permute-start(f32[128,16,128]{2,1,0:T(8,128)} %get-tuple-element.69.high), channel_id=1, source_target_pairs={{0,1},{1,2},{2,3},{3,4},{4,5},{5,6},{6,7},{7,8},{8,9},{9,10},{10,1... | collective-permute-start | bytes 3145736 | tf_op jit(solution)/shard_map/ppermute | solution.py:346
  90.3 22.0 %collective-permute-start.4 = (f32[128,16,128]{2,1,0:T(8,128)}, f32[128,16,128]{2,1,0:T(8,128)}, u32[]{:S(2)}, u32[]{:S(2)}) collective-permute-start(f32[128,16,128]{2,1,0:T(8,128)} %get-tuple-element.68.low), channel_id=1, source_target_pairs={{1,0},{2,1},{3,2},{4,3},{5,4},{6,5},{7,6},{8,7},{9,8},{10,9},{11,1... | collective-permute-start | bytes 3145736 | tf_op jit(solution)/shard_map/ppermute | solution.py:346
  107.6 19.6 %copy-start.1 = (f32[2048,128]{1,0:T(8,128)}, f32[2048,128]{1,0:T(8,128)S(1)}, u32[]{:S(2)}) copy-start(f32[2048,128]{1,0:T(8,128)S(1)} %get-tuple-element.66) | copy-start | bytes 3145732
  107.6 19.6 %collective-permute-start.9 = (f32[128,16,128]{2,1,0:T(8,128)S(1)}, f32[128,16,128]{2,1,0:T(8,128)S(1)}, u32[]{:S(2)}, u32[]{:S(2)}) collective-permute-start(f32[128,16,128]{2,1,0:T(8,128)S(1)} %bitcast.54), channel_id=1, source_target_pairs={{0,1},{1,2},{2,3},{3,4},{4,5},{5,6},{6,7},{7,8},{8,9},{9,10},{10,1... | collective-permute-start | bytes 3145736 | tf_op jit(solution)/shard_map/ppermute | solution.py:346
  109.6 17.7 %collective-permute-start.10 = (f32[128,16,128]{2,1,0:T(8,128)S(1)}, f32[128,16,128]{2,1,0:T(8,128)S(1)}, u32[]{:S(2)}, u32[]{:S(2)}) collective-permute-start(f32[128,16,128]{2,1,0:T(8,128)S(1)} %bitcast.51), channel_id=1, source_target_pairs={{1,0},{2,1},{3,2},{4,3},{5,4},{6,5},{7,6},{8,7},{9,8},{10,9},{11,1... | collective-permute-start | bytes 3145736 | tf_op jit(solution)/shard_map/ppermute | solution.py:346
  121.6 16.1 %collective-permute-start.8 = (f32[128,16,128]{2,1,0:T(8,128)S(1)}, f32[128,16,128]{2,1,0:T(8,128)S(1)}, u32[]{:S(2)}, u32[]{:S(2)}) collective-permute-start(f32[128,16,128]{2,1,0:T(8,128)S(1)} %bitcast.57), channel_id=1, source_target_pairs={{1,0},{2,1},{3,2},{4,3},{5,4},{6,5},{7,6},{8,7},{9,8},{10,9},{11,1... | collective-permute-start | bytes 3145736 | tf_op jit(solution)/shard_map/ppermute | solution.py:346
  123.5 15.4 %collective-permute-start.7 = (f32[128,16,128]{2,1,0:T(8,128)S(1)}, f32[128,16,128]{2,1,0:T(8,128)S(1)}, u32[]{:S(2)}, u32[]{:S(2)}) collective-permute-start(f32[128,16,128]{2,1,0:T(8,128)S(1)} %bitcast.60), channel_id=1, source_target_pairs={{0,1},{1,2},{2,3},{3,4},{4,5},{5,6},{6,7},{7,8},{8,9},{9,10},{10,1... | collective-permute-start | bytes 3145736 | tf_op jit(solution)/shard_map/ppermute | solution.py:346
  141.7 46.8 %all-to-all-start.1 = ((f32[32,2,2,32,128]{4,3,2,1,0:T(8,128)}), f32[32,2,2,32,128]{4,3,2,1,0:T(8,128)S(1)}, u32[]{:S(2)}, u32[]{:S(2)}) async-start(f32[32,2,2,32,128]{4,3,2,1,0:T(8,128)} %get-tuple-element.75), calls=%async_computation.1 | async-start | bytes 4194304 | tf_op jit(solution)/shard_map/all_to_all | solution.py:350
  160.2 9.1 %collective-permute-start.18 = (f32[33,16,128]{2,1,0:T(8,128)S(1)}, f32[33,16,128]{2,1,0:T(8,128)S(1)}, u32[]{:S(2)}, u32[]{:S(2)}) collective-permute-start(f32[33,16,128]{2,1,0:T(8,128)S(1)} %get-tuple-element.89), channel_id=1, source_target_pairs={{0,32},{32,64},{64,96},{96,0},{1,33},{33,65},{65,97},{97,1},{2,34}... | collective-permute-start | bytes 811016 | tf_op jit(solution)/shard_map/ppermute | solution.py:346
  162.2 13.1 %collective-permute-start.20 = (f32[33,16,128]{2,1,0:T(8,128)S(1)}, f32[33,16,128]{2,1,0:T(8,128)S(1)}, u32[]{:S(2)}, u32[]{:S(2)}) collective-permute-start(f32[33,16,128]{2,1,0:T(8,128)S(1)} %get-tuple-element.91), channel_id=1, source_target_pairs={{0,64},{32,96},{64,0},{96,32},{1,65},{33,97},{65,1},{97,33},{2,66}... | collective-permute-start | bytes 811016 | tf_op jit(solution)/shard_map/ppermute | solution.py:346
  163.2 12.4 %collective-permute-start.22 = (f32[33,16,128]{2,1,0:T(8,128)S(1)}, f32[33,16,128]{2,1,0:T(8,128)S(1)}, u32[]{:S(2)}, u32[]{:S(2)}) collective-permute-start(f32[33,16,128]{2,1,0:T(8,128)S(1)} %get-tuple-element.93), channel_id=1, source_target_pairs={{0,96},{32,0},{64,32},{96,64},{1,97},{33,1},{65,33},{97,65},{2,98}... | collective-permute-start | bytes 811016 | tf_op jit(solution)/shard_map/ppermute | solution.py:346
  166.1 15.3 %collective-permute-start.17 = (f32[33,16,128]{2,1,0:T(8,128)S(1)}, f32[33,16,128]{2,1,0:T(8,128)S(1)}, u32[]{:S(2)}, u32[]{:S(2)}) collective-permute-start(f32[33,16,128]{2,1,0:T(8,128)S(1)} %get-tuple-element.88), channel_id=1, source_target_pairs={{0,32},{32,64},{64,96},{96,0},{1,33},{33,65},{65,97},{97,1},{2,34}... | collective-permute-start | bytes 811016 | tf_op jit(solution)/shard_map/ppermute | solution.py:346
  166.2 20.7 %collective-permute-start.19 = (f32[33,16,128]{2,1,0:T(8,128)S(1)}, f32[33,16,128]{2,1,0:T(8,128)S(1)}, u32[]{:S(2)}, u32[]{:S(2)}) collective-permute-start(f32[33,16,128]{2,1,0:T(8,128)S(1)} %get-tuple-element.90), channel_id=1, source_target_pairs={{0,64},{32,96},{64,0},{96,32},{1,65},{33,97},{65,1},{97,33},{2,66}... | collective-permute-start | bytes 811016 | tf_op jit(solution)/shard_map/ppermute | solution.py:346
  169.3 17.8 %collective-permute-start.21 = (f32[33,16,128]{2,1,0:T(8,128)S(1)}, f32[33,16,128]{2,1,0:T(8,128)S(1)}, u32[]{:S(2)}, u32[]{:S(2)}) collective-permute-start(f32[33,16,128]{2,1,0:T(8,128)S(1)} %get-tuple-element.92), channel_id=1, source_target_pairs={{0,96},{32,0},{64,32},{96,64},{1,97},{33,1},{65,33},{97,65},{2,98}... | collective-permute-start | bytes 811016 | tf_op jit(solution)/shard_map/ppermute | solution.py:346
  188.5 37.2 %all-to-all-start.2 = ((f32[32,4,2,16,128]{4,3,2,1,0:T(8,128)}), f32[32,4,2,16,128]{4,3,2,1,0:T(8,128)}, u32[]{:S(2)}, u32[]{:S(2)}) async-start(f32[32,4,2,16,128]{4,3,2,1,0:T(8,128)} %get-tuple-element.95), calls=%async_computation.2 | async-start | bytes 4194304 | tf_op jit(solution)/shard_map/all_to_all | solution.py:350
  197.9 47.8 %copy-start = (f32[32,128,128]{2,1,0:T(8,128)S(1)}, f32[32,128,128]{2,1,0:T(8,128)}, u32[]{:S(2)}) copy-start(f32[32,128,128]{2,1,0:T(8,128)} %param.4) | copy-start | bytes 6291460
  197.9 8.9 %collective-permute-start.11 = (f32[8,2,32,128]{3,2,1,0:T(8,128)S(1)}, f32[8,2,32,128]{3,2,1,0:T(8,128)S(1)}, u32[]{:S(2)}, u32[]{:S(2)}) collective-permute-start(f32[8,2,32,128]{3,2,1,0:T(8,128)S(1)} %get-tuple-element.79), channel_id=1, source_target_pairs={{0,32},{32,64},{64,96},{96,0},{1,33},{33,65},{65,97},{97,1},{2,34}... | collective-permute-start | bytes 786440 | tf_op jit(solution)/shard_map/ppermute | solution.py:346
  199.3 13.9 %collective-permute-start.12 = (f32[8,2,32,128]{3,2,1,0:T(8,128)S(1)}, f32[8,2,32,128]{3,2,1,0:T(8,128)S(1)}, u32[]{:S(2)}, u32[]{:S(2)}) collective-permute-start(f32[8,2,32,128]{3,2,1,0:T(8,128)S(1)} %get-tuple-element.80), channel_id=1, source_target_pairs={{0,64},{32,96},{64,0},{96,32},{1,65},{33,97},{65,1},{97,33},{2,66}... | collective-permute-start | bytes 786440 | tf_op jit(solution)/shard_map/ppermute | solution.py:346
  201.4 11.8 %collective-permute-start.13 = (f32[8,2,32,128]{3,2,1,0:T(8,128)S(1)}, f32[8,2,32,128]{3,2,1,0:T(8,128)S(1)}, u32[]{:S(2)}, u32[]{:S(2)}) collective-permute-start(f32[8,2,32,128]{3,2,1,0:T(8,128)S(1)} %get-tuple-element.81), channel_id=1, source_target_pairs={{0,96},{32,0},{64,32},{96,64},{1,97},{33,1},{65,33},{97,65},{2,98}... | collective-permute-start | bytes 786440 | tf_op jit(solution)/shard_map/ppermute | solution.py:346
  213.3 17.9 %collective-permute-start.16 = (f32[8,2,32,128]{3,2,1,0:T(8,128)S(1)}, f32[8,2,32,128]{3,2,1,0:T(8,128)S(1)}, u32[]{:S(2)}, u32[]{:S(2)}) collective-permute-start(f32[8,2,32,128]{3,2,1,0:T(8,128)S(1)} %shard_map.54.refs_0_), channel_id=1, source_target_pairs={{0,96},{32,0},{64,32},{96,64},{1,97},{33,1},{65,33},{97,65},{2,98}... | collective-permute-start | bytes 786440 | tf_op jit(solution)/shard_map/ppermute | solution.py:346
  216.2 15.1 %collective-permute-start.15 = (f32[8,2,32,128]{3,2,1,0:T(8,128)S(1)}, f32[8,2,32,128]{3,2,1,0:T(8,128)S(1)}, u32[]{:S(2)}, u32[]{:S(2)}) collective-permute-start(f32[8,2,32,128]{3,2,1,0:T(8,128)S(1)} %shard_map.54.refs_0_), channel_id=1, source_target_pairs={{0,64},{32,96},{64,0},{96,32},{1,65},{33,97},{65,1},{97,33},{2,66}... | collective-permute-start | bytes 786440 | tf_op jit(solution)/shard_map/ppermute | solution.py:346
  216.8 14.8 %collective-permute-start.14 = (f32[8,2,32,128]{3,2,1,0:T(8,128)S(1)}, f32[8,2,32,128]{3,2,1,0:T(8,128)S(1)}, u32[]{:S(2)}, u32[]{:S(2)}) collective-permute-start(f32[8,2,32,128]{3,2,1,0:T(8,128)S(1)} %shard_map.54.refs_0_), channel_id=1, source_target_pairs={{0,32},{32,64},{64,96},{96,0},{1,33},{33,65},{65,97},{97,1},{2,34}... | collective-permute-start | bytes 786440 | tf_op jit(solution)/shard_map/ppermute | solution.py:346
  228.0 7.0 %collective-permute-start.25 = (f32[32,16,128]{2,1,0:T(8,128)S(1)}, f32[32,16,128]{2,1,0:T(8,128)S(1)}, u32[]{:S(2)}, u32[]{:S(2)}) collective-permute-start(f32[32,16,128]{2,1,0:T(8,128)S(1)} %shard_map.58.refs_4_), channel_id=1, source_target_pairs={{0,96},{32,0},{64,32},{96,64},{1,97},{33,1},{65,33},{97,65},{2,98}... | collective-permute-start | bytes 786440 | tf_op jit(solution)/shard_map/ppermute | solution.py:346
  230.3 7.5 %collective-permute-start.24 = (f32[32,16,128]{2,1,0:T(8,128)S(1)}, f32[32,16,128]{2,1,0:T(8,128)S(1)}, u32[]{:S(2)}, u32[]{:S(2)}) collective-permute-start(f32[32,16,128]{2,1,0:T(8,128)S(1)} %shard_map.58.refs_4_), channel_id=1, source_target_pairs={{0,64},{32,96},{64,0},{96,32},{1,65},{33,97},{65,1},{97,33},{2,66}... | collective-permute-start | bytes 786440 | tf_op jit(solution)/shard_map/ppermute | solution.py:346
  231.2 14.5 %collective-permute-start.23 = (f32[32,16,128]{2,1,0:T(8,128)S(1)}, f32[32,16,128]{2,1,0:T(8,128)S(1)}, u32[]{:S(2)}, u32[]{:S(2)}) collective-permute-start(f32[32,16,128]{2,1,0:T(8,128)S(1)} %shard_map.58.refs_4_), channel_id=1, source_target_pairs={{0,32},{32,64},{64,96},{96,0},{1,33},{33,65},{65,97},{97,1},{2,34}... | collective-permute-start | bytes 786440 | tf_op jit(solution)/shard_map/ppermute | solution.py:346
  (17 other events, 102.0 us)

commit v3 on v2

--- a/solution.py
+++ b/solution.py
@@ -37,7 +37,7 @@
     ]
     return pl.pallas_call(
         kernel,
-        out_shape=[pltpu.HBM(s, F32) if n in far else jax.ShapeDtypeStruct(s, F32) for n, s in enumerate(outs)],
+        out_shape=[(pltpu.HBM if n in far else jax.ShapeDtypeStruct)(s, F32) for n, s in enumerate(outs)],
         grid=grid,
         in_specs=in_specs,
         out_specs=out_specs or [VMEM] * len(outs),
@@ -71,24 +71,39 @@
     return full[:, :NX] + full[:, NX:]
 
 
-def pack_kernel(table, last, est, send, kept0, kept1, turned):
-    for z in range(ROWS):
-        turned[pl.ds(z * PITCH, NY), :] = est[pl.ds(z * NY, NY), :]
-
-    def rows(tile, j):
-        return turned[pl.ds(tile * YT + j, ROWS, stride=PITCH), :]
-
-    def step(slot, carry):
-        for v in range(2):
-            tile = table[v, slot]
-            for j in range(YT):
-                send[slot, v, j] = rows(tile, j)
-        return carry
-
-    lax.fori_loop(0, GRID, step, 0, unroll=4)
+def pack_kernel(table, last, est, send, kept0, kept1, block, turned, in_sems, out_sem, kept_sem):
+    count = in_sems.shape[0]
+    rows = ZD // count
+    loads = []
+    for n in range(count):
+        part = pl.ds(n * rows * NY, rows * NY)
+        loads.append(pltpu.make_async_copy(est.at[part], block.at[part], in_sems.at[n]))
+        loads[-1].start()
+    for n, load in enumerate(loads):
+        load.wait()
+
+        def turn(z, carry):
+            at = pl.multiple_of(z * NY, NY)
+            turned[pl.ds(z, NY, stride=WORK), :] = block[pl.ds(at, NY), :]
+            return carry
+
+        lax.fori_loop(n * rows, (n + 1) * rows, turn, 0, unroll=4)
+
+    def tile(index):
+        return tiles.at[pl.ds(index * YT, YT), pl.ds(0, ZD), :]
+
+    tiles = turned.reshape(NY, WORK, NX)
     for v, kept in enumerate((kept0, kept1)):
-        for j in range(YT):
-            kept[0, j] = rows(last[v], j)
+
+        def step(slot, carry, v=v):
+            pltpu.make_async_copy(tile(table[v, slot]), send.at[slot, v], out_sem).start()
+            return carry
+
+        lax.fori_loop(0, GRID, step, 0, unroll=4)
+        pltpu.make_async_copy(tile(last[v]), kept.at[0], kept_sem.at[v]).start()
+    pltpu.make_async_copy(send, send, out_sem).wait()
+    for v, kept in enumerate((kept0, kept1)):
+        pltpu.make_async_copy(kept, kept, kept_sem.at[v]).wait()
 
 
 def unpack_kernel(v, table, recv, kept, low, high, sems):
@@ -161,13 +176,13 @@
 
 
 def adjoint_first_kernel(v, table, top, low, high, bottom, zmat, *refs):
-    parts = (top, low, high, bottom)
+    parts = [p.reshape(NY // 2, PAD, NX) for p in (top, low, high, bottom)]
     send, kept = refs[-2:]
     slots = send.shape[0]
     base = pl.program_id(0) * slots
 
     def move(c):
-        done = left_dot(zmat[v], padded_pair(parts, c * YT, c * YT + 1))
+        done = left_dot(zmat[v], padded_pair(parts, c * 2, c * 2 + 1))
         return done[:, :NX], done[:, NX:]
 
     def step(slot, carry):
@@ -182,11 +197,11 @@
 
 
 def adjoint_last_kernel(v, table, plane, top, low, high, bottom, zmat, *refs):
-    parts = (top, low, high, bottom)
+    parts = [p.reshape(NY // 2, PAD, NX) for p in (top, low, high, bottom)]
     *outs, work = refs
 
     def step(slot, carry):
-        y = table[v, slot] * YT + 2
+        y = table[v, slot] * 2
         done = left_dot(zmat[v], padded_pair(parts, y, y + 1))
         work[slot, pl.ds(0, ZD), :] = done[:, :NX]
         work[slot, pl.ds(ZD, ZD), :] = done[:, NX:]
@@ -358,7 +373,7 @@
     own = lax.axis_index("slab")
     plane = lax.axis_index("view")
     pack, last, place, chosen, arriving = tables(tile_map, own)
-    mats = bands(psf_taps, own)
+    mats = [pltpu.with_memory_space_constraint(m, pltpu.HBM) for m in bands(psf_taps, own)]
     est = estimate.reshape(ZD * NY, NX)
     far_est = pltpu.with_memory_space_constraint(est, pltpu.HBM)
     rec = recorded.reshape(-1, ZD * NY, NX)
@@ -398,19 +413,19 @@
 
     far_rec = pltpu.with_memory_space_constraint(rec, pltpu.HBM)
     views = rec.shape[0]
-    steps = lambda *block: pl.BlockSpec(block, lambda s: (*[0] * (len(block) - 2), s, 0))
     send, *kept = call(
         pack_kernel,
         (pack, last, far_est),
         ((GRID, views, YT, ZD, NX), (1, YT, ZD, NX), (1, YT, ZD, NX)),
-        ins={2: steps(ROWS * NY, NX)},
-        out_specs=[
-            steps(GRID, views, YT, ROWS, NX),
-            steps(1, YT, ROWS, NX),
-            steps(1, YT, ROWS, NX),
+        ins={2: ANY},
+        out_specs=[ANY, ANY, ANY],
+        scratch=[
+            pltpu.VMEM((ZD * NY, NX), F32),
+            pltpu.VMEM((NY * WORK, NX), F32),
+            pltpu.SemaphoreType.DMA((STEPS,)),
+            pltpu.SemaphoreType.DMA,
+            pltpu.SemaphoreType.DMA((views,)),
         ],
-        grid=(STEPS,),
-        scratch=[pltpu.VMEM((ROWS * PITCH, NX), F32)],
         moved=2 * big,
         far=(0, 1, 2),
     )
@@ -428,18 +443,21 @@
     ready1 = padded(*back1)
     half = (GRID, views, 2, ZD, NX)
 
+    def rows_of_tiles(at, which):
+        return {at + n: pl.BlockSpec((GRID, 2, PAD, NX), lambda s: (0, which, 0, 0)) for n in range(4)}
+
     def adjoint_first(v, parts, buffer=None):
-        operands = (chosen, *parts, mats[5])
+        operands = (chosen, *[p.reshape(GRID, YT, PAD, NX) for p in parts], mats[5])
         return call(
             functools.partial(adjoint_first_kernel, v),
             operands if buffer is None else (*operands, buffer),
             (half, (2, ZD, NX)),
-            ins={6: ANY},
+            ins=rows_of_tiles(1, 0) | {6: ANY},
             out_specs=[
-                pl.BlockSpec((GRID // STEPS, 1, 2, ZD, NX), lambda s: (s, v, 0, 0, 0)),
+                pl.BlockSpec((GRID // 2, 1, 2, ZD, NX), lambda s: (s, v, 0, 0, 0)),
                 pl.BlockSpec((2, ZD, NX), lambda s: (0, 0, 0)),
             ],
-            grid=(STEPS,),
+            grid=(2,),
             flops=1 << 30,
             moved=2 * big,
             far=(0,),
@@ -449,8 +467,10 @@
     def adjoint_last(v, parts):
         return call(
             functools.partial(adjoint_last_kernel, v),
-            (chosen, plane.reshape(1), *parts, mats[5]),
+            (chosen, plane.reshape(1), *[p.reshape(GRID, YT, PAD, NX) for p in parts], mats[5]),
             ((GRID + 1, PAD, NX),) * PLANES,
+            ins=rows_of_tiles(2, 1),
+            grid=(1,),
             scratch=[pltpu.VMEM((GRID + 1, 2 * ZD, NX), F32)],
             flops=1 << 30,
             moved=2 * big,

time: 250 us -> 250 us (level)
  waiting for transfers between devices: 112 us -> 107 us
  local copies, waits for them, and re-layouts: 6.76 us -> 10.4 us
  other arithmetic: 7.63 us -> 10.4 us
    all_to_all x3, waiting for transfers between devices: 55.4 us -> 52.7 us  [exchange(): return lax.all_to_all(value, axis, 0, 0, tiled=True)]
    unnamed x40 -> x44, local copies, waits for them, and re-layouts: 6.18 us -> 7.41 us
  transfers between devices with their start and end apart: 29 -> 29, of which waited for: 17 -> 17; matrix products, arithmetic and copies ran while one was open for 2% -> 4% of each run, Pallas kernels for 15% -> 15%
where the time goes in v3:
time: 250 us; the launch traced here: 248 us
  waiting for transfers between devices  107 us (43%)
  starting transfers between devices  76.7 us (31%)
  Pallas kernels  43.5 us (17%)
  other arithmetic  10.4 us (4%)
  local copies, waits for them, and re-layouts  10.4 us (4%)
    ppermute x26, waiting for transfers between devices, shifted(): return lax.ppermute(value, axis, pairs)  54.1 us
    all_to_all x3, waiting for transfers between devices, exchange(): return lax.all_to_all(value, axis, 0, 0, tiled=True)  52.7 us
    ppermute x26, starting transfers between devices, shifted(): return lax.ppermute(value, axis, pairs)  46.9 us
    pallas_call x14, Pallas kernels, call(): pl.pallas_call(kernel, out_shape=[(pltpu.HBM if n in far else jax.ShapeDt...  43.5 us
    all_to_all x3, starting transfers between devices, exchange(): return lax.all_to_all(value, axis, 0, 0, tiled=True)  29.7 us
    unnamed x44, local copies, waits for them, and re-layouts  7.41 us
  transfers between devices with their start and end apart: 29, of which 17 were waited for; matrix products, arithmetic and copies ran while one was open for 4% of the time, Pallas kernels for 15%

profile of v3, /device:TPU:1, one launch (start us, length us, event | category | flops | bytes accessed | tf_op | source)
XLA Modules:
  0.0 248.3 jit_solution(4045257380242832798)
XLA Ops:
  4.0 4.6 %collective-permute-start.2 = (s32[2,32]{1,0:T(2,128)S(1)}, s32[2,32]{1,0:T(2,128)S(1)}, u32[]{:S(2)}, u32[]{:S(2)}) collective-permute-start(s32[2,32]{1,0:T(2,128)S(1)} %select_reduce_fusion.2.table.refs_0_), channel_id=1, source_target_pairs={{0,96},{32,0},{64,32},{96,64},{1,97},{33,1},{65,33},{97,65},{2,98}... | collective-permute-start | bytes 776 | tf_op jit(solution)/shard_map/ppermute | solution.py:361
  9.4 4.2 %shard_map.46 = (f32[32,2,4,32,128]{4,3,2,1,0:T(8,128)}, f32[1,4,32,128]{3,2,1,0:T(8,128)}, f32[1,4,32,128]{3,2,1,0:T(8,128)}) custom-call(s32[2,32]{1,0:T(2,128)S(1)} %and_select_fusion.1.table, s32[2]{0:T(128)S(1)} %get-tuple-element.119.last, f32[4096,128]{1,0:T(8,128)} %bitcast.57), custom_call_target="tpu_custom_call" | custom-call | bytes 4194304 | tf_op jit(solution)/shard_map/pallas_call | solution.py:38
  13.7 8.7 %all-to-all-start = ((f32[32,2,4,32,128]{4,3,2,1,0:T(8,128)}), f32[32,2,4,32,128]{4,3,2,1,0:T(8,128)}, u32[]{:S(2)}, u32[]{:S(2)}) async-start(f32[32,2,4,32,128]{4,3,2,1,0:T(8,128)} %get-tuple-element.51), calls=%async_computation | async-start | bytes 8388608 | tf_op jit(solution)/shard_map/all_to_all | solution.py:365
  29.1 43.9 %all-to-all-done.recv = f32[32,2,4,32,128]{4,3,2,1,0:T(8,128)} async-done(((f32[32,2,4,32,128]{4,3,2,1,0:T(8,128)}), f32[32,2,4,32,128]{4,3,2,1,0:T(8,128)}, u32[]{:S(2)}, u32[]{:S(2)}) %all-to-all-start) | async-done | bytes 4194336 | tf_op jit(solution)/shard_map/all_to_all | solution.py:365
  73.0 2.1 shard_map.47
  75.1 4.3 %collective-permute-start.5 = (f32[128,16,128]{2,1,0:T(8,128)S(1)}, f32[128,16,128]{2,1,0:T(8,128)}, u32[]{:S(2)}, u32[]{:S(2)}) collective-permute-start(f32[128,16,128]{2,1,0:T(8,128)S(1)} %get-tuple-element.59.high), channel_id=1, source_target_pairs={{0,1},{1,2},{2,3},{3,4},{4,5},{5,6},{6,7},{7,8},{8,9},{9,10},{10,1... | collective-permute-start | bytes 3145736 | tf_op jit(solution)/shard_map/ppermute | solution.py:361
  79.4 3.5 %collective-permute-start.6 = (f32[128,16,128]{2,1,0:T(8,128)S(1)}, f32[128,16,128]{2,1,0:T(8,128)}, u32[]{:S(2)}, u32[]{:S(2)}) collective-permute-start(f32[128,16,128]{2,1,0:T(8,128)S(1)} %get-tuple-element.54.low), channel_id=1, source_target_pairs={{1,0},{2,1},{3,2},{4,3},{5,4},{6,5},{7,6},{8,7},{9,8},{10,9},{11,1... | collective-permute-start | bytes 3145736 | tf_op jit(solution)/shard_map/ppermute | solution.py:361
  83.0 3.1 %shard_map.48 = (f32[128,16,128]{2,1,0:T(8,128)S(1)}, f32[128,16,128]{2,1,0:T(8,128)}) custom-call(s32[2,32]{1,0:T(2,128)S(1)} %broadcast_select_fusion.1.table, f32[32,2,4,32,128]{4,3,2,1,0:T(8,128)} %all-to-all-done.recv, f32[1,4,32,128]{3,2,1,0:T(8,128)S(1)} %copy-done.15), custom_call_target="tpu_custom_call" | custom-call | bytes 4194304 | tf_op jit(solution)/shard_map/pallas_call | solution.py:38
  88.2 3.2 %collective-permute-start.4 = (f32[128,16,128]{2,1,0:T(8,128)S(1)}, f32[128,16,128]{2,1,0:T(8,128)}, u32[]{:S(2)}, u32[]{:S(2)}) collective-permute-start(f32[128,16,128]{2,1,0:T(8,128)S(1)} %get-tuple-element.68.low), channel_id=1, source_target_pairs={{1,0},{2,1},{3,2},{4,3},{5,4},{6,5},{7,6},{8,7},{9,8},{10,9},{11,1... | collective-permute-start | bytes 3145736 | tf_op jit(solution)/shard_map/ppermute | solution.py:361
  98.1 8.8 %shard_map.49 = (f32[2048,128]{1,0:T(8,128)S(1)}, f32[2048,128]{1,0:T(8,128)S(1)}) custom-call(f32[128,16,128]{2,1,0:T(8,128)} %collective-permute-done.5.top, f32[128,16,128]{2,1,0:T(8,128)S(1)} %copy-done.18, f32[128,16,128]{2,1,0:T(8,128)S(1)} %copy-done.20, f32[128,16,128]{2,1,0:T(8,128)} %collective-permute-done.6.bottom, f32[2,4096,128]{2,1,0:T(8,128)} %bitcast.84, ...), custom_call_target="tpu_custom_call" | custom-call | flops 5368709120 | bytes 8388608 | tf_op jit(solution)/shard_map/pallas_call | solution.py:38
  108.9 2.6 %collective-permute-start.10 = (f32[128,16,128]{2,1,0:T(8,128)S(1)}, f32[128,16,128]{2,1,0:T(8,128)S(1)}, u32[]{:S(2)}, u32[]{:S(2)}) collective-permute-start(f32[128,16,128]{2,1,0:T(8,128)S(1)} %bitcast.59), channel_id=1, source_target_pairs={{1,0},{2,1},{3,2},{4,3},{5,4},{6,5},{7,6},{8,7},{9,8},{10,9},{11,1... | collective-permute-start | bytes 3145736 | tf_op jit(solution)/shard_map/ppermute | solution.py:361
  111.5 9.1 %shard_map.50 = (f32[2048,128]{1,0:T(8,128)S(1)}, f32[2048,128]{1,0:T(8,128)S(1)}) custom-call(f32[128,16,128]{2,1,0:T(8,128)} %collective-permute-done.3.top, f32[128,16,128]{2,1,0:T(8,128)S(1)} %get-tuple-element.68.low, f32[128,16,128]{2,1,0:T(8,128)} %get-tuple-element.69.high, f32[128,16,128]{2,1,0:T(8,128)} %collective-permute-done.4.bottom, ...), custom_call_target="tpu_custom_call" | custom-call | flops 5368709120 | bytes 8388608 | tf_op jit(solution)/shard_map/pallas_call | solution.py:38
  122.6 3.6 %collective-permute-start.7 = (f32[128,16,128]{2,1,0:T(8,128)S(1)}, f32[128,16,128]{2,1,0:T(8,128)S(1)}, u32[]{:S(2)}, u32[]{:S(2)}) collective-permute-start(f32[128,16,128]{2,1,0:T(8,128)S(1)} %bitcast.72), channel_id=1, source_target_pairs={{0,1},{1,2},{2,3},{3,4},{4,5},{5,6},{6,7},{7,8},{8,9},{9,10},{10,1... | collective-permute-start | bytes 3145736 | tf_op jit(solution)/shard_map/ppermute | solution.py:361
  126.4 2.5 %shard_map.51 = (f32[32,2,2,32,128]{4,3,2,1,0:T(8,128)}, f32[2,32,128]{2,1,0:T(8,128)S(1)}) custom-call(s32[2,33]{1,0:T(2,128)S(1)} %select_reduce_fusion.6.table, f32[32,4,16,128]{3,2,1,0:T(8,128)S(1)} %bitcast.65, f32[32,4,16,128]{3,2,1,0:T(8,128)S(1)} %bitcast.60, f32[32,4,16,128]{3,2,1,0:T(8,128)S(1)} %bitcast.63, f32[32,4,16,128]{3,2,1,0:T(8,128)S(1)} %bitcast.67, ...), custom_call_target="tpu_custom_call" | custom-call | flops 1073741824 | bytes 4194304 | tf_op jit(solution)/shard_map/pallas_call | solution.py:38
  128.9 7.9 %collective-permute-done.8 = f32[128,16,128]{2,1,0:T(8,128)S(1)} collective-permute-done((f32[128,16,128]{2,1,0:T(8,128)S(1)}, f32[128,16,128]{2,1,0:T(8,128)S(1)}, u32[]{:S(2)}, u32[]{:S(2)}) %collective-permute-start.8) | collective-permute-done | bytes 1048608 | tf_op jit(solution)/shard_map/ppermute | solution.py:361
  138.0 2.5 %shard_map.52 = (f32[32,2,2,32,128]{4,3,2,1,0:T(8,128)}, f32[2,32,128]{2,1,0:T(8,128)S(1)}) custom-call(s32[2,33]{1,0:T(2,128)S(1)} %select_reduce_fusion.6.table, f32[32,4,16,128]{3,2,1,0:T(8,128)S(1)} %bitcast.77, f32[32,4,16,128]{3,2,1,0:T(8,128)S(1)} %bitcast.70, f32[32,4,16,128]{3,2,1,0:T(8,128)S(1)} %bitcast.73, ...), custom_call_target="tpu_custom_call", output_to_operand_aliasing={{0}: (6, {})} | custom-call | flops 1073741824 | bytes 4194304 | tf_op jit(solution)/shard_map/pallas_call | solution.py:38
  140.5 12.6 %all-to-all-start.1 = ((f32[32,2,2,32,128]{4,3,2,1,0:T(8,128)}), f32[32,2,2,32,128]{4,3,2,1,0:T(8,128)S(1)}, u32[]{:S(2)}, u32[]{:S(2)}) async-start(f32[32,2,2,32,128]{4,3,2,1,0:T(8,128)} %get-tuple-element.75), calls=%async_computation.1 | async-start | bytes 4194304 | tf_op jit(solution)/shard_map/all_to_all | solution.py:365
  169.5 5.6 %collective-permute-done.20.refs_5_ = f32[33,16,128]{2,1,0:T(8,128)S(1)} collective-permute-done((f32[33,16,128]{2,1,0:T(8,128)S(1)}, f32[33,16,128]{2,1,0:T(8,128)S(1)}, u32[]{:S(2)}, u32[]{:S(2)}) %collective-permute-start.20) | collective-permute-done | bytes 270368 | tf_op jit(solution)/shard_map/ppermute | solution.py:361
  175.4 5.8 %collective-permute-done.17.refs_2_ = f32[33,16,128]{2,1,0:T(8,128)S(1)} collective-permute-done((f32[33,16,128]{2,1,0:T(8,128)S(1)}, f32[33,16,128]{2,1,0:T(8,128)S(1)}, u32[]{:S(2)}, u32[]{:S(2)}) %collective-permute-start.17) | collective-permute-done | bytes 270368 | tf_op jit(solution)/shard_map/ppermute | solution.py:361
  181.2 5.5 %collective-permute-done.19.refs_4_ = f32[33,16,128]{2,1,0:T(8,128)S(1)} collective-permute-done((f32[33,16,128]{2,1,0:T(8,128)S(1)}, f32[33,16,128]{2,1,0:T(8,128)S(1)}, u32[]{:S(2)}, u32[]{:S(2)}) %collective-permute-start.19) | collective-permute-done | bytes 270368 | tf_op jit(solution)/shard_map/ppermute | solution.py:361
  188.3 8.4 %all-to-all-start.2 = ((f32[32,4,2,16,128]{4,3,2,1,0:T(8,128)}), f32[32,4,2,16,128]{4,3,2,1,0:T(8,128)}, u32[]{:S(2)}, u32[]{:S(2)}) async-start(f32[32,4,2,16,128]{4,3,2,1,0:T(8,128)} %get-tuple-element.95), calls=%async_computation.2 | async-start | bytes 4194304 | tf_op jit(solution)/shard_map/all_to_all | solution.py:365
  199.1 2.1 collective-permute-start.12
  202.1 4.4 %collective-permute-done.11.second = f32[8,2,32,128]{3,2,1,0:T(8,128)S(1)} collective-permute-done((f32[8,2,32,128]{3,2,1,0:T(8,128)S(1)}, f32[8,2,32,128]{3,2,1,0:T(8,128)S(1)}, u32[]{:S(2)}, u32[]{:S(2)}) %collective-permute-start.11) | collective-permute-done | bytes 262176 | tf_op jit(solution)/shard_map/ppermute | solution.py:361
  206.6 6.4 %collective-permute-done.12.third = f32[8,2,32,128]{3,2,1,0:T(8,128)S(1)} collective-permute-done((f32[8,2,32,128]{3,2,1,0:T(8,128)S(1)}, f32[8,2,32,128]{3,2,1,0:T(8,128)S(1)}, u32[]{:S(2)}, u32[]{:S(2)}) %collective-permute-start.12) | collective-permute-done | bytes 262176 | tf_op jit(solution)/shard_map/ppermute | solution.py:361
  213.1 2.9 %collective-permute-start.16 = (f32[8,2,32,128]{3,2,1,0:T(8,128)S(1)}, f32[8,2,32,128]{3,2,1,0:T(8,128)S(1)}, u32[]{:S(2)}, u32[]{:S(2)}) collective-permute-start(f32[8,2,32,128]{3,2,1,0:T(8,128)S(1)} %shard_map.54.refs_0_), channel_id=1, source_target_pairs={{0,96},{32,0},{64,32},{96,64},{1,97},{33,1},{65,33},{97,65},{2,98}... | collective-permute-start | bytes 786440 | tf_op jit(solution)/shard_map/ppermute | solution.py:361
  216.6 8.8 %all-to-all-done.2.refs_4_ = f32[32,4,2,16,128]{4,3,2,1,0:T(8,128)} async-done(((f32[32,4,2,16,128]{4,3,2,1,0:T(8,128)}), f32[32,4,2,16,128]{4,3,2,1,0:T(8,128)}, u32[]{:S(2)}, u32[]{:S(2)}) %all-to-all-start.2) | async-done | bytes 2097184 | tf_op jit(solution)/shard_map/all_to_all | solution.py:365
  225.4 2.3 shard_map.58.refs_4_
  227.7 2.4 collective-permute-start.25
  231.3 3.4 %collective-permute-done.25.refs_7_ = f32[32,16,128]{2,1,0:T(8,128)S(1)} collective-permute-done((f32[32,16,128]{2,1,0:T(8,128)S(1)}, f32[32,16,128]{2,1,0:T(8,128)S(1)}, u32[]{:S(2)}, u32[]{:S(2)}) %collective-permute-start.25) | collective-permute-done | bytes 262176 | tf_op jit(solution)/shard_map/ppermute | solution.py:361
  234.7 2.9 %collective-permute-done.24.refs_6_ = f32[32,16,128]{2,1,0:T(8,128)S(1)} collective-permute-done((f32[32,16,128]{2,1,0:T(8,128)S(1)}, f32[32,16,128]{2,1,0:T(8,128)S(1)}, u32[]{:S(2)}, u32[]{:S(2)}) %collective-permute-start.24) | collective-permute-done | bytes 262176 | tf_op jit(solution)/shard_map/ppermute | solution.py:361
  237.6 7.8 %collective-permute-done.23.refs_5_ = f32[32,16,128]{2,1,0:T(8,128)S(1)} collective-permute-done((f32[32,16,128]{2,1,0:T(8,128)S(1)}, f32[32,16,128]{2,1,0:T(8,128)S(1)}, u32[]{:S(2)}, u32[]{:S(2)}) %collective-permute-start.23) | collective-permute-done | bytes 262176 | tf_op jit(solution)/shard_map/ppermute | solution.py:361
  245.4 2.8 %shard_map.59 = f32[4096,128]{1,0:T(8,128)} custom-call(s32[4]{0:T(128)S(1)} %and_select_fusion.3.place, f32[4096,128]{1,0:T(8,128)S(1)} %bitcast.58, f32[8,2,32,128]{3,2,1,0:T(8,128)S(1)} %shard_map.54.refs_0_, f32[8,2,32,128]{3,2,1,0:T(8,128)S(1)} %collective-permute-done.14.refs_1_, f32[8,2,32,128]{3,2,1,0:T(8,128)S(1)} %collective-permute-done.15.refs_2_, ...), custom_call_target="tpu_custom_call" | custom-call | bytes 6291456 | tf_op jit(solution)/shard_map/pallas_call | solution.py:38
  (137 shorter events, 48.7 us)
Async XLA Ops:
  4.0 25.1 %collective-permute-start.2 = (s32[2,32]{1,0:T(2,128)S(1)}, s32[2,32]{1,0:T(2,128)S(1)}, u32[]{:S(2)}, u32[]{:S(2)}) collective-permute-start(s32[2,32]{1,0:T(2,128)S(1)} %select_reduce_fusion.2.table.refs_0_), channel_id=1, source_target_pairs={{0,96},{32,0},{64,32},{96,64},{1,97},{33,1},{65,33},{97,65},{2,98}... | collective-permute-start | bytes 776 | tf_op jit(solution)/shard_map/ppermute | solution.py:361
  8.7 20.4 %collective-permute-start.1 = (s32[2,32]{1,0:T(2,128)S(1)}, s32[2,32]{1,0:T(2,128)S(1)}, u32[]{:S(2)}, u32[]{:S(2)}) collective-permute-start(s32[2,32]{1,0:T(2,128)S(1)} %select_reduce_fusion.2.table.refs_0_), channel_id=1, source_target_pairs={{0,64},{32,96},{64,0},{96,32},{1,65},{33,97},{65,1},{97,33},{2,66}... | collective-permute-start | bytes 776 | tf_op jit(solution)/shard_map/ppermute | solution.py:361
  8.7 20.4 %collective-permute-start = (s32[2,32]{1,0:T(2,128)S(1)}, s32[2,32]{1,0:T(2,128)S(1)}, u32[]{:S(2)}, u32[]{:S(2)}) collective-permute-start(s32[2,32]{1,0:T(2,128)S(1)} %select_reduce_fusion.2.table.refs_0_), channel_id=1, source_target_pairs={{0,32},{32,64},{64,96},{96,0},{1,33},{33,65},{65,97},{97,1},{2,34}... | collective-permute-start | bytes 776 | tf_op jit(solution)/shard_map/ppermute | solution.py:361
  13.7 59.4 %all-to-all-start = ((f32[32,2,4,32,128]{4,3,2,1,0:T(8,128)}), f32[32,2,4,32,128]{4,3,2,1,0:T(8,128)}, u32[]{:S(2)}, u32[]{:S(2)}) async-start(f32[32,2,4,32,128]{4,3,2,1,0:T(8,128)} %get-tuple-element.51), calls=%async_computation | async-start | bytes 8388608 | tf_op jit(solution)/shard_map/all_to_all | solution.py:365
  26.3 46.7 %copy-start.16 = (f32[1,4,32,128]{3,2,1,0:T(8,128)S(1)}, f32[1,4,32,128]{3,2,1,0:T(8,128)}, u32[]{:S(2)}) copy-start(f32[1,4,32,128]{3,2,1,0:T(8,128)} %get-tuple-element.53.kept) | copy-start | bytes 196612
  75.1 18.9 %collective-permute-start.5 = (f32[128,16,128]{2,1,0:T(8,128)S(1)}, f32[128,16,128]{2,1,0:T(8,128)}, u32[]{:S(2)}, u32[]{:S(2)}) collective-permute-start(f32[128,16,128]{2,1,0:T(8,128)S(1)} %get-tuple-element.59.high), channel_id=1, source_target_pairs={{0,1},{1,2},{2,3},{3,4},{4,5},{5,6},{6,7},{7,8},{8,9},{9,10},{10,1... | collective-permute-start | bytes 3145736 | tf_op jit(solution)/shard_map/ppermute | solution.py:361
  79.4 16.2 %collective-permute-start.6 = (f32[128,16,128]{2,1,0:T(8,128)S(1)}, f32[128,16,128]{2,1,0:T(8,128)}, u32[]{:S(2)}, u32[]{:S(2)}) collective-permute-start(f32[128,16,128]{2,1,0:T(8,128)S(1)} %get-tuple-element.54.low), channel_id=1, source_target_pairs={{1,0},{2,1},{3,2},{4,3},{5,4},{6,5},{7,6},{8,7},{9,8},{10,9},{11,1... | collective-permute-start | bytes 3145736 | tf_op jit(solution)/shard_map/ppermute | solution.py:361
  86.1 25.4 %collective-permute-start.3 = (f32[128,16,128]{2,1,0:T(8,128)}, f32[128,16,128]{2,1,0:T(8,128)}, u32[]{:S(2)}, u32[]{:S(2)}) collective-permute-start(f32[128,16,128]{2,1,0:T(8,128)} %get-tuple-element.69.high), channel_id=1, source_target_pairs={{0,1},{1,2},{2,3},{3,4},{4,5},{5,6},{6,7},{7,8},{8,9},{9,10},{10,1... | collective-permute-start | bytes 3145736 | tf_op jit(solution)/shard_map/ppermute | solution.py:361
  88.2 23.4 %collective-permute-start.4 = (f32[128,16,128]{2,1,0:T(8,128)S(1)}, f32[128,16,128]{2,1,0:T(8,128)}, u32[]{:S(2)}, u32[]{:S(2)}) collective-permute-start(f32[128,16,128]{2,1,0:T(8,128)S(1)} %get-tuple-element.68.low), channel_id=1, source_target_pairs={{1,0},{2,1},{3,2},{4,3},{5,4},{6,5},{7,6},{8,7},{9,8},{10,9},{11,1... | collective-permute-start | bytes 3145736 | tf_op jit(solution)/shard_map/ppermute | solution.py:361
  106.9 19.5 %copy-start.1 = (f32[2048,128]{1,0:T(8,128)}, f32[2048,128]{1,0:T(8,128)S(1)}, u32[]{:S(2)}) copy-start(f32[2048,128]{1,0:T(8,128)S(1)} %get-tuple-element.66) | copy-start | bytes 3145732
  106.9 19.4 %collective-permute-start.9 = (f32[128,16,128]{2,1,0:T(8,128)S(1)}, f32[128,16,128]{2,1,0:T(8,128)S(1)}, u32[]{:S(2)}, u32[]{:S(2)}) collective-permute-start(f32[128,16,128]{2,1,0:T(8,128)S(1)} %bitcast.62), channel_id=1, source_target_pairs={{0,1},{1,2},{2,3},{3,4},{4,5},{5,6},{6,7},{7,8},{8,9},{9,10},{10,1... | collective-permute-start | bytes 3145736 | tf_op jit(solution)/shard_map/ppermute | solution.py:361
  108.9 17.5 %collective-permute-start.10 = (f32[128,16,128]{2,1,0:T(8,128)S(1)}, f32[128,16,128]{2,1,0:T(8,128)S(1)}, u32[]{:S(2)}, u32[]{:S(2)}) collective-permute-start(f32[128,16,128]{2,1,0:T(8,128)S(1)} %bitcast.59), channel_id=1, source_target_pairs={{1,0},{2,1},{3,2},{4,3},{5,4},{6,5},{7,6},{8,7},{9,8},{10,9},{11,1... | collective-permute-start | bytes 3145736 | tf_op jit(solution)/shard_map/ppermute | solution.py:361
  120.7 16.1 %collective-permute-start.8 = (f32[128,16,128]{2,1,0:T(8,128)S(1)}, f32[128,16,128]{2,1,0:T(8,128)S(1)}, u32[]{:S(2)}, u32[]{:S(2)}) collective-permute-start(f32[128,16,128]{2,1,0:T(8,128)S(1)} %bitcast.69), channel_id=1, source_target_pairs={{1,0},{2,1},{3,2},{4,3},{5,4},{6,5},{7,6},{8,7},{9,8},{10,9},{11,1... | collective-permute-start | bytes 3145736 | tf_op jit(solution)/shard_map/ppermute | solution.py:361
  122.6 15.4 %collective-permute-start.7 = (f32[128,16,128]{2,1,0:T(8,128)S(1)}, f32[128,16,128]{2,1,0:T(8,128)S(1)}, u32[]{:S(2)}, u32[]{:S(2)}) collective-permute-start(f32[128,16,128]{2,1,0:T(8,128)S(1)} %bitcast.72), channel_id=1, source_target_pairs={{0,1},{1,2},{2,3},{3,4},{4,5},{5,6},{6,7},{7,8},{8,9},{9,10},{10,1... | collective-permute-start | bytes 3145736 | tf_op jit(solution)/shard_map/ppermute | solution.py:361
  140.5 47.7 %all-to-all-start.1 = ((f32[32,2,2,32,128]{4,3,2,1,0:T(8,128)}), f32[32,2,2,32,128]{4,3,2,1,0:T(8,128)S(1)}, u32[]{:S(2)}, u32[]{:S(2)}) async-start(f32[32,2,2,32,128]{4,3,2,1,0:T(8,128)} %get-tuple-element.75), calls=%async_computation.1 | async-start | bytes 4194304 | tf_op jit(solution)/shard_map/all_to_all | solution.py:365
  160.0 9.1 %collective-permute-start.18 = (f32[33,16,128]{2,1,0:T(8,128)S(1)}, f32[33,16,128]{2,1,0:T(8,128)S(1)}, u32[]{:S(2)}, u32[]{:S(2)}) collective-permute-start(f32[33,16,128]{2,1,0:T(8,128)S(1)} %get-tuple-element.89), channel_id=1, source_target_pairs={{0,32},{32,64},{64,96},{96,0},{1,33},{33,65},{65,97},{97,1},{2,34}... | collective-permute-start | bytes 811016 | tf_op jit(solution)/shard_map/ppermute | solution.py:361
  162.0 13.1 %collective-permute-start.20 = (f32[33,16,128]{2,1,0:T(8,128)S(1)}, f32[33,16,128]{2,1,0:T(8,128)S(1)}, u32[]{:S(2)}, u32[]{:S(2)}) collective-permute-start(f32[33,16,128]{2,1,0:T(8,128)S(1)} %get-tuple-element.91), channel_id=1, source_target_pairs={{0,64},{32,96},{64,0},{96,32},{1,65},{33,97},{65,1},{97,33},{2,66}... | collective-permute-start | bytes 811016 | tf_op jit(solution)/shard_map/ppermute | solution.py:361
  162.9 12.4 %collective-permute-start.22 = (f32[33,16,128]{2,1,0:T(8,128)S(1)}, f32[33,16,128]{2,1,0:T(8,128)S(1)}, u32[]{:S(2)}, u32[]{:S(2)}) collective-permute-start(f32[33,16,128]{2,1,0:T(8,128)S(1)} %get-tuple-element.93), channel_id=1, source_target_pairs={{0,96},{32,0},{64,32},{96,64},{1,97},{33,1},{65,33},{97,65},{2,98}... | collective-permute-start | bytes 811016 | tf_op jit(solution)/shard_map/ppermute | solution.py:361
  166.2 15.0 %collective-permute-start.17 = (f32[33,16,128]{2,1,0:T(8,128)S(1)}, f32[33,16,128]{2,1,0:T(8,128)S(1)}, u32[]{:S(2)}, u32[]{:S(2)}) collective-permute-start(f32[33,16,128]{2,1,0:T(8,128)S(1)} %get-tuple-element.88), channel_id=1, source_target_pairs={{0,32},{32,64},{64,96},{96,0},{1,33},{33,65},{65,97},{97,1},{2,34}... | collective-permute-start | bytes 811016 | tf_op jit(solution)/shard_map/ppermute | solution.py:361
  166.3 20.4 %collective-permute-start.19 = (f32[33,16,128]{2,1,0:T(8,128)S(1)}, f32[33,16,128]{2,1,0:T(8,128)S(1)}, u32[]{:S(2)}, u32[]{:S(2)}) collective-permute-start(f32[33,16,128]{2,1,0:T(8,128)S(1)} %get-tuple-element.90), channel_id=1, source_target_pairs={{0,64},{32,96},{64,0},{96,32},{1,65},{33,97},{65,1},{97,33},{2,66}... | collective-permute-start | bytes 811016 | tf_op jit(solution)/shard_map/ppermute | solution.py:361
  169.1 17.8 %collective-permute-start.21 = (f32[33,16,128]{2,1,0:T(8,128)S(1)}, f32[33,16,128]{2,1,0:T(8,128)S(1)}, u32[]{:S(2)}, u32[]{:S(2)}) collective-permute-start(f32[33,16,128]{2,1,0:T(8,128)S(1)} %get-tuple-element.92), channel_id=1, source_target_pairs={{0,96},{32,0},{64,32},{96,64},{1,97},{33,1},{65,33},{97,65},{2,98}... | collective-permute-start | bytes 811016 | tf_op jit(solution)/shard_map/ppermute | solution.py:361
  188.3 37.2 %all-to-all-start.2 = ((f32[32,4,2,16,128]{4,3,2,1,0:T(8,128)}), f32[32,4,2,16,128]{4,3,2,1,0:T(8,128)}, u32[]{:S(2)}, u32[]{:S(2)}) async-start(f32[32,4,2,16,128]{4,3,2,1,0:T(8,128)} %get-tuple-element.95), calls=%async_computation.2 | async-start | bytes 4194304 | tf_op jit(solution)/shard_map/all_to_all | solution.py:365
  197.6 47.8 %copy-start = (f32[32,128,128]{2,1,0:T(8,128)S(1)}, f32[32,128,128]{2,1,0:T(8,128)}, u32[]{:S(2)}) copy-start(f32[32,128,128]{2,1,0:T(8,128)} %param.4) | copy-start | bytes 6291460
  197.6 8.9 %collective-permute-start.11 = (f32[8,2,32,128]{3,2,1,0:T(8,128)S(1)}, f32[8,2,32,128]{3,2,1,0:T(8,128)S(1)}, u32[]{:S(2)}, u32[]{:S(2)}) collective-permute-start(f32[8,2,32,128]{3,2,1,0:T(8,128)S(1)} %get-tuple-element.79), channel_id=1, source_target_pairs={{0,32},{32,64},{64,96},{96,0},{1,33},{33,65},{65,97},{97,1},{2,34}... | collective-permute-start | bytes 786440 | tf_op jit(solution)/shard_map/ppermute | solution.py:361
  199.1 13.9 %collective-permute-start.12 = (f32[8,2,32,128]{3,2,1,0:T(8,128)S(1)}, f32[8,2,32,128]{3,2,1,0:T(8,128)S(1)}, u32[]{:S(2)}, u32[]{:S(2)}) collective-permute-start(f32[8,2,32,128]{3,2,1,0:T(8,128)S(1)} %get-tuple-element.80), channel_id=1, source_target_pairs={{0,64},{32,96},{64,0},{96,32},{1,65},{33,97},{65,1},{97,33},{2,66}... | collective-permute-start | bytes 786440 | tf_op jit(solution)/shard_map/ppermute | solution.py:361
  201.2 11.8 %collective-permute-start.13 = (f32[8,2,32,128]{3,2,1,0:T(8,128)S(1)}, f32[8,2,32,128]{3,2,1,0:T(8,128)S(1)}, u32[]{:S(2)}, u32[]{:S(2)}) collective-permute-start(f32[8,2,32,128]{3,2,1,0:T(8,128)S(1)} %get-tuple-element.81), channel_id=1, source_target_pairs={{0,96},{32,0},{64,32},{96,64},{1,97},{33,1},{65,33},{97,65},{2,98}... | collective-permute-start | bytes 786440 | tf_op jit(solution)/shard_map/ppermute | solution.py:361
  213.1 17.9 %collective-permute-start.16 = (f32[8,2,32,128]{3,2,1,0:T(8,128)S(1)}, f32[8,2,32,128]{3,2,1,0:T(8,128)S(1)}, u32[]{:S(2)}, u32[]{:S(2)}) collective-permute-start(f32[8,2,32,128]{3,2,1,0:T(8,128)S(1)} %shard_map.54.refs_0_), channel_id=1, source_target_pairs={{0,96},{32,0},{64,32},{96,64},{1,97},{33,1},{65,33},{97,65},{2,98}... | collective-permute-start | bytes 786440 | tf_op jit(solution)/shard_map/ppermute | solution.py:361
  216.0 15.1 %collective-permute-start.15 = (f32[8,2,32,128]{3,2,1,0:T(8,128)S(1)}, f32[8,2,32,128]{3,2,1,0:T(8,128)S(1)}, u32[]{:S(2)}, u32[]{:S(2)}) collective-permute-start(f32[8,2,32,128]{3,2,1,0:T(8,128)S(1)} %shard_map.54.refs_0_), channel_id=1, source_target_pairs={{0,64},{32,96},{64,0},{96,32},{1,65},{33,97},{65,1},{97,33},{2,66}... | collective-permute-start | bytes 786440 | tf_op jit(solution)/shard_map/ppermute | solution.py:361
  216.5 14.8 %collective-permute-start.14 = (f32[8,2,32,128]{3,2,1,0:T(8,128)S(1)}, f32[8,2,32,128]{3,2,1,0:T(8,128)S(1)}, u32[]{:S(2)}, u32[]{:S(2)}) collective-permute-start(f32[8,2,32,128]{3,2,1,0:T(8,128)S(1)} %shard_map.54.refs_0_), channel_id=1, source_target_pairs={{0,32},{32,64},{64,96},{96,0},{1,33},{33,65},{65,97},{97,1},{2,34}... | collective-permute-start | bytes 786440 | tf_op jit(solution)/shard_map/ppermute | solution.py:361
  227.7 7.0 %collective-permute-start.25 = (f32[32,16,128]{2,1,0:T(8,128)S(1)}, f32[32,16,128]{2,1,0:T(8,128)S(1)}, u32[]{:S(2)}, u32[]{:S(2)}) collective-permute-start(f32[32,16,128]{2,1,0:T(8,128)S(1)} %shard_map.58.refs_4_), channel_id=1, source_target_pairs={{0,96},{32,0},{64,32},{96,64},{1,97},{33,1},{65,33},{97,65},{2,98}... | collective-permute-start | bytes 786440 | tf_op jit(solution)/shard_map/ppermute | solution.py:361
  230.1 7.5 %collective-permute-start.24 = (f32[32,16,128]{2,1,0:T(8,128)S(1)}, f32[32,16,128]{2,1,0:T(8,128)S(1)}, u32[]{:S(2)}, u32[]{:S(2)}) collective-permute-start(f32[32,16,128]{2,1,0:T(8,128)S(1)} %shard_map.58.refs_4_), channel_id=1, source_target_pairs={{0,64},{32,96},{64,0},{96,32},{1,65},{33,97},{65,1},{97,33},{2,66}... | collective-permute-start | bytes 786440 | tf_op jit(solution)/shard_map/ppermute | solution.py:361
  230.9 14.5 %collective-permute-start.23 = (f32[32,16,128]{2,1,0:T(8,128)S(1)}, f32[32,16,128]{2,1,0:T(8,128)S(1)}, u32[]{:S(2)}, u32[]{:S(2)}) collective-permute-start(f32[32,16,128]{2,1,0:T(8,128)S(1)} %shard_map.58.refs_4_), channel_id=1, source_target_pairs={{0,32},{32,64},{64,96},{96,0},{1,33},{33,65},{65,97},{97,1},{2,34}... | collective-permute-start | bytes 786440 | tf_op jit(solution)/shard_map/ppermute | solution.py:361
  (19 other events, 113.1 us)

commit v4 on v3

--- a/solution.py
+++ b/solution.py
@@ -19,9 +19,11 @@
 NPAD = ZD + 2 * PAD
 PLANES = 4
 STEPS = 4
+WIDE = 4
 ROWS = ZD // STEPS
 PITCH = NY + 8
 WORK = ZD + 8
+SLOT = PAD + 8
 
 F32 = jnp.float32
 BF16 = jnp.bfloat16
@@ -135,18 +137,16 @@
     return jnp.concatenate(columns, axis=1)
 
 
-def blur_kernel(v, top, low, high, bottom, rec, zmat, xmat, ymat, ymat_t, xmat_t, out_low, out_high, work, seen_rows, sem):
+def blur_kernel(v, top, low, high, bottom, rec, zmat, xmat, ymat, ymat_t, xmat_t, out_low, out_high, work, seen_rows, sem, done, out_sems):
     zmat, xmat, ymat, ymat_t, xmat_t = (r.at[0] for r in (zmat, xmat, ymat, ymat_t, xmat_t))
     parts = (top, low, high, bottom)
     fetch = pltpu.make_async_copy(rec.at[v], seen_rows, sem)
     fetch.start()
 
     def forward(group, carry):
-        rows = []
-        for pair in range(2):
-            y = group * 4 + pair * 2
-            blurred = left_dot(zmat[...], padded_pair(parts, y, y + 1))
-            rows += [blurred[:, :NX], blurred[:, NX:]]
+        y = group * 4
+        blurred = left_dot(zmat[...], padded_pair(parts, y, y + 1, y + 2, y + 3))
+        rows = [blurred[:, i * NX : (i + 1) * NX] for i in range(4)]
         done = right_dot(jnp.concatenate(rows, axis=0), xmat[...])
         for i in range(4):
             at = pl.multiple_of((group * 4 + i) * WORK, 8)
@@ -156,23 +156,30 @@
     lax.fori_loop(0, NY // 4, forward, 0, unroll=8)
     fetch.wait()
 
-    for base, out in ((0, out_low), (PAD, out_high)):
-
-        def backward(step, carry, base=base, out=out):
-            zz = step * 2
-            z = base + zz
-            x = jnp.concatenate([work[pl.ds(z + i, NY, stride=WORK), :] for i in range(2)], axis=1)
+    stores = []
+    for n, out in enumerate((out_low, out_high)):
+
+        def backward(step, carry, n=n):
+            zz = step * WIDE
+            z = n * PAD + zz
+            x = jnp.concatenate([work[pl.ds(z + i, NY, stride=WORK), :] for i in range(WIDE)], axis=1)
             seen = jnp.concatenate(
-                [seen_rows[pl.ds(pl.multiple_of((z + i) * NY, NY), NY), :] for i in range(2)], axis=1
+                [seen_rows[pl.ds(pl.multiple_of((z + i) * NY, NY), NY), :] for i in range(WIDE)], axis=1
             )
             ratio = seen / left_dot(ymat[...], x)
             back = left_dot(ymat_t[...], ratio)
-            back = right_dot(jnp.concatenate([back[:, :NX], back[:, NX:]], axis=0), xmat_t[...])
-            for i in range(2):
-                out[pl.ds(zz + i, NY, stride=PAD), :] = back[i * NY : (i + 1) * NY]
+            back = jnp.concatenate([back[:, i * NX : (i + 1) * NX] for i in range(WIDE)], axis=0)
+            back = right_dot(back, xmat_t[...])
+            for i in range(WIDE):
+                done[n, pl.ds(zz + i, NY, stride=SLOT), :] = back[i * NY : (i + 1) * NY]
             return carry
 
-        lax.fori_loop(0, PAD // 2, backward, 0, unroll=8)
+        lax.fori_loop(0, PAD // WIDE, backward, 0, unroll=PAD // WIDE)
+        rows = done.at[n].reshape(NY, SLOT, NX).at[:, pl.ds(0, PAD), :]
+        stores.append(pltpu.make_async_copy(rows, out, out_sems.at[n]))
+        stores[-1].start()
+    for store in stores:
+        store.wait()
 
 
 def adjoint_first_kernel(v, table, top, low, high, bottom, zmat, *refs):
@@ -288,14 +295,25 @@
         out[rows, :] = est[rows, :] * turned[pl.ds(z * PITCH, NY), :]
 
 
-def stacked(matrix, axis):
+def bands_kernel(plain, xmat, ymat, ymat_t, xmat_t):
+    for v in range(plain.shape[0]):
+        for matrix, left, right in ((plain[v, 0], ymat_t, None), (plain[v, 1], None, xmat)):
+            for _ in range(2):
+                high, low = halves(matrix)
+                if left is not None:
+                    left[v] = jnp.concatenate([jnp.concatenate([p, p], axis=1) for p in (high, low)], axis=0)
+                    left = ymat
+                else:
+                    right[v] = jnp.concatenate([jnp.concatenate([high, low], axis=1)] * 2, axis=0)
+                    right = xmat_t
+                matrix = matrix.T
+
+
+def stacked(matrix):
     high = lax.reduce_precision(matrix, 8, 7)
     low = matrix - high
-    if axis == 0:
-        both = jnp.concatenate([high, low], axis=-2)
-        return jnp.concatenate([both, both], axis=-1).astype(BF16)
-    both = jnp.concatenate([high, low], axis=-1)
-    return jnp.concatenate([both, both], axis=-2).astype(BF16)
+    both = jnp.concatenate([high, low], axis=-2)
+    return jnp.concatenate([both, both], axis=-1).astype(BF16)
 
 
 def band(weights, positions):
@@ -309,9 +327,15 @@
     plain = band(weights[:, 1:].reshape(-1, TAPS), i[:, None] - i[None, :] + HALF)
     plain = plain / jnp.sum(plain, axis=1, keepdims=True)
     plain = plain.reshape(-1, 2, NX, NX)
-    turned = plain.transpose(0, 1, 3, 2)
-    ymat, xmat = turned[:, 0], plain[:, 1]
-    ymat_t, xmat_t = plain[:, 0], turned[:, 1]
+    shape = (plain.shape[0], 2 * NX, 2 * NX)
+    xmat, ymat, ymat_t, xmat_t = pl.pallas_call(
+        bands_kernel,
+        out_shape=[jax.ShapeDtypeStruct(shape, BF16)] * 4,
+        in_specs=[VMEM],
+        out_specs=[VMEM] * 4,
+        name="bands",
+        compiler_params=pltpu.CompilerParams(vmem_limit_bytes=8 << 20),
+    )(plain)
 
     wz = weights[:, 0]
     rows = own * ZD + jnp.arange(NPAD, dtype=jnp.int32) - PAD
@@ -324,12 +348,12 @@
     zmat = band(wz, k - o - 1) / divisor[:, PAD : PAD + ZD, None]
     zmat_t = band(wz, o - k + 2 * PAD - 1) / divisor[:, None, :]
     return (
-        stacked(zmat, 0),
-        stacked(xmat, 1),
-        stacked(ymat, 0),
-        stacked(ymat_t, 0),
-        stacked(xmat_t, 1),
-        stacked(zmat_t, 0),
+        stacked(zmat),
+        xmat,
+        ymat,
+        ymat_t,
+        xmat_t,
+        stacked(zmat_t),
     )
 
 
@@ -397,7 +421,8 @@
         low, high = call(
             functools.partial(blur_kernel, v),
             (*parts, far_rec, *mats[:5]),
-            ((NY * PAD, NX), (NY * PAD, NX)),
+            (strip, strip),
+            out_specs=[ANY, ANY],
             ins={4: ANY}
             | {5 + n: pl.BlockSpec((1, *m.shape[1:]), lambda s: (v, 0, 0)) for n, m in enumerate(mats[:5])},
             grid=(1,),
@@ -405,11 +430,13 @@
                 pltpu.VMEM((NY * WORK, NX), F32),
                 pltpu.VMEM((ZD * NY, NX), F32),
                 pltpu.SemaphoreType.DMA,
+                pltpu.VMEM((2, NY * SLOT, NX), F32),
+                pltpu.SemaphoreType.DMA((2,)),
             ],
             flops=5 << 30,
             moved=4 * big,
         )
-        return low.reshape(strip), high.reshape(strip)
+        return low, high
 
     far_rec = pltpu.with_memory_space_constraint(rec, pltpu.HBM)
     views = rec.shape[0]

time: 250 us -> 244 us (0.976)
  waiting for transfers between devices: 107 us -> 113 us
  Pallas kernels: 43.5 us -> 38.5 us
    ppermute x26, waiting for transfers between devices: 54.1 us -> 60.9 us  [shifted(): return lax.ppermute(value, axis, pairs)]
    pallas_call x14, Pallas kernels: 43.5 us -> 38.4 us  [call(): pl.pallas_call(kernel, out_shape=[(pltpu.HBM if n in far else jax.ShapeDt...]
    optimization_barrier x2 -> x0, local copies, waits for them, and re-layouts: 2.65 us -> none  [local(): recv, *rest = lax.optimization_barrier((recv, *mats, *places))]
  transfers between devices with their start and end apart: 29 -> 29, of which waited for: 17 -> 19; matrix products, arithmetic and copies ran while one was open for 4% -> 2% of each run, Pallas kernels for 15% -> 13%
where the time goes in v4:
time: 244 us; the launch traced here: 243 us
  waiting for transfers between devices  113 us (46%)
  starting transfers between devices  74.9 us (31%)
  Pallas kernels  38.5 us (16%)
  other arithmetic  8.37 us (3%)
  local copies, waits for them, and re-layouts  7.96 us (3%)
    ppermute x26, waiting for transfers between devices, shifted(): return lax.ppermute(value, axis, pairs)  60.9 us
    all_to_all x3, waiting for transfers between devices, exchange(): return lax.all_to_all(value, axis, 0, 0, tiled=True)  52 us
    ppermute x26, starting transfers between devices, shifted(): return lax.ppermute(value, axis, pairs)  45.6 us
    pallas_call x14, Pallas kernels, call(): pl.pallas_call(kernel, out_shape=[(pltpu.HBM if n in far else jax.ShapeDt...  38.4 us
    all_to_all x3, starting transfers between devices, exchange(): return lax.all_to_all(value, axis, 0, 0, tiled=True)  29.3 us
    unnamed x44, local copies, waits for them, and re-layouts  7.77 us
  transfers between devices with their start and end apart: 29, of which 19 were waited for; matrix products, arithmetic and copies ran while one was open for 2% of the time, Pallas kernels for 13%

profile of v4, /device:TPU:1, one launch (start us, length us, event | category | flops | bytes accessed | tf_op | source)
XLA Modules:
  0.0 243.0 jit_solution(1797223578294204311)
XLA Ops:
  4.0 4.6 %collective-permute-start.2 = (s32[2,32]{1,0:T(2,128)S(1)}, s32[2,32]{1,0:T(2,128)S(1)}, u32[]{:S(2)}, u32[]{:S(2)}) collective-permute-start(s32[2,32]{1,0:T(2,128)S(1)} %select_reduce_fusion.2.table.refs_0_), channel_id=1, source_target_pairs={{0,96},{32,0},{64,32},{96,64},{1,97},{33,1},{65,33},{97,65},{2,98}... | collective-permute-start | bytes 776 | tf_op jit(solution)/shard_map/ppermute | solution.py:385
  9.4 4.3 %shard_map.46 = (f32[32,2,4,32,128]{4,3,2,1,0:T(8,128)}, f32[1,4,32,128]{3,2,1,0:T(8,128)}, f32[1,4,32,128]{3,2,1,0:T(8,128)}) custom-call(s32[2,32]{1,0:T(2,128)S(1)} %and_select_fusion.1.table, s32[2]{0:T(128)S(1)} %get-tuple-element.119.last, f32[4096,128]{1,0:T(8,128)} %bitcast.19), custom_call_target="tpu_custom_call" | custom-call | bytes 4194304 | tf_op jit(solution)/shard_map/pallas_call | solution.py:40
  13.7 8.7 %all-to-all-start = ((f32[32,2,4,32,128]{4,3,2,1,0:T(8,128)}), f32[32,2,4,32,128]{4,3,2,1,0:T(8,128)}, u32[]{:S(2)}, u32[]{:S(2)}) async-start(f32[32,2,4,32,128]{4,3,2,1,0:T(8,128)} %get-tuple-element.55), calls=%async_computation | async-start | bytes 8388608 | tf_op jit(solution)/shard_map/all_to_all | solution.py:389
  29.9 43.2 %all-to-all-done.recv = f32[32,2,4,32,128]{4,3,2,1,0:T(8,128)} async-done(((f32[32,2,4,32,128]{4,3,2,1,0:T(8,128)}), f32[32,2,4,32,128]{4,3,2,1,0:T(8,128)}, u32[]{:S(2)}, u32[]{:S(2)}) %all-to-all-start) | async-done | bytes 4194336 | tf_op jit(solution)/shard_map/all_to_all | solution.py:389
  75.2 4.3 %collective-permute-start.5 = (f32[128,16,128]{2,1,0:T(8,128)S(1)}, f32[128,16,128]{2,1,0:T(8,128)S(1)}, u32[]{:S(2)}, u32[]{:S(2)}) collective-permute-start(f32[128,16,128]{2,1,0:T(8,128)S(1)} %get-tuple-element.67.high), channel_id=1, source_target_pairs={{0,1},{1,2},{2,3},{3,4},{4,5},{5,6},{6,7},{7,8},{8,9},{9,10},{10,1... | collective-permute-start | bytes 3145736 | tf_op jit(solution)/shard_map/ppermute | solution.py:385
  79.5 2.6 %collective-permute-start.6 = (f32[128,16,128]{2,1,0:T(8,128)S(1)}, f32[128,16,128]{2,1,0:T(8,128)S(1)}, u32[]{:S(2)}, u32[]{:S(2)}) collective-permute-start(f32[128,16,128]{2,1,0:T(8,128)S(1)} %get-tuple-element.62.low), channel_id=1, source_target_pairs={{1,0},{2,1},{3,2},{4,3},{5,4},{6,5},{7,6},{8,7},{9,8},{10,9},{11,1... | collective-permute-start | bytes 3145736 | tf_op jit(solution)/shard_map/ppermute | solution.py:385
  82.1 2.1 shard_map.48
  84.2 3.0 %collective-permute-start.3 = (f32[128,16,128]{2,1,0:T(8,128)S(1)}, f32[128,16,128]{2,1,0:T(8,128)S(1)}, u32[]{:S(2)}, u32[]{:S(2)}) collective-permute-start(f32[128,16,128]{2,1,0:T(8,128)S(1)} %get-tuple-element.77.high), channel_id=1, source_target_pairs={{0,1},{1,2},{2,3},{3,4},{4,5},{5,6},{6,7},{7,8},{8,9},{9,10},{10,1... | collective-permute-start | bytes 3145736 | tf_op jit(solution)/shard_map/ppermute | solution.py:385
  91.2 4.4 %collective-permute-done.6.bottom = f32[128,16,128]{2,1,0:T(8,128)S(1)} collective-permute-done((f32[128,16,128]{2,1,0:T(8,128)S(1)}, f32[128,16,128]{2,1,0:T(8,128)S(1)}, u32[]{:S(2)}, u32[]{:S(2)}) %collective-permute-start.6) | collective-permute-done | bytes 1048608 | tf_op jit(solution)/shard_map/ppermute | solution.py:385
  95.6 6.9 %shard_map.49 = (f32[128,16,128]{2,1,0:T(8,128)S(1)}, f32[128,16,128]{2,1,0:T(8,128)S(1)}) custom-call(f32[128,16,128]{2,1,0:T(8,128)S(1)} %collective-permute-done.5.top, f32[128,16,128]{2,1,0:T(8,128)S(1)} %get-tuple-element.62.low, f32[128,16,128]{2,1,0:T(8,128)S(1)} %get-tuple-element.67.high, f32[128,16,128]{2,1,0:T(8,128)S(1)} %collective-permute-done.6.bottom, ...), custom_call_target="tpu_custom_call" | custom-call | flops 5368709120 | bytes 8388608 | tf_op jit(solution)/shard_map/pallas_call | solution.py:40
  104.4 3.8 %collective-permute-start.9 = (f32[128,16,128]{2,1,0:T(8,128)S(1)}, f32[128,16,128]{2,1,0:T(8,128)S(1)}, u32[]{:S(2)}, u32[]{:S(2)}) collective-permute-start(f32[128,16,128]{2,1,0:T(8,128)S(1)} %get-tuple-element.74), channel_id=1, source_target_pairs={{0,1},{1,2},{2,3},{3,4},{4,5},{5,6},{6,7},{7,8},{8,9},{9,10},{10,1... | collective-permute-start | bytes 3145736 | tf_op jit(solution)/shard_map/ppermute | solution.py:385
  108.3 6.9 %shard_map.50 = (f32[128,16,128]{2,1,0:T(8,128)S(1)}, f32[128,16,128]{2,1,0:T(8,128)S(1)}) custom-call(f32[128,16,128]{2,1,0:T(8,128)S(1)} %collective-permute-done.3.top, f32[128,16,128]{2,1,0:T(8,128)S(1)} %get-tuple-element.76.low, f32[128,16,128]{2,1,0:T(8,128)S(1)} %get-tuple-element.77.high, f32[128,16,128]{2,1,0:T(8,128)S(1)} %collective-permute-done.4.bottom, ...), custom_call_target="tpu_custom_call" | custom-call | flops 5368709120 | bytes 8388608 | tf_op jit(solution)/shard_map/pallas_call | solution.py:40
  117.1 2.5 %collective-permute-start.8 = (f32[128,16,128]{2,1,0:T(8,128)S(1)}, f32[128,16,128]{2,1,0:T(8,128)S(1)}, u32[]{:S(2)}, u32[]{:S(2)}) collective-permute-start(f32[128,16,128]{2,1,0:T(8,128)S(1)} %get-tuple-element.80), channel_id=1, source_target_pairs={{1,0},{2,1},{3,2},{4,3},{5,4},{6,5},{7,6},{8,7},{9,8},{10,9},{11,1... | collective-permute-start | bytes 3145736 | tf_op jit(solution)/shard_map/ppermute | solution.py:385
  119.8 2.5 %shard_map.51 = (f32[32,2,2,32,128]{4,3,2,1,0:T(8,128)}, f32[2,32,128]{2,1,0:T(8,128)S(1)}) custom-call(s32[2,33]{1,0:T(2,128)S(1)} %select_reduce_fusion.6.table, f32[32,4,16,128]{3,2,1,0:T(8,128)S(1)} %bitcast.27, f32[32,4,16,128]{3,2,1,0:T(8,128)S(1)} %bitcast.21, f32[32,4,16,128]{3,2,1,0:T(8,128)S(1)} %bitcast.23, f32[32,4,16,128]{3,2,1,0:T(8,128)S(1)} %bitcast.25, ...), custom_call_target="tpu_custom_call" | custom-call | flops 1073741824 | bytes 4194304 | tf_op jit(solution)/shard_map/pallas_call | solution.py:40
  122.2 8.8 %collective-permute-done.7 = f32[128,16,128]{2,1,0:T(8,128)S(1)} collective-permute-done((f32[128,16,128]{2,1,0:T(8,128)S(1)}, f32[128,16,128]{2,1,0:T(8,128)S(1)}, u32[]{:S(2)}, u32[]{:S(2)}) %collective-permute-start.7) | collective-permute-done | bytes 1048608 | tf_op jit(solution)/shard_map/ppermute | solution.py:385
  131.0 2.2 collective-permute-done.8
  133.2 2.5 %shard_map.52 = (f32[32,2,2,32,128]{4,3,2,1,0:T(8,128)}, f32[2,32,128]{2,1,0:T(8,128)S(1)}) custom-call(s32[2,33]{1,0:T(2,128)S(1)} %select_reduce_fusion.6.table, f32[32,4,16,128]{3,2,1,0:T(8,128)S(1)} %bitcast.33, f32[32,4,16,128]{3,2,1,0:T(8,128)S(1)} %bitcast.29, f32[32,4,16,128]{3,2,1,0:T(8,128)S(1)} %bitcast.31, ...), custom_call_target="tpu_custom_call", output_to_operand_aliasing={{0}: (6, {})} | custom-call | flops 1073741824 | bytes 4194304 | tf_op jit(solution)/shard_map/pallas_call | solution.py:40
  135.7 12.2 %all-to-all-start.1 = ((f32[32,2,2,32,128]{4,3,2,1,0:T(8,128)}), f32[32,2,2,32,128]{4,3,2,1,0:T(8,128)S(1)}, u32[]{:S(2)}, u32[]{:S(2)}) async-start(f32[32,2,2,32,128]{4,3,2,1,0:T(8,128)} %get-tuple-element.83), calls=%async_computation.1 | async-start | bytes 4194304 | tf_op jit(solution)/shard_map/all_to_all | solution.py:389
  164.3 5.6 %collective-permute-done.20.refs_5_ = f32[33,16,128]{2,1,0:T(8,128)S(1)} collective-permute-done((f32[33,16,128]{2,1,0:T(8,128)S(1)}, f32[33,16,128]{2,1,0:T(8,128)S(1)}, u32[]{:S(2)}, u32[]{:S(2)}) %collective-permute-start.20) | collective-permute-done | bytes 270368 | tf_op jit(solution)/shard_map/ppermute | solution.py:385
  170.1 5.8 %collective-permute-done.17.refs_2_ = f32[33,16,128]{2,1,0:T(8,128)S(1)} collective-permute-done((f32[33,16,128]{2,1,0:T(8,128)S(1)}, f32[33,16,128]{2,1,0:T(8,128)S(1)}, u32[]{:S(2)}, u32[]{:S(2)}) %collective-permute-start.17) | collective-permute-done | bytes 270368 | tf_op jit(solution)/shard_map/ppermute | solution.py:385
  176.0 5.5 %collective-permute-done.19.refs_4_ = f32[33,16,128]{2,1,0:T(8,128)S(1)} collective-permute-done((f32[33,16,128]{2,1,0:T(8,128)S(1)}, f32[33,16,128]{2,1,0:T(8,128)S(1)}, u32[]{:S(2)}, u32[]{:S(2)}) %collective-permute-start.19) | collective-permute-done | bytes 270368 | tf_op jit(solution)/shard_map/ppermute | solution.py:385
  183.0 8.4 %all-to-all-start.2 = ((f32[32,4,2,16,128]{4,3,2,1,0:T(8,128)}), f32[32,4,2,16,128]{4,3,2,1,0:T(8,128)}, u32[]{:S(2)}, u32[]{:S(2)}) async-start(f32[32,4,2,16,128]{4,3,2,1,0:T(8,128)} %get-tuple-element.103), calls=%async_computation.2 | async-start | bytes 4194304 | tf_op jit(solution)/shard_map/all_to_all | solution.py:389
  196.9 4.4 %collective-permute-done.11.second = f32[8,2,32,128]{3,2,1,0:T(8,128)S(1)} collective-permute-done((f32[8,2,32,128]{3,2,1,0:T(8,128)S(1)}, f32[8,2,32,128]{3,2,1,0:T(8,128)S(1)}, u32[]{:S(2)}, u32[]{:S(2)}) %collective-permute-start.11) | collective-permute-done | bytes 262176 | tf_op jit(solution)/shard_map/ppermute | solution.py:385
  201.3 6.4 %collective-permute-done.12.third = f32[8,2,32,128]{3,2,1,0:T(8,128)S(1)} collective-permute-done((f32[8,2,32,128]{3,2,1,0:T(8,128)S(1)}, f32[8,2,32,128]{3,2,1,0:T(8,128)S(1)}, u32[]{:S(2)}, u32[]{:S(2)}) %collective-permute-start.12) | collective-permute-done | bytes 262176 | tf_op jit(solution)/shard_map/ppermute | solution.py:385
  207.8 2.9 %collective-permute-start.16 = (f32[8,2,32,128]{3,2,1,0:T(8,128)S(1)}, f32[8,2,32,128]{3,2,1,0:T(8,128)S(1)}, u32[]{:S(2)}, u32[]{:S(2)}) collective-permute-start(f32[8,2,32,128]{3,2,1,0:T(8,128)S(1)} %shard_map.54.refs_0_), channel_id=1, source_target_pairs={{0,96},{32,0},{64,32},{96,64},{1,97},{33,1},{65,33},{97,65},{2,98}... | collective-permute-start | bytes 786440 | tf_op jit(solution)/shard_map/ppermute | solution.py:385
  211.4 8.8 %all-to-all-done.2.refs_4_ = f32[32,4,2,16,128]{4,3,2,1,0:T(8,128)} async-done(((f32[32,4,2,16,128]{4,3,2,1,0:T(8,128)}), f32[32,4,2,16,128]{4,3,2,1,0:T(8,128)}, u32[]{:S(2)}, u32[]{:S(2)}) %all-to-all-start.2) | async-done | bytes 2097184 | tf_op jit(solution)/shard_map/all_to_all | solution.py:389
  220.2 2.3 shard_map.58.refs_4_
  222.5 2.4 collective-permute-start.25
  226.1 3.4 %collective-permute-done.25.refs_7_ = f32[32,16,128]{2,1,0:T(8,128)S(1)} collective-permute-done((f32[32,16,128]{2,1,0:T(8,128)S(1)}, f32[32,16,128]{2,1,0:T(8,128)S(1)}, u32[]{:S(2)}, u32[]{:S(2)}) %collective-permute-start.25) | collective-permute-done | bytes 262176 | tf_op jit(solution)/shard_map/ppermute | solution.py:385
  229.5 2.9 %collective-permute-done.24.refs_6_ = f32[32,16,128]{2,1,0:T(8,128)S(1)} collective-permute-done((f32[32,16,128]{2,1,0:T(8,128)S(1)}, f32[32,16,128]{2,1,0:T(8,128)S(1)}, u32[]{:S(2)}, u32[]{:S(2)}) %collective-permute-start.24) | collective-permute-done | bytes 262176 | tf_op jit(solution)/shard_map/ppermute | solution.py:385
  232.4 7.8 %collective-permute-done.23.refs_5_ = f32[32,16,128]{2,1,0:T(8,128)S(1)} collective-permute-done((f32[32,16,128]{2,1,0:T(8,128)S(1)}, f32[32,16,128]{2,1,0:T(8,128)S(1)}, u32[]{:S(2)}, u32[]{:S(2)}) %collective-permute-start.23) | collective-permute-done | bytes 262176 | tf_op jit(solution)/shard_map/ppermute | solution.py:385
  240.2 2.8 %shard_map.59 = f32[4096,128]{1,0:T(8,128)} custom-call(s32[4]{0:T(128)S(1)} %and_select_fusion.3.place, f32[4096,128]{1,0:T(8,128)S(1)} %bitcast.20, f32[8,2,32,128]{3,2,1,0:T(8,128)S(1)} %shard_map.54.refs_0_, f32[8,2,32,128]{3,2,1,0:T(8,128)S(1)} %collective-permute-done.14.refs_1_, f32[8,2,32,128]{3,2,1,0:T(8,128)S(1)} %collective-permute-done.15.refs_2_, ...), custom_call_target="tpu_custom_call" | custom-call | bytes 6291456 | tf_op jit(solution)/shard_map/pallas_call | solution.py:40
  (125 shorter events, 47.8 us)
Async XLA Ops:
  4.0 25.9 %collective-permute-start.2 = (s32[2,32]{1,0:T(2,128)S(1)}, s32[2,32]{1,0:T(2,128)S(1)}, u32[]{:S(2)}, u32[]{:S(2)}) collective-permute-start(s32[2,32]{1,0:T(2,128)S(1)} %select_reduce_fusion.2.table.refs_0_), channel_id=1, source_target_pairs={{0,96},{32,0},{64,32},{96,64},{1,97},{33,1},{65,33},{97,65},{2,98}... | collective-permute-start | bytes 776 | tf_op jit(solution)/shard_map/ppermute | solution.py:385
  8.7 21.2 %collective-permute-start.1 = (s32[2,32]{1,0:T(2,128)S(1)}, s32[2,32]{1,0:T(2,128)S(1)}, u32[]{:S(2)}, u32[]{:S(2)}) collective-permute-start(s32[2,32]{1,0:T(2,128)S(1)} %select_reduce_fusion.2.table.refs_0_), channel_id=1, source_target_pairs={{0,64},{32,96},{64,0},{96,32},{1,65},{33,97},{65,1},{97,33},{2,66}... | collective-permute-start | bytes 776 | tf_op jit(solution)/shard_map/ppermute | solution.py:385
  8.7 21.2 %collective-permute-start = (s32[2,32]{1,0:T(2,128)S(1)}, s32[2,32]{1,0:T(2,128)S(1)}, u32[]{:S(2)}, u32[]{:S(2)}) collective-permute-start(s32[2,32]{1,0:T(2,128)S(1)} %select_reduce_fusion.2.table.refs_0_), channel_id=1, source_target_pairs={{0,32},{32,64},{64,96},{96,0},{1,33},{33,65},{65,97},{97,1},{2,34}... | collective-permute-start | bytes 776 | tf_op jit(solution)/shard_map/ppermute | solution.py:385
  13.7 59.4 %all-to-all-start = ((f32[32,2,4,32,128]{4,3,2,1,0:T(8,128)}), f32[32,2,4,32,128]{4,3,2,1,0:T(8,128)}, u32[]{:S(2)}, u32[]{:S(2)}) async-start(f32[32,2,4,32,128]{4,3,2,1,0:T(8,128)} %get-tuple-element.55), calls=%async_computation | async-start | bytes 8388608 | tf_op jit(solution)/shard_map/all_to_all | solution.py:389
  22.4 50.7 %copy-start.16 = (f32[1,4,32,128]{3,2,1,0:T(8,128)S(1)}, f32[1,4,32,128]{3,2,1,0:T(8,128)}, u32[]{:S(2)}) copy-start(f32[1,4,32,128]{3,2,1,0:T(8,128)} %get-tuple-element.61.kept) | copy-start | bytes 196612
  75.2 16.0 %collective-permute-start.5 = (f32[128,16,128]{2,1,0:T(8,128)S(1)}, f32[128,16,128]{2,1,0:T(8,128)S(1)}, u32[]{:S(2)}, u32[]{:S(2)}) collective-permute-start(f32[128,16,128]{2,1,0:T(8,128)S(1)} %get-tuple-element.67.high), channel_id=1, source_target_pairs={{0,1},{1,2},{2,3},{3,4},{4,5},{5,6},{6,7},{7,8},{8,9},{9,10},{10,1... | collective-permute-start | bytes 3145736 | tf_op jit(solution)/shard_map/ppermute | solution.py:385
  79.5 16.1 %collective-permute-start.6 = (f32[128,16,128]{2,1,0:T(8,128)S(1)}, f32[128,16,128]{2,1,0:T(8,128)S(1)}, u32[]{:S(2)}, u32[]{:S(2)}) collective-permute-start(f32[128,16,128]{2,1,0:T(8,128)S(1)} %get-tuple-element.62.low), channel_id=1, source_target_pairs={{1,0},{2,1},{3,2},{4,3},{5,4},{6,5},{7,6},{8,7},{9,8},{10,9},{11,1... | collective-permute-start | bytes 3145736 | tf_op jit(solution)/shard_map/ppermute | solution.py:385
  84.2 24.1 %collective-permute-start.3 = (f32[128,16,128]{2,1,0:T(8,128)S(1)}, f32[128,16,128]{2,1,0:T(8,128)S(1)}, u32[]{:S(2)}, u32[]{:S(2)}) collective-permute-start(f32[128,16,128]{2,1,0:T(8,128)S(1)} %get-tuple-element.77.high), channel_id=1, source_target_pairs={{0,1},{1,2},{2,3},{3,4},{4,5},{5,6},{6,7},{7,8},{8,9},{9,10},{10,1... | collective-permute-start | bytes 3145736 | tf_op jit(solution)/shard_map/ppermute | solution.py:385
  87.2 21.1 %collective-permute-start.4 = (f32[128,16,128]{2,1,0:T(8,128)S(1)}, f32[128,16,128]{2,1,0:T(8,128)S(1)}, u32[]{:S(2)}, u32[]{:S(2)}) collective-permute-start(f32[128,16,128]{2,1,0:T(8,128)S(1)} %get-tuple-element.76.low), channel_id=1, source_target_pairs={{1,0},{2,1},{3,2},{4,3},{5,4},{6,5},{7,6},{8,7},{9,8},{10,9},{11,1... | collective-permute-start | bytes 3145736 | tf_op jit(solution)/shard_map/ppermute | solution.py:385
  102.5 17.2 %collective-permute-start.10 = (f32[128,16,128]{2,1,0:T(8,128)S(1)}, f32[128,16,128]{2,1,0:T(8,128)S(1)}, u32[]{:S(2)}, u32[]{:S(2)}) collective-permute-start(f32[128,16,128]{2,1,0:T(8,128)S(1)} %get-tuple-element.73), channel_id=1, source_target_pairs={{1,0},{2,1},{3,2},{4,3},{5,4},{6,5},{7,6},{8,7},{9,8},{10,9},{11,1... | collective-permute-start | bytes 3145736 | tf_op jit(solution)/shard_map/ppermute | solution.py:385
  104.4 15.4 %collective-permute-start.9 = (f32[128,16,128]{2,1,0:T(8,128)S(1)}, f32[128,16,128]{2,1,0:T(8,128)S(1)}, u32[]{:S(2)}, u32[]{:S(2)}) collective-permute-start(f32[128,16,128]{2,1,0:T(8,128)S(1)} %get-tuple-element.74), channel_id=1, source_target_pairs={{0,1},{1,2},{2,3},{3,4},{4,5},{5,6},{6,7},{7,8},{8,9},{9,10},{10,1... | collective-permute-start | bytes 3145736 | tf_op jit(solution)/shard_map/ppermute | solution.py:385
  115.1 18.1 %copy-start.7 = (f32[128,16,128]{2,1,0:T(8,128)}, f32[128,16,128]{2,1,0:T(8,128)S(1)}, u32[]{:S(2)}) copy-start(f32[128,16,128]{2,1,0:T(8,128)S(1)} %get-tuple-element.80) | copy-start | bytes 3145732
  115.2 15.8 %collective-permute-start.7 = (f32[128,16,128]{2,1,0:T(8,128)S(1)}, f32[128,16,128]{2,1,0:T(8,128)S(1)}, u32[]{:S(2)}, u32[]{:S(2)}) collective-permute-start(f32[128,16,128]{2,1,0:T(8,128)S(1)} %get-tuple-element.79), channel_id=1, source_target_pairs={{0,1},{1,2},{2,3},{3,4},{4,5},{5,6},{6,7},{7,8},{8,9},{9,10},{10,1... | collective-permute-start | bytes 3145736 | tf_op jit(solution)/shard_map/ppermute | solution.py:385
  117.1 16.1 %collective-permute-start.8 = (f32[128,16,128]{2,1,0:T(8,128)S(1)}, f32[128,16,128]{2,1,0:T(8,128)S(1)}, u32[]{:S(2)}, u32[]{:S(2)}) collective-permute-start(f32[128,16,128]{2,1,0:T(8,128)S(1)} %get-tuple-element.80), channel_id=1, source_target_pairs={{1,0},{2,1},{3,2},{4,3},{5,4},{6,5},{7,6},{8,7},{9,8},{10,9},{11,1... | collective-permute-start | bytes 3145736 | tf_op jit(solution)/shard_map/ppermute | solution.py:385
  135.7 47.3 %all-to-all-start.1 = ((f32[32,2,2,32,128]{4,3,2,1,0:T(8,128)}), f32[32,2,2,32,128]{4,3,2,1,0:T(8,128)S(1)}, u32[]{:S(2)}, u32[]{:S(2)}) async-start(f32[32,2,2,32,128]{4,3,2,1,0:T(8,128)} %get-tuple-element.83), calls=%async_computation.1 | async-start | bytes 4194304 | tf_op jit(solution)/shard_map/all_to_all | solution.py:389
  154.8 9.1 %collective-permute-start.18 = (f32[33,16,128]{2,1,0:T(8,128)S(1)}, f32[33,16,128]{2,1,0:T(8,128)S(1)}, u32[]{:S(2)}, u32[]{:S(2)}) collective-permute-start(f32[33,16,128]{2,1,0:T(8,128)S(1)} %get-tuple-element.97), channel_id=1, source_target_pairs={{0,32},{32,64},{64,96},{96,0},{1,33},{33,65},{65,97},{97,1},{2,34}... | collective-permute-start | bytes 811016 | tf_op jit(solution)/shard_map/ppermute | solution.py:385
  156.8 13.1 %collective-permute-start.20 = (f32[33,16,128]{2,1,0:T(8,128)S(1)}, f32[33,16,128]{2,1,0:T(8,128)S(1)}, u32[]{:S(2)}, u32[]{:S(2)}) collective-permute-start(f32[33,16,128]{2,1,0:T(8,128)S(1)} %get-tuple-element.99), channel_id=1, source_target_pairs={{0,64},{32,96},{64,0},{96,32},{1,65},{33,97},{65,1},{97,33},{2,66}... | collective-permute-start | bytes 811016 | tf_op jit(solution)/shard_map/ppermute | solution.py:385
  157.7 12.4 %collective-permute-start.22 = (f32[33,16,128]{2,1,0:T(8,128)S(1)}, f32[33,16,128]{2,1,0:T(8,128)S(1)}, u32[]{:S(2)}, u32[]{:S(2)}) collective-permute-start(f32[33,16,128]{2,1,0:T(8,128)S(1)} %get-tuple-element.101), channel_id=1, source_target_pairs={{0,96},{32,0},{64,32},{96,64},{1,97},{33,1},{65,33},{97,65},{2,98}... | collective-permute-start | bytes 811016 | tf_op jit(solution)/shard_map/ppermute | solution.py:385
  161.0 14.9 %collective-permute-start.17 = (f32[33,16,128]{2,1,0:T(8,128)S(1)}, f32[33,16,128]{2,1,0:T(8,128)S(1)}, u32[]{:S(2)}, u32[]{:S(2)}) collective-permute-start(f32[33,16,128]{2,1,0:T(8,128)S(1)} %get-tuple-element.96), channel_id=1, source_target_pairs={{0,32},{32,64},{64,96},{96,0},{1,33},{33,65},{65,97},{97,1},{2,34}... | collective-permute-start | bytes 811016 | tf_op jit(solution)/shard_map/ppermute | solution.py:385
  161.1 20.4 %collective-permute-start.19 = (f32[33,16,128]{2,1,0:T(8,128)S(1)}, f32[33,16,128]{2,1,0:T(8,128)S(1)}, u32[]{:S(2)}, u32[]{:S(2)}) collective-permute-start(f32[33,16,128]{2,1,0:T(8,128)S(1)} %get-tuple-element.98), channel_id=1, source_target_pairs={{0,64},{32,96},{64,0},{96,32},{1,65},{33,97},{65,1},{97,33},{2,66}... | collective-permute-start | bytes 811016 | tf_op jit(solution)/shard_map/ppermute | solution.py:385
  163.9 17.8 %collective-permute-start.21 = (f32[33,16,128]{2,1,0:T(8,128)S(1)}, f32[33,16,128]{2,1,0:T(8,128)S(1)}, u32[]{:S(2)}, u32[]{:S(2)}) collective-permute-start(f32[33,16,128]{2,1,0:T(8,128)S(1)} %get-tuple-element.100), channel_id=1, source_target_pairs={{0,96},{32,0},{64,32},{96,64},{1,97},{33,1},{65,33},{97,65},{2,98}... | collective-permute-start | bytes 811016 | tf_op jit(solution)/shard_map/ppermute | solution.py:385
  183.0 37.2 %all-to-all-start.2 = ((f32[32,4,2,16,128]{4,3,2,1,0:T(8,128)}), f32[32,4,2,16,128]{4,3,2,1,0:T(8,128)}, u32[]{:S(2)}, u32[]{:S(2)}) async-start(f32[32,4,2,16,128]{4,3,2,1,0:T(8,128)} %get-tuple-element.103), calls=%async_computation.2 | async-start | bytes 4194304 | tf_op jit(solution)/shard_map/all_to_all | solution.py:389
  192.4 47.8 %copy-start = (f32[32,128,128]{2,1,0:T(8,128)S(1)}, f32[32,128,128]{2,1,0:T(8,128)}, u32[]{:S(2)}) copy-start(f32[32,128,128]{2,1,0:T(8,128)} %param.4) | copy-start | bytes 6291460
  192.4 8.9 %collective-permute-start.11 = (f32[8,2,32,128]{3,2,1,0:T(8,128)S(1)}, f32[8,2,32,128]{3,2,1,0:T(8,128)S(1)}, u32[]{:S(2)}, u32[]{:S(2)}) collective-permute-start(f32[8,2,32,128]{3,2,1,0:T(8,128)S(1)} %get-tuple-element.87), channel_id=1, source_target_pairs={{0,32},{32,64},{64,96},{96,0},{1,33},{33,65},{65,97},{97,1},{2,34}... | collective-permute-start | bytes 786440 | tf_op jit(solution)/shard_map/ppermute | solution.py:385
  193.8 13.9 %collective-permute-start.12 = (f32[8,2,32,128]{3,2,1,0:T(8,128)S(1)}, f32[8,2,32,128]{3,2,1,0:T(8,128)S(1)}, u32[]{:S(2)}, u32[]{:S(2)}) collective-permute-start(f32[8,2,32,128]{3,2,1,0:T(8,128)S(1)} %get-tuple-element.88), channel_id=1, source_target_pairs={{0,64},{32,96},{64,0},{96,32},{1,65},{33,97},{65,1},{97,33},{2,66}... | collective-permute-start | bytes 786440 | tf_op jit(solution)/shard_map/ppermute | solution.py:385
  195.9 11.8 %collective-permute-start.13 = (f32[8,2,32,128]{3,2,1,0:T(8,128)S(1)}, f32[8,2,32,128]{3,2,1,0:T(8,128)S(1)}, u32[]{:S(2)}, u32[]{:S(2)}) collective-permute-start(f32[8,2,32,128]{3,2,1,0:T(8,128)S(1)} %get-tuple-element.89), channel_id=1, source_target_pairs={{0,96},{32,0},{64,32},{96,64},{1,97},{33,1},{65,33},{97,65},{2,98}... | collective-permute-start | bytes 786440 | tf_op jit(solution)/shard_map/ppermute | solution.py:385
  207.8 17.9 %collective-permute-start.16 = (f32[8,2,32,128]{3,2,1,0:T(8,128)S(1)}, f32[8,2,32,128]{3,2,1,0:T(8,128)S(1)}, u32[]{:S(2)}, u32[]{:S(2)}) collective-permute-start(f32[8,2,32,128]{3,2,1,0:T(8,128)S(1)} %shard_map.54.refs_0_), channel_id=1, source_target_pairs={{0,96},{32,0},{64,32},{96,64},{1,97},{33,1},{65,33},{97,65},{2,98}... | collective-permute-start | bytes 786440 | tf_op jit(solution)/shard_map/ppermute | solution.py:385
  210.7 15.1 %collective-permute-start.15 = (f32[8,2,32,128]{3,2,1,0:T(8,128)S(1)}, f32[8,2,32,128]{3,2,1,0:T(8,128)S(1)}, u32[]{:S(2)}, u32[]{:S(2)}) collective-permute-start(f32[8,2,32,128]{3,2,1,0:T(8,128)S(1)} %shard_map.54.refs_0_), channel_id=1, source_target_pairs={{0,64},{32,96},{64,0},{96,32},{1,65},{33,97},{65,1},{97,33},{2,66}... | collective-permute-start | bytes 786440 | tf_op jit(solution)/shard_map/ppermute | solution.py:385
  211.3 14.8 %collective-permute-start.14 = (f32[8,2,32,128]{3,2,1,0:T(8,128)S(1)}, f32[8,2,32,128]{3,2,1,0:T(8,128)S(1)}, u32[]{:S(2)}, u32[]{:S(2)}) collective-permute-start(f32[8,2,32,128]{3,2,1,0:T(8,128)S(1)} %shard_map.54.refs_0_), channel_id=1, source_target_pairs={{0,32},{32,64},{64,96},{96,0},{1,33},{33,65},{65,97},{97,1},{2,34}... | collective-permute-start | bytes 786440 | tf_op jit(solution)/shard_map/ppermute | solution.py:385
  222.5 7.0 %collective-permute-start.25 = (f32[32,16,128]{2,1,0:T(8,128)S(1)}, f32[32,16,128]{2,1,0:T(8,128)S(1)}, u32[]{:S(2)}, u32[]{:S(2)}) collective-permute-start(f32[32,16,128]{2,1,0:T(8,128)S(1)} %shard_map.58.refs_4_), channel_id=1, source_target_pairs={{0,96},{32,0},{64,32},{96,64},{1,97},{33,1},{65,33},{97,65},{2,98}... | collective-permute-start | bytes 786440 | tf_op jit(solution)/shard_map/ppermute | solution.py:385
  224.8 7.5 %collective-permute-start.24 = (f32[32,16,128]{2,1,0:T(8,128)S(1)}, f32[32,16,128]{2,1,0:T(8,128)S(1)}, u32[]{:S(2)}, u32[]{:S(2)}) collective-permute-start(f32[32,16,128]{2,1,0:T(8,128)S(1)} %shard_map.58.refs_4_), channel_id=1, source_target_pairs={{0,64},{32,96},{64,0},{96,32},{1,65},{33,97},{65,1},{97,33},{2,66}... | collective-permute-start | bytes 786440 | tf_op jit(solution)/shard_map/ppermute | solution.py:385
  225.7 14.5 %collective-permute-start.23 = (f32[32,16,128]{2,1,0:T(8,128)S(1)}, f32[32,16,128]{2,1,0:T(8,128)S(1)}, u32[]{:S(2)}, u32[]{:S(2)}) collective-permute-start(f32[32,16,128]{2,1,0:T(8,128)S(1)} %shard_map.58.refs_4_), channel_id=1, source_target_pairs={{0,32},{32,64},{64,96},{96,0},{1,33},{33,65},{65,97},{97,1},{2,34}... | collective-permute-start | bytes 786440 | tf_op jit(solution)/shard_map/ppermute | solution.py:385
  (19 other events, 92.4 us)

commit v5 on v4

--- a/solution.py
+++ b/solution.py
@@ -19,7 +19,7 @@
 NPAD = ZD + 2 * PAD
 PLANES = 4
 STEPS = 4
-WIDE = 4
+WIDE = 8
 ROWS = ZD // STEPS
 PITCH = NY + 8
 WORK = ZD + 8
@@ -192,11 +192,14 @@
         done = left_dot(zmat[v], padded_pair(parts, c * 2, c * 2 + 1))
         return done[:, :NX], done[:, NX:]
 
-    def step(slot, carry):
-        send[slot, 0, 0], send[slot, 0, 1] = move(table[v, base + slot])
+    def step(n, carry):
+        at = [table[v, base + n * 2 + i] * 2 for i in range(2)]
+        done = left_dot(zmat[v], padded_pair(parts, at[0], at[0] + 1, at[1], at[1] + 1))
+        for i in range(4):
+            send[n * 2 + i // 2, 0, i % 2] = done[:, i * NX : (i + 1) * NX]
         return carry
 
-    lax.fori_loop(0, slots, step, 0, unroll=slots)
+    lax.fori_loop(0, slots // 2, step, 0, unroll=slots // 2)
 
     @pl.when(pl.program_id(0) == 0)
     def _():
@@ -207,14 +210,20 @@
     parts = [p.reshape(NY // 2, PAD, NX) for p in (top, low, high, bottom)]
     *outs, work = refs
 
-    def step(slot, carry):
-        y = table[v, slot] * 2
-        done = left_dot(zmat[v], padded_pair(parts, y, y + 1))
-        work[slot, pl.ds(0, ZD), :] = done[:, :NX]
-        work[slot, pl.ds(ZD, ZD), :] = done[:, NX:]
+    def put(*slots):
+        at = [table[v, slot] * 2 for slot in slots]
+        done = left_dot(zmat[v], padded_pair(parts, *[y + i for y in at for i in range(2)]))
+        for n, slot in enumerate(slots):
+            for i in range(2):
+                first = (2 * n + i) * NX
+                work[slot, pl.ds(i * ZD, ZD), :] = done[:, first : first + NX]
+
+    def step(n, carry):
+        put(n * 2, n * 2 + 1)
         return carry
 
-    lax.fori_loop(0, GRID + 1, step, 0, unroll=11)
+    lax.fori_loop(0, GRID // 2, step, 0, unroll=8)
+    put(GRID)
     for hop, out in enumerate(outs):
         quarter = lax.rem(plane[0] + hop, PLANES)
         out[...] = work[:, pl.ds(pl.multiple_of(quarter * PAD, PAD), PAD), :]

time: 244 us -> 243 us (level)
  transfers between devices with their start and end apart: 29 -> 29, of which waited for: 19 -> 19; matrix products, arithmetic and copies ran while one was open for 2% -> 2% of each run, Pallas kernels for 13% -> 12%
where the time goes in v5:
time: 243 us; the launch traced here: 242 us
  waiting for transfers between devices  113 us (47%)
  starting transfers between devices  74.9 us (31%)
  Pallas kernels  37 us (15%)
  other arithmetic  8.37 us (3%)
  local copies, waits for them, and re-layouts  7.96 us (3%)
    ppermute x26, waiting for transfers between devices, shifted(): return lax.ppermute(value, axis, pairs)  61.1 us
    all_to_all x3, waiting for transfers between devices, exchange(): return lax.all_to_all(value, axis, 0, 0, tiled=True)  52 us
    ppermute x26, starting transfers between devices, shifted(): return lax.ppermute(value, axis, pairs)  45.6 us
    pallas_call x14, Pallas kernels, call(): pl.pallas_call(kernel, out_shape=[(pltpu.HBM if n in far else jax.ShapeDt...  36.9 us
    all_to_all x3, starting transfers between devices, exchange(): return lax.all_to_all(value, axis, 0, 0, tiled=True)  29.3 us
    unnamed x44, local copies, waits for them, and re-layouts  7.77 us
  transfers between devices with their start and end apart: 29, of which 19 were waited for; matrix products, arithmetic and copies ran while one was open for 2% of the time, Pallas kernels for 12%

profile of v5, /device:TPU:1, one launch (start us, length us, event | category | flops | bytes accessed | tf_op | source)
XLA Modules:
  0.0 241.7 jit_solution(15771807297001051915)
XLA Ops:
  4.0 4.6 %collective-permute-start.2 = (s32[2,32]{1,0:T(2,128)S(1)}, s32[2,32]{1,0:T(2,128)S(1)}, u32[]{:S(2)}, u32[]{:S(2)}) collective-permute-start(s32[2,32]{1,0:T(2,128)S(1)} %select_reduce_fusion.2.table.refs_0_), channel_id=1, source_target_pairs={{0,96},{32,0},{64,32},{96,64},{1,97},{33,1},{65,33},{97,65},{2,98}... | collective-permute-start | bytes 776 | tf_op jit(solution)/shard_map/ppermute | solution.py:394
  9.4 4.3 %shard_map.46 = (f32[32,2,4,32,128]{4,3,2,1,0:T(8,128)}, f32[1,4,32,128]{3,2,1,0:T(8,128)}, f32[1,4,32,128]{3,2,1,0:T(8,128)}) custom-call(s32[2,32]{1,0:T(2,128)S(1)} %and_select_fusion.1.table, s32[2]{0:T(128)S(1)} %get-tuple-element.119.last, f32[4096,128]{1,0:T(8,128)} %bitcast.19), custom_call_target="tpu_custom_call" | custom-call | bytes 4194304 | tf_op jit(solution)/shard_map/pallas_call | solution.py:40
  13.7 8.7 %all-to-all-start = ((f32[32,2,4,32,128]{4,3,2,1,0:T(8,128)}), f32[32,2,4,32,128]{4,3,2,1,0:T(8,128)}, u32[]{:S(2)}, u32[]{:S(2)}) async-start(f32[32,2,4,32,128]{4,3,2,1,0:T(8,128)} %get-tuple-element.55), calls=%async_computation | async-start | bytes 8388608 | tf_op jit(solution)/shard_map/all_to_all | solution.py:398
  29.9 43.2 %all-to-all-done.recv = f32[32,2,4,32,128]{4,3,2,1,0:T(8,128)} async-done(((f32[32,2,4,32,128]{4,3,2,1,0:T(8,128)}), f32[32,2,4,32,128]{4,3,2,1,0:T(8,128)}, u32[]{:S(2)}, u32[]{:S(2)}) %all-to-all-start) | async-done | bytes 4194336 | tf_op jit(solution)/shard_map/all_to_all | solution.py:398
  75.2 4.3 %collective-permute-start.5 = (f32[128,16,128]{2,1,0:T(8,128)S(1)}, f32[128,16,128]{2,1,0:T(8,128)S(1)}, u32[]{:S(2)}, u32[]{:S(2)}) collective-permute-start(f32[128,16,128]{2,1,0:T(8,128)S(1)} %get-tuple-element.67.high), channel_id=1, source_target_pairs={{0,1},{1,2},{2,3},{3,4},{4,5},{5,6},{6,7},{7,8},{8,9},{9,10},{10,1... | collective-permute-start | bytes 3145736 | tf_op jit(solution)/shard_map/ppermute | solution.py:394
  79.5 2.6 %collective-permute-start.6 = (f32[128,16,128]{2,1,0:T(8,128)S(1)}, f32[128,16,128]{2,1,0:T(8,128)S(1)}, u32[]{:S(2)}, u32[]{:S(2)}) collective-permute-start(f32[128,16,128]{2,1,0:T(8,128)S(1)} %get-tuple-element.62.low), channel_id=1, source_target_pairs={{1,0},{2,1},{3,2},{4,3},{5,4},{6,5},{7,6},{8,7},{9,8},{10,9},{11,1... | collective-permute-start | bytes 3145736 | tf_op jit(solution)/shard_map/ppermute | solution.py:394
  82.1 2.1 shard_map.48
  84.2 3.0 %collective-permute-start.3 = (f32[128,16,128]{2,1,0:T(8,128)S(1)}, f32[128,16,128]{2,1,0:T(8,128)S(1)}, u32[]{:S(2)}, u32[]{:S(2)}) collective-permute-start(f32[128,16,128]{2,1,0:T(8,128)S(1)} %get-tuple-element.77.high), channel_id=1, source_target_pairs={{0,1},{1,2},{2,3},{3,4},{4,5},{5,6},{6,7},{7,8},{8,9},{9,10},{10,1... | collective-permute-start | bytes 3145736 | tf_op jit(solution)/shard_map/ppermute | solution.py:394
  91.2 4.4 %collective-permute-done.6.bottom = f32[128,16,128]{2,1,0:T(8,128)S(1)} collective-permute-done((f32[128,16,128]{2,1,0:T(8,128)S(1)}, f32[128,16,128]{2,1,0:T(8,128)S(1)}, u32[]{:S(2)}, u32[]{:S(2)}) %collective-permute-start.6) | collective-permute-done | bytes 1048608 | tf_op jit(solution)/shard_map/ppermute | solution.py:394
  95.6 6.3 %shard_map.49 = (f32[128,16,128]{2,1,0:T(8,128)S(1)}, f32[128,16,128]{2,1,0:T(8,128)S(1)}) custom-call(f32[128,16,128]{2,1,0:T(8,128)S(1)} %collective-permute-done.5.top, f32[128,16,128]{2,1,0:T(8,128)S(1)} %get-tuple-element.62.low, f32[128,16,128]{2,1,0:T(8,128)S(1)} %get-tuple-element.67.high, f32[128,16,128]{2,1,0:T(8,128)S(1)} %collective-permute-done.6.bottom, ...), custom_call_target="tpu_custom_call" | custom-call | flops 5368709120 | bytes 8388608 | tf_op jit(solution)/shard_map/pallas_call | solution.py:40
  103.8 3.8 %collective-permute-start.9 = (f32[128,16,128]{2,1,0:T(8,128)S(1)}, f32[128,16,128]{2,1,0:T(8,128)S(1)}, u32[]{:S(2)}, u32[]{:S(2)}) collective-permute-start(f32[128,16,128]{2,1,0:T(8,128)S(1)} %get-tuple-element.74), channel_id=1, source_target_pairs={{0,1},{1,2},{2,3},{3,4},{4,5},{5,6},{6,7},{7,8},{8,9},{9,10},{10,1... | collective-permute-start | bytes 3145736 | tf_op jit(solution)/shard_map/ppermute | solution.py:394
  107.7 6.3 %shard_map.50 = (f32[128,16,128]{2,1,0:T(8,128)S(1)}, f32[128,16,128]{2,1,0:T(8,128)S(1)}) custom-call(f32[128,16,128]{2,1,0:T(8,128)S(1)} %collective-permute-done.3.top, f32[128,16,128]{2,1,0:T(8,128)S(1)} %get-tuple-element.76.low, f32[128,16,128]{2,1,0:T(8,128)S(1)} %get-tuple-element.77.high, f32[128,16,128]{2,1,0:T(8,128)S(1)} %collective-permute-done.4.bottom, ...), custom_call_target="tpu_custom_call" | custom-call | flops 5368709120 | bytes 8388608 | tf_op jit(solution)/shard_map/pallas_call | solution.py:40
  115.9 2.5 %collective-permute-start.8 = (f32[128,16,128]{2,1,0:T(8,128)S(1)}, f32[128,16,128]{2,1,0:T(8,128)S(1)}, u32[]{:S(2)}, u32[]{:S(2)}) collective-permute-start(f32[128,16,128]{2,1,0:T(8,128)S(1)} %get-tuple-element.80), channel_id=1, source_target_pairs={{1,0},{2,1},{3,2},{4,3},{5,4},{6,5},{7,6},{8,7},{9,8},{10,9},{11,1... | collective-permute-start | bytes 3145736 | tf_op jit(solution)/shard_map/ppermute | solution.py:394
  119.2 2.5 %shard_map.51 = (f32[32,2,2,32,128]{4,3,2,1,0:T(8,128)}, f32[2,32,128]{2,1,0:T(8,128)S(1)}) custom-call(s32[2,33]{1,0:T(2,128)S(1)} %select_reduce_fusion.6.table, f32[32,4,16,128]{3,2,1,0:T(8,128)S(1)} %bitcast.27, f32[32,4,16,128]{3,2,1,0:T(8,128)S(1)} %bitcast.21, f32[32,4,16,128]{3,2,1,0:T(8,128)S(1)} %bitcast.23, f32[32,4,16,128]{3,2,1,0:T(8,128)S(1)} %bitcast.25, ...), custom_call_target="tpu_custom_call" | custom-call | flops 1073741824 | bytes 4194304 | tf_op jit(solution)/shard_map/pallas_call | solution.py:40
  121.7 8.8 %collective-permute-done.7 = f32[128,16,128]{2,1,0:T(8,128)S(1)} collective-permute-done((f32[128,16,128]{2,1,0:T(8,128)S(1)}, f32[128,16,128]{2,1,0:T(8,128)S(1)}, u32[]{:S(2)}, u32[]{:S(2)}) %collective-permute-start.7) | collective-permute-done | bytes 1048608 | tf_op jit(solution)/shard_map/ppermute | solution.py:394
  132.0 2.5 %shard_map.52 = (f32[32,2,2,32,128]{4,3,2,1,0:T(8,128)}, f32[2,32,128]{2,1,0:T(8,128)S(1)}) custom-call(s32[2,33]{1,0:T(2,128)S(1)} %select_reduce_fusion.6.table, f32[32,4,16,128]{3,2,1,0:T(8,128)S(1)} %bitcast.33, f32[32,4,16,128]{3,2,1,0:T(8,128)S(1)} %bitcast.29, f32[32,4,16,128]{3,2,1,0:T(8,128)S(1)} %bitcast.31, ...), custom_call_target="tpu_custom_call", output_to_operand_aliasing={{0}: (6, {})} | custom-call | flops 1073741824 | bytes 4194304 | tf_op jit(solution)/shard_map/pallas_call | solution.py:40
  134.5 12.2 %all-to-all-start.1 = ((f32[32,2,2,32,128]{4,3,2,1,0:T(8,128)}), f32[32,2,2,32,128]{4,3,2,1,0:T(8,128)S(1)}, u32[]{:S(2)}, u32[]{:S(2)}) async-start(f32[32,2,2,32,128]{4,3,2,1,0:T(8,128)} %get-tuple-element.83), calls=%async_computation.1 | async-start | bytes 4194304 | tf_op jit(solution)/shard_map/all_to_all | solution.py:398
  163.0 5.6 %collective-permute-done.20.refs_5_ = f32[33,16,128]{2,1,0:T(8,128)S(1)} collective-permute-done((f32[33,16,128]{2,1,0:T(8,128)S(1)}, f32[33,16,128]{2,1,0:T(8,128)S(1)}, u32[]{:S(2)}, u32[]{:S(2)}) %collective-permute-start.20) | collective-permute-done | bytes 270368 | tf_op jit(solution)/shard_map/ppermute | solution.py:394
  168.8 5.8 %collective-permute-done.17.refs_2_ = f32[33,16,128]{2,1,0:T(8,128)S(1)} collective-permute-done((f32[33,16,128]{2,1,0:T(8,128)S(1)}, f32[33,16,128]{2,1,0:T(8,128)S(1)}, u32[]{:S(2)}, u32[]{:S(2)}) %collective-permute-start.17) | collective-permute-done | bytes 270368 | tf_op jit(solution)/shard_map/ppermute | solution.py:394
  174.6 5.5 %collective-permute-done.19.refs_4_ = f32[33,16,128]{2,1,0:T(8,128)S(1)} collective-permute-done((f32[33,16,128]{2,1,0:T(8,128)S(1)}, f32[33,16,128]{2,1,0:T(8,128)S(1)}, u32[]{:S(2)}, u32[]{:S(2)}) %collective-permute-start.19) | collective-permute-done | bytes 270368 | tf_op jit(solution)/shard_map/ppermute | solution.py:394
  181.7 8.4 %all-to-all-start.2 = ((f32[32,4,2,16,128]{4,3,2,1,0:T(8,128)}), f32[32,4,2,16,128]{4,3,2,1,0:T(8,128)}, u32[]{:S(2)}, u32[]{:S(2)}) async-start(f32[32,4,2,16,128]{4,3,2,1,0:T(8,128)} %get-tuple-element.103), calls=%async_computation.2 | async-start | bytes 4194304 | tf_op jit(solution)/shard_map/all_to_all | solution.py:398
  192.5 2.1 collective-permute-start.12
  195.6 4.4 %collective-permute-done.11.second = f32[8,2,32,128]{3,2,1,0:T(8,128)S(1)} collective-permute-done((f32[8,2,32,128]{3,2,1,0:T(8,128)S(1)}, f32[8,2,32,128]{3,2,1,0:T(8,128)S(1)}, u32[]{:S(2)}, u32[]{:S(2)}) %collective-permute-start.11) | collective-permute-done | bytes 262176 | tf_op jit(solution)/shard_map/ppermute | solution.py:394
  200.0 6.4 %collective-permute-done.12.third = f32[8,2,32,128]{3,2,1,0:T(8,128)S(1)} collective-permute-done((f32[8,2,32,128]{3,2,1,0:T(8,128)S(1)}, f32[8,2,32,128]{3,2,1,0:T(8,128)S(1)}, u32[]{:S(2)}, u32[]{:S(2)}) %collective-permute-start.12) | collective-permute-done | bytes 262176 | tf_op jit(solution)/shard_map/ppermute | solution.py:394
  206.5 2.9 %collective-permute-start.16 = (f32[8,2,32,128]{3,2,1,0:T(8,128)S(1)}, f32[8,2,32,128]{3,2,1,0:T(8,128)S(1)}, u32[]{:S(2)}, u32[]{:S(2)}) collective-permute-start(f32[8,2,32,128]{3,2,1,0:T(8,128)S(1)} %shard_map.54.refs_0_), channel_id=1, source_target_pairs={{0,96},{32,0},{64,32},{96,64},{1,97},{33,1},{65,33},{97,65},{2,98}... | collective-permute-start | bytes 786440 | tf_op jit(solution)/shard_map/ppermute | solution.py:394
  210.1 8.8 %all-to-all-done.2.refs_4_ = f32[32,4,2,16,128]{4,3,2,1,0:T(8,128)} async-done(((f32[32,4,2,16,128]{4,3,2,1,0:T(8,128)}), f32[32,4,2,16,128]{4,3,2,1,0:T(8,128)}, u32[]{:S(2)}, u32[]{:S(2)}) %all-to-all-start.2) | async-done | bytes 2097184 | tf_op jit(solution)/shard_map/all_to_all | solution.py:398
  218.9 2.3 shard_map.58.refs_4_
  221.1 2.4 collective-permute-start.25
  224.7 3.4 %collective-permute-done.25.refs_7_ = f32[32,16,128]{2,1,0:T(8,128)S(1)} collective-permute-done((f32[32,16,128]{2,1,0:T(8,128)S(1)}, f32[32,16,128]{2,1,0:T(8,128)S(1)}, u32[]{:S(2)}, u32[]{:S(2)}) %collective-permute-start.25) | collective-permute-done | bytes 262176 | tf_op jit(solution)/shard_map/ppermute | solution.py:394
  228.2 2.9 %collective-permute-done.24.refs_6_ = f32[32,16,128]{2,1,0:T(8,128)S(1)} collective-permute-done((f32[32,16,128]{2,1,0:T(8,128)S(1)}, f32[32,16,128]{2,1,0:T(8,128)S(1)}, u32[]{:S(2)}, u32[]{:S(2)}) %collective-permute-start.24) | collective-permute-done | bytes 262176 | tf_op jit(solution)/shard_map/ppermute | solution.py:394
  231.1 7.8 %collective-permute-done.23.refs_5_ = f32[32,16,128]{2,1,0:T(8,128)S(1)} collective-permute-done((f32[32,16,128]{2,1,0:T(8,128)S(1)}, f32[32,16,128]{2,1,0:T(8,128)S(1)}, u32[]{:S(2)}, u32[]{:S(2)}) %collective-permute-start.23) | collective-permute-done | bytes 262176 | tf_op jit(solution)/shard_map/ppermute | solution.py:394
  238.9 2.8 %shard_map.59 = f32[4096,128]{1,0:T(8,128)} custom-call(s32[4]{0:T(128)S(1)} %and_select_fusion.3.place, f32[4096,128]{1,0:T(8,128)S(1)} %bitcast.20, f32[8,2,32,128]{3,2,1,0:T(8,128)S(1)} %shard_map.54.refs_0_, f32[8,2,32,128]{3,2,1,0:T(8,128)S(1)} %collective-permute-done.14.refs_1_, f32[8,2,32,128]{3,2,1,0:T(8,128)S(1)} %collective-permute-done.15.refs_2_, ...), custom_call_target="tpu_custom_call" | custom-call | bytes 6291456 | tf_op jit(solution)/shard_map/pallas_call | solution.py:40
  (125 shorter events, 47.7 us)
Async XLA Ops:
  4.0 25.9 %collective-permute-start.2 = (s32[2,32]{1,0:T(2,128)S(1)}, s32[2,32]{1,0:T(2,128)S(1)}, u32[]{:S(2)}, u32[]{:S(2)}) collective-permute-start(s32[2,32]{1,0:T(2,128)S(1)} %select_reduce_fusion.2.table.refs_0_), channel_id=1, source_target_pairs={{0,96},{32,0},{64,32},{96,64},{1,97},{33,1},{65,33},{97,65},{2,98}... | collective-permute-start | bytes 776 | tf_op jit(solution)/shard_map/ppermute | solution.py:394
  8.7 21.2 %collective-permute-start.1 = (s32[2,32]{1,0:T(2,128)S(1)}, s32[2,32]{1,0:T(2,128)S(1)}, u32[]{:S(2)}, u32[]{:S(2)}) collective-permute-start(s32[2,32]{1,0:T(2,128)S(1)} %select_reduce_fusion.2.table.refs_0_), channel_id=1, source_target_pairs={{0,64},{32,96},{64,0},{96,32},{1,65},{33,97},{65,1},{97,33},{2,66}... | collective-permute-start | bytes 776 | tf_op jit(solution)/shard_map/ppermute | solution.py:394
  8.7 21.2 %collective-permute-start = (s32[2,32]{1,0:T(2,128)S(1)}, s32[2,32]{1,0:T(2,128)S(1)}, u32[]{:S(2)}, u32[]{:S(2)}) collective-permute-start(s32[2,32]{1,0:T(2,128)S(1)} %select_reduce_fusion.2.table.refs_0_), channel_id=1, source_target_pairs={{0,32},{32,64},{64,96},{96,0},{1,33},{33,65},{65,97},{97,1},{2,34}... | collective-permute-start | bytes 776 | tf_op jit(solution)/shard_map/ppermute | solution.py:394
  13.7 59.4 %all-to-all-start = ((f32[32,2,4,32,128]{4,3,2,1,0:T(8,128)}), f32[32,2,4,32,128]{4,3,2,1,0:T(8,128)}, u32[]{:S(2)}, u32[]{:S(2)}) async-start(f32[32,2,4,32,128]{4,3,2,1,0:T(8,128)} %get-tuple-element.55), calls=%async_computation | async-start | bytes 8388608 | tf_op jit(solution)/shard_map/all_to_all | solution.py:398
  22.4 50.7 %copy-start.16 = (f32[1,4,32,128]{3,2,1,0:T(8,128)S(1)}, f32[1,4,32,128]{3,2,1,0:T(8,128)}, u32[]{:S(2)}) copy-start(f32[1,4,32,128]{3,2,1,0:T(8,128)} %get-tuple-element.61.kept) | copy-start | bytes 196612
  75.2 16.0 %collective-permute-start.5 = (f32[128,16,128]{2,1,0:T(8,128)S(1)}, f32[128,16,128]{2,1,0:T(8,128)S(1)}, u32[]{:S(2)}, u32[]{:S(2)}) collective-permute-start(f32[128,16,128]{2,1,0:T(8,128)S(1)} %get-tuple-element.67.high), channel_id=1, source_target_pairs={{0,1},{1,2},{2,3},{3,4},{4,5},{5,6},{6,7},{7,8},{8,9},{9,10},{10,1... | collective-permute-start | bytes 3145736 | tf_op jit(solution)/shard_map/ppermute | solution.py:394
  79.5 16.1 %collective-permute-start.6 = (f32[128,16,128]{2,1,0:T(8,128)S(1)}, f32[128,16,128]{2,1,0:T(8,128)S(1)}, u32[]{:S(2)}, u32[]{:S(2)}) collective-permute-start(f32[128,16,128]{2,1,0:T(8,128)S(1)} %get-tuple-element.62.low), channel_id=1, source_target_pairs={{1,0},{2,1},{3,2},{4,3},{5,4},{6,5},{7,6},{8,7},{9,8},{10,9},{11,1... | collective-permute-start | bytes 3145736 | tf_op jit(solution)/shard_map/ppermute | solution.py:394
  84.2 23.5 %collective-permute-start.3 = (f32[128,16,128]{2,1,0:T(8,128)S(1)}, f32[128,16,128]{2,1,0:T(8,128)S(1)}, u32[]{:S(2)}, u32[]{:S(2)}) collective-permute-start(f32[128,16,128]{2,1,0:T(8,128)S(1)} %get-tuple-element.77.high), channel_id=1, source_target_pairs={{0,1},{1,2},{2,3},{3,4},{4,5},{5,6},{6,7},{7,8},{8,9},{9,10},{10,1... | collective-permute-start | bytes 3145736 | tf_op jit(solution)/shard_map/ppermute | solution.py:394
  87.2 20.5 %collective-permute-start.4 = (f32[128,16,128]{2,1,0:T(8,128)S(1)}, f32[128,16,128]{2,1,0:T(8,128)S(1)}, u32[]{:S(2)}, u32[]{:S(2)}) collective-permute-start(f32[128,16,128]{2,1,0:T(8,128)S(1)} %get-tuple-element.76.low), channel_id=1, source_target_pairs={{1,0},{2,1},{3,2},{4,3},{5,4},{6,5},{7,6},{8,7},{9,8},{10,9},{11,1... | collective-permute-start | bytes 3145736 | tf_op jit(solution)/shard_map/ppermute | solution.py:394
  101.9 16.6 %collective-permute-start.10 = (f32[128,16,128]{2,1,0:T(8,128)S(1)}, f32[128,16,128]{2,1,0:T(8,128)S(1)}, u32[]{:S(2)}, u32[]{:S(2)}) collective-permute-start(f32[128,16,128]{2,1,0:T(8,128)S(1)} %get-tuple-element.73), channel_id=1, source_target_pairs={{1,0},{2,1},{3,2},{4,3},{5,4},{6,5},{7,6},{8,7},{9,8},{10,9},{11,1... | collective-permute-start | bytes 3145736 | tf_op jit(solution)/shard_map/ppermute | solution.py:394
  103.8 15.4 %collective-permute-start.9 = (f32[128,16,128]{2,1,0:T(8,128)S(1)}, f32[128,16,128]{2,1,0:T(8,128)S(1)}, u32[]{:S(2)}, u32[]{:S(2)}) collective-permute-start(f32[128,16,128]{2,1,0:T(8,128)S(1)} %get-tuple-element.74), channel_id=1, source_target_pairs={{0,1},{1,2},{2,3},{3,4},{4,5},{5,6},{6,7},{7,8},{8,9},{9,10},{10,1... | collective-permute-start | bytes 3145736 | tf_op jit(solution)/shard_map/ppermute | solution.py:394
  114.0 18.1 %copy-start.7 = (f32[128,16,128]{2,1,0:T(8,128)}, f32[128,16,128]{2,1,0:T(8,128)S(1)}, u32[]{:S(2)}) copy-start(f32[128,16,128]{2,1,0:T(8,128)S(1)} %get-tuple-element.80) | copy-start | bytes 3145732
  114.0 16.4 %collective-permute-start.7 = (f32[128,16,128]{2,1,0:T(8,128)S(1)}, f32[128,16,128]{2,1,0:T(8,128)S(1)}, u32[]{:S(2)}, u32[]{:S(2)}) collective-permute-start(f32[128,16,128]{2,1,0:T(8,128)S(1)} %get-tuple-element.79), channel_id=1, source_target_pairs={{0,1},{1,2},{2,3},{3,4},{4,5},{5,6},{6,7},{7,8},{8,9},{9,10},{10,1... | collective-permute-start | bytes 3145736 | tf_op jit(solution)/shard_map/ppermute | solution.py:394
  115.9 16.1 %collective-permute-start.8 = (f32[128,16,128]{2,1,0:T(8,128)S(1)}, f32[128,16,128]{2,1,0:T(8,128)S(1)}, u32[]{:S(2)}, u32[]{:S(2)}) collective-permute-start(f32[128,16,128]{2,1,0:T(8,128)S(1)} %get-tuple-element.80), channel_id=1, source_target_pairs={{1,0},{2,1},{3,2},{4,3},{5,4},{6,5},{7,6},{8,7},{9,8},{10,9},{11,1... | collective-permute-start | bytes 3145736 | tf_op jit(solution)/shard_map/ppermute | solution.py:394
  134.5 47.2 %all-to-all-start.1 = ((f32[32,2,2,32,128]{4,3,2,1,0:T(8,128)}), f32[32,2,2,32,128]{4,3,2,1,0:T(8,128)S(1)}, u32[]{:S(2)}, u32[]{:S(2)}) async-start(f32[32,2,2,32,128]{4,3,2,1,0:T(8,128)} %get-tuple-element.83), calls=%async_computation.1 | async-start | bytes 4194304 | tf_op jit(solution)/shard_map/all_to_all | solution.py:398
  153.4 9.1 %collective-permute-start.18 = (f32[33,16,128]{2,1,0:T(8,128)S(1)}, f32[33,16,128]{2,1,0:T(8,128)S(1)}, u32[]{:S(2)}, u32[]{:S(2)}) collective-permute-start(f32[33,16,128]{2,1,0:T(8,128)S(1)} %get-tuple-element.97), channel_id=1, source_target_pairs={{0,32},{32,64},{64,96},{96,0},{1,33},{33,65},{65,97},{97,1},{2,34}... | collective-permute-start | bytes 811016 | tf_op jit(solution)/shard_map/ppermute | solution.py:394
  155.4 13.1 %collective-permute-start.20 = (f32[33,16,128]{2,1,0:T(8,128)S(1)}, f32[33,16,128]{2,1,0:T(8,128)S(1)}, u32[]{:S(2)}, u32[]{:S(2)}) collective-permute-start(f32[33,16,128]{2,1,0:T(8,128)S(1)} %get-tuple-element.99), channel_id=1, source_target_pairs={{0,64},{32,96},{64,0},{96,32},{1,65},{33,97},{65,1},{97,33},{2,66}... | collective-permute-start | bytes 811016 | tf_op jit(solution)/shard_map/ppermute | solution.py:394
  156.4 12.4 %collective-permute-start.22 = (f32[33,16,128]{2,1,0:T(8,128)S(1)}, f32[33,16,128]{2,1,0:T(8,128)S(1)}, u32[]{:S(2)}, u32[]{:S(2)}) collective-permute-start(f32[33,16,128]{2,1,0:T(8,128)S(1)} %get-tuple-element.101), channel_id=1, source_target_pairs={{0,96},{32,0},{64,32},{96,64},{1,97},{33,1},{65,33},{97,65},{2,98}... | collective-permute-start | bytes 811016 | tf_op jit(solution)/shard_map/ppermute | solution.py:394
  159.6 15.1 %collective-permute-start.17 = (f32[33,16,128]{2,1,0:T(8,128)S(1)}, f32[33,16,128]{2,1,0:T(8,128)S(1)}, u32[]{:S(2)}, u32[]{:S(2)}) collective-permute-start(f32[33,16,128]{2,1,0:T(8,128)S(1)} %get-tuple-element.96), channel_id=1, source_target_pairs={{0,32},{32,64},{64,96},{96,0},{1,33},{33,65},{65,97},{97,1},{2,34}... | collective-permute-start | bytes 811016 | tf_op jit(solution)/shard_map/ppermute | solution.py:394
  159.6 20.5 %collective-permute-start.19 = (f32[33,16,128]{2,1,0:T(8,128)S(1)}, f32[33,16,128]{2,1,0:T(8,128)S(1)}, u32[]{:S(2)}, u32[]{:S(2)}) collective-permute-start(f32[33,16,128]{2,1,0:T(8,128)S(1)} %get-tuple-element.98), channel_id=1, source_target_pairs={{0,64},{32,96},{64,0},{96,32},{1,65},{33,97},{65,1},{97,33},{2,66}... | collective-permute-start | bytes 811016 | tf_op jit(solution)/shard_map/ppermute | solution.py:394
  162.5 17.8 %collective-permute-start.21 = (f32[33,16,128]{2,1,0:T(8,128)S(1)}, f32[33,16,128]{2,1,0:T(8,128)S(1)}, u32[]{:S(2)}, u32[]{:S(2)}) collective-permute-start(f32[33,16,128]{2,1,0:T(8,128)S(1)} %get-tuple-element.100), channel_id=1, source_target_pairs={{0,96},{32,0},{64,32},{96,64},{1,97},{33,1},{65,33},{97,65},{2,98}... | collective-permute-start | bytes 811016 | tf_op jit(solution)/shard_map/ppermute | solution.py:394
  181.7 37.2 %all-to-all-start.2 = ((f32[32,4,2,16,128]{4,3,2,1,0:T(8,128)}), f32[32,4,2,16,128]{4,3,2,1,0:T(8,128)}, u32[]{:S(2)}, u32[]{:S(2)}) async-start(f32[32,4,2,16,128]{4,3,2,1,0:T(8,128)} %get-tuple-element.103), calls=%async_computation.2 | async-start | bytes 4194304 | tf_op jit(solution)/shard_map/all_to_all | solution.py:398
  191.1 47.8 %copy-start = (f32[32,128,128]{2,1,0:T(8,128)S(1)}, f32[32,128,128]{2,1,0:T(8,128)}, u32[]{:S(2)}) copy-start(f32[32,128,128]{2,1,0:T(8,128)} %param.4) | copy-start | bytes 6291460
  191.1 8.9 %collective-permute-start.11 = (f32[8,2,32,128]{3,2,1,0:T(8,128)S(1)}, f32[8,2,32,128]{3,2,1,0:T(8,128)S(1)}, u32[]{:S(2)}, u32[]{:S(2)}) collective-permute-start(f32[8,2,32,128]{3,2,1,0:T(8,128)S(1)} %get-tuple-element.87), channel_id=1, source_target_pairs={{0,32},{32,64},{64,96},{96,0},{1,33},{33,65},{65,97},{97,1},{2,34}... | collective-permute-start | bytes 786440 | tf_op jit(solution)/shard_map/ppermute | solution.py:394
  192.5 13.9 %collective-permute-start.12 = (f32[8,2,32,128]{3,2,1,0:T(8,128)S(1)}, f32[8,2,32,128]{3,2,1,0:T(8,128)S(1)}, u32[]{:S(2)}, u32[]{:S(2)}) collective-permute-start(f32[8,2,32,128]{3,2,1,0:T(8,128)S(1)} %get-tuple-element.88), channel_id=1, source_target_pairs={{0,64},{32,96},{64,0},{96,32},{1,65},{33,97},{65,1},{97,33},{2,66}... | collective-permute-start | bytes 786440 | tf_op jit(solution)/shard_map/ppermute | solution.py:394
  194.6 11.8 %collective-permute-start.13 = (f32[8,2,32,128]{3,2,1,0:T(8,128)S(1)}, f32[8,2,32,128]{3,2,1,0:T(8,128)S(1)}, u32[]{:S(2)}, u32[]{:S(2)}) collective-permute-start(f32[8,2,32,128]{3,2,1,0:T(8,128)S(1)} %get-tuple-element.89), channel_id=1, source_target_pairs={{0,96},{32,0},{64,32},{96,64},{1,97},{33,1},{65,33},{97,65},{2,98}... | collective-permute-start | bytes 786440 | tf_op jit(solution)/shard_map/ppermute | solution.py:394
  206.5 17.9 %collective-permute-start.16 = (f32[8,2,32,128]{3,2,1,0:T(8,128)S(1)}, f32[8,2,32,128]{3,2,1,0:T(8,128)S(1)}, u32[]{:S(2)}, u32[]{:S(2)}) collective-permute-start(f32[8,2,32,128]{3,2,1,0:T(8,128)S(1)} %shard_map.54.refs_0_), channel_id=1, source_target_pairs={{0,96},{32,0},{64,32},{96,64},{1,97},{33,1},{65,33},{97,65},{2,98}... | collective-permute-start | bytes 786440 | tf_op jit(solution)/shard_map/ppermute | solution.py:394
  209.4 15.1 %collective-permute-start.15 = (f32[8,2,32,128]{3,2,1,0:T(8,128)S(1)}, f32[8,2,32,128]{3,2,1,0:T(8,128)S(1)}, u32[]{:S(2)}, u32[]{:S(2)}) collective-permute-start(f32[8,2,32,128]{3,2,1,0:T(8,128)S(1)} %shard_map.54.refs_0_), channel_id=1, source_target_pairs={{0,64},{32,96},{64,0},{96,32},{1,65},{33,97},{65,1},{97,33},{2,66}... | collective-permute-start | bytes 786440 | tf_op jit(solution)/shard_map/ppermute | solution.py:394
  210.0 14.8 %collective-permute-start.14 = (f32[8,2,32,128]{3,2,1,0:T(8,128)S(1)}, f32[8,2,32,128]{3,2,1,0:T(8,128)S(1)}, u32[]{:S(2)}, u32[]{:S(2)}) collective-permute-start(f32[8,2,32,128]{3,2,1,0:T(8,128)S(1)} %shard_map.54.refs_0_), channel_id=1, source_target_pairs={{0,32},{32,64},{64,96},{96,0},{1,33},{33,65},{65,97},{97,1},{2,34}... | collective-permute-start | bytes 786440 | tf_op jit(solution)/shard_map/ppermute | solution.py:394
  221.1 7.0 %collective-permute-start.25 = (f32[32,16,128]{2,1,0:T(8,128)S(1)}, f32[32,16,128]{2,1,0:T(8,128)S(1)}, u32[]{:S(2)}, u32[]{:S(2)}) collective-permute-start(f32[32,16,128]{2,1,0:T(8,128)S(1)} %shard_map.58.refs_4_), channel_id=1, source_target_pairs={{0,96},{32,0},{64,32},{96,64},{1,97},{33,1},{65,33},{97,65},{2,98}... | collective-permute-start | bytes 786440 | tf_op jit(solution)/shard_map/ppermute | solution.py:394
  223.5 7.5 %collective-permute-start.24 = (f32[32,16,128]{2,1,0:T(8,128)S(1)}, f32[32,16,128]{2,1,0:T(8,128)S(1)}, u32[]{:S(2)}, u32[]{:S(2)}) collective-permute-start(f32[32,16,128]{2,1,0:T(8,128)S(1)} %shard_map.58.refs_4_), channel_id=1, source_target_pairs={{0,64},{32,96},{64,0},{96,32},{1,65},{33,97},{65,1},{97,33},{2,66}... | collective-permute-start | bytes 786440 | tf_op jit(solution)/shard_map/ppermute | solution.py:394
  224.4 14.5 %collective-permute-start.23 = (f32[32,16,128]{2,1,0:T(8,128)S(1)}, f32[32,16,128]{2,1,0:T(8,128)S(1)}, u32[]{:S(2)}, u32[]{:S(2)}) collective-permute-start(f32[32,16,128]{2,1,0:T(8,128)S(1)} %shard_map.58.refs_4_), channel_id=1, source_target_pairs={{0,32},{32,64},{64,96},{96,0},{1,33},{33,65},{65,97},{97,1},{2,34}... | collective-permute-start | bytes 786440 | tf_op jit(solution)/shard_map/ppermute | solution.py:394
  (19 other events, 91.8 us)

commit v6 on v5

--- a/solution.py
+++ b/solution.py
@@ -153,7 +153,7 @@
             work[pl.ds(at, ZD), :] = done[i * ZD : (i + 1) * ZD]
         return carry
 
-    lax.fori_loop(0, NY // 4, forward, 0, unroll=8)
+    lax.fori_loop(0, NY // 4, forward, 0, unroll=16)
     fetch.wait()
 
     stores = []
@@ -255,7 +255,7 @@
             out[n] = factors[0] * factors[1]
             return carry
 
-        lax.fori_loop(0, quarter, step, 0, unroll=2)
+        lax.fori_loop(0, quarter, step, 0, unroll=8)
 
 
 def product_last_kernel(*refs):
@@ -272,7 +272,7 @@
         out[t] = factors[0]
         return carry
 
-    lax.fori_loop(0, GRID, step, 0, unroll=4)
+    lax.fori_loop(0, GRID, step, 0, unroll=8)
 
 
 def quarter_kernel(first, second, third, fourth, out):

time: 243 us -> 242 us (level)
  transfers between devices with their start and end apart: 29 -> 29, of which waited for: 19 -> 20; matrix products, arithmetic and copies ran while one was open for 2% -> 2% of each run, Pallas kernels for 12% -> 12%
where the time goes in v6:
time: 242 us; the launch traced here: 241 us
  waiting for transfers between devices  113 us (47%)
  starting transfers between devices  74.9 us (31%)
  Pallas kernels  35.8 us (15%)
  other arithmetic  8.37 us (3%)
  local copies, waits for them, and re-layouts  7.96 us (3%)
    ppermute x26, waiting for transfers between devices, shifted(): return lax.ppermute(value, axis, pairs)  61 us
    all_to_all x3, waiting for transfers between devices, exchange(): return lax.all_to_all(value, axis, 0, 0, tiled=True)  52.1 us
    ppermute x26, starting transfers between devices, shifted(): return lax.ppermute(value, axis, pairs)  45.6 us
    pallas_call x14, Pallas kernels, call(): pl.pallas_call(kernel, out_shape=[(pltpu.HBM if n in far else jax.ShapeDt...  35.7 us
    all_to_all x3, starting transfers between devices, exchange(): return lax.all_to_all(value, axis, 0, 0, tiled=True)  29.3 us
    unnamed x44, local copies, waits for them, and re-layouts  7.77 us
  transfers between devices with their start and end apart: 29, of which 20 were waited for; matrix products, arithmetic and copies ran while one was open for 2% of the time, Pallas kernels for 12%

profile of v6, /device:TPU:1, one launch (start us, length us, event | category | flops | bytes accessed | tf_op | source)
XLA Modules:
  0.0 240.6 jit_solution(4278468830538857335)
XLA Ops:
  4.0 4.6 %collective-permute-start.2 = (s32[2,32]{1,0:T(2,128)S(1)}, s32[2,32]{1,0:T(2,128)S(1)}, u32[]{:S(2)}, u32[]{:S(2)}) collective-permute-start(s32[2,32]{1,0:T(2,128)S(1)} %select_reduce_fusion.2.table.refs_0_), channel_id=1, source_target_pairs={{0,96},{32,0},{64,32},{96,64},{1,97},{33,1},{65,33},{97,65},{2,98}... | collective-permute-start | bytes 776 | tf_op jit(solution)/shard_map/ppermute | solution.py:394
  9.4 4.3 %shard_map.46 = (f32[32,2,4,32,128]{4,3,2,1,0:T(8,128)}, f32[1,4,32,128]{3,2,1,0:T(8,128)}, f32[1,4,32,128]{3,2,1,0:T(8,128)}) custom-call(s32[2,32]{1,0:T(2,128)S(1)} %and_select_fusion.1.table, s32[2]{0:T(128)S(1)} %get-tuple-element.119.last, f32[4096,128]{1,0:T(8,128)} %bitcast.19), custom_call_target="tpu_custom_call" | custom-call | bytes 4194304 | tf_op jit(solution)/shard_map/pallas_call | solution.py:40
  13.7 8.7 %all-to-all-start = ((f32[32,2,4,32,128]{4,3,2,1,0:T(8,128)}), f32[32,2,4,32,128]{4,3,2,1,0:T(8,128)}, u32[]{:S(2)}, u32[]{:S(2)}) async-start(f32[32,2,4,32,128]{4,3,2,1,0:T(8,128)} %get-tuple-element.55), calls=%async_computation | async-start | bytes 8388608 | tf_op jit(solution)/shard_map/all_to_all | solution.py:398
  29.9 43.2 %all-to-all-done.recv = f32[32,2,4,32,128]{4,3,2,1,0:T(8,128)} async-done(((f32[32,2,4,32,128]{4,3,2,1,0:T(8,128)}), f32[32,2,4,32,128]{4,3,2,1,0:T(8,128)}, u32[]{:S(2)}, u32[]{:S(2)}) %all-to-all-start) | async-done | bytes 4194336 | tf_op jit(solution)/shard_map/all_to_all | solution.py:398
  75.2 4.3 %collective-permute-start.5 = (f32[128,16,128]{2,1,0:T(8,128)S(1)}, f32[128,16,128]{2,1,0:T(8,128)S(1)}, u32[]{:S(2)}, u32[]{:S(2)}) collective-permute-start(f32[128,16,128]{2,1,0:T(8,128)S(1)} %get-tuple-element.67.high), channel_id=1, source_target_pairs={{0,1},{1,2},{2,3},{3,4},{4,5},{5,6},{6,7},{7,8},{8,9},{9,10},{10,1... | collective-permute-start | bytes 3145736 | tf_op jit(solution)/shard_map/ppermute | solution.py:394
  79.5 2.6 %collective-permute-start.6 = (f32[128,16,128]{2,1,0:T(8,128)S(1)}, f32[128,16,128]{2,1,0:T(8,128)S(1)}, u32[]{:S(2)}, u32[]{:S(2)}) collective-permute-start(f32[128,16,128]{2,1,0:T(8,128)S(1)} %get-tuple-element.62.low), channel_id=1, source_target_pairs={{1,0},{2,1},{3,2},{4,3},{5,4},{6,5},{7,6},{8,7},{9,8},{10,9},{11,1... | collective-permute-start | bytes 3145736 | tf_op jit(solution)/shard_map/ppermute | solution.py:394
  82.1 2.1 shard_map.48
  84.2 3.0 %collective-permute-start.3 = (f32[128,16,128]{2,1,0:T(8,128)S(1)}, f32[128,16,128]{2,1,0:T(8,128)S(1)}, u32[]{:S(2)}, u32[]{:S(2)}) collective-permute-start(f32[128,16,128]{2,1,0:T(8,128)S(1)} %get-tuple-element.77.high), channel_id=1, source_target_pairs={{0,1},{1,2},{2,3},{3,4},{4,5},{5,6},{6,7},{7,8},{8,9},{9,10},{10,1... | collective-permute-start | bytes 3145736 | tf_op jit(solution)/shard_map/ppermute | solution.py:394
  91.2 4.4 %collective-permute-done.6.bottom = f32[128,16,128]{2,1,0:T(8,128)S(1)} collective-permute-done((f32[128,16,128]{2,1,0:T(8,128)S(1)}, f32[128,16,128]{2,1,0:T(8,128)S(1)}, u32[]{:S(2)}, u32[]{:S(2)}) %collective-permute-start.6) | collective-permute-done | bytes 1048608 | tf_op jit(solution)/shard_map/ppermute | solution.py:394
  95.6 5.8 %shard_map.49 = (f32[128,16,128]{2,1,0:T(8,128)S(1)}, f32[128,16,128]{2,1,0:T(8,128)S(1)}) custom-call(f32[128,16,128]{2,1,0:T(8,128)S(1)} %collective-permute-done.5.top, f32[128,16,128]{2,1,0:T(8,128)S(1)} %get-tuple-element.62.low, f32[128,16,128]{2,1,0:T(8,128)S(1)} %get-tuple-element.67.high, f32[128,16,128]{2,1,0:T(8,128)S(1)} %collective-permute-done.6.bottom, ...), custom_call_target="tpu_custom_call" | custom-call | flops 5368709120 | bytes 8388608 | tf_op jit(solution)/shard_map/pallas_call | solution.py:40
  103.3 3.8 %collective-permute-start.9 = (f32[128,16,128]{2,1,0:T(8,128)S(1)}, f32[128,16,128]{2,1,0:T(8,128)S(1)}, u32[]{:S(2)}, u32[]{:S(2)}) collective-permute-start(f32[128,16,128]{2,1,0:T(8,128)S(1)} %get-tuple-element.74), channel_id=1, source_target_pairs={{0,1},{1,2},{2,3},{3,4},{4,5},{5,6},{6,7},{7,8},{8,9},{9,10},{10,1... | collective-permute-start | bytes 3145736 | tf_op jit(solution)/shard_map/ppermute | solution.py:394
  107.1 5.8 %shard_map.50 = (f32[128,16,128]{2,1,0:T(8,128)S(1)}, f32[128,16,128]{2,1,0:T(8,128)S(1)}) custom-call(f32[128,16,128]{2,1,0:T(8,128)S(1)} %collective-permute-done.3.top, f32[128,16,128]{2,1,0:T(8,128)S(1)} %get-tuple-element.76.low, f32[128,16,128]{2,1,0:T(8,128)S(1)} %get-tuple-element.77.high, f32[128,16,128]{2,1,0:T(8,128)S(1)} %collective-permute-done.4.bottom, ...), custom_call_target="tpu_custom_call" | custom-call | flops 5368709120 | bytes 8388608 | tf_op jit(solution)/shard_map/pallas_call | solution.py:40
  114.9 2.5 %collective-permute-start.8 = (f32[128,16,128]{2,1,0:T(8,128)S(1)}, f32[128,16,128]{2,1,0:T(8,128)S(1)}, u32[]{:S(2)}, u32[]{:S(2)}) collective-permute-start(f32[128,16,128]{2,1,0:T(8,128)S(1)} %get-tuple-element.80), channel_id=1, source_target_pairs={{1,0},{2,1},{3,2},{4,3},{5,4},{6,5},{7,6},{8,7},{9,8},{10,9},{11,1... | collective-permute-start | bytes 3145736 | tf_op jit(solution)/shard_map/ppermute | solution.py:394
  118.7 2.5 %shard_map.51 = (f32[32,2,2,32,128]{4,3,2,1,0:T(8,128)}, f32[2,32,128]{2,1,0:T(8,128)S(1)}) custom-call(s32[2,33]{1,0:T(2,128)S(1)} %select_reduce_fusion.6.table, f32[32,4,16,128]{3,2,1,0:T(8,128)S(1)} %bitcast.27, f32[32,4,16,128]{3,2,1,0:T(8,128)S(1)} %bitcast.21, f32[32,4,16,128]{3,2,1,0:T(8,128)S(1)} %bitcast.23, f32[32,4,16,128]{3,2,1,0:T(8,128)S(1)} %bitcast.25, ...), custom_call_target="tpu_custom_call" | custom-call | flops 1073741824 | bytes 4194304 | tf_op jit(solution)/shard_map/pallas_call | solution.py:40
  121.1 8.8 %collective-permute-done.7 = f32[128,16,128]{2,1,0:T(8,128)S(1)} collective-permute-done((f32[128,16,128]{2,1,0:T(8,128)S(1)}, f32[128,16,128]{2,1,0:T(8,128)S(1)}, u32[]{:S(2)}, u32[]{:S(2)}) %collective-permute-start.7) | collective-permute-done | bytes 1048608 | tf_op jit(solution)/shard_map/ppermute | solution.py:394
  131.0 2.5 %shard_map.52 = (f32[32,2,2,32,128]{4,3,2,1,0:T(8,128)}, f32[2,32,128]{2,1,0:T(8,128)S(1)}) custom-call(s32[2,33]{1,0:T(2,128)S(1)} %select_reduce_fusion.6.table, f32[32,4,16,128]{3,2,1,0:T(8,128)S(1)} %bitcast.33, f32[32,4,16,128]{3,2,1,0:T(8,128)S(1)} %bitcast.29, f32[32,4,16,128]{3,2,1,0:T(8,128)S(1)} %bitcast.31, ...), custom_call_target="tpu_custom_call", output_to_operand_aliasing={{0}: (6, {})} | custom-call | flops 1073741824 | bytes 4194304 | tf_op jit(solution)/shard_map/pallas_call | solution.py:40
  133.5 12.2 %all-to-all-start.1 = ((f32[32,2,2,32,128]{4,3,2,1,0:T(8,128)}), f32[32,2,2,32,128]{4,3,2,1,0:T(8,128)S(1)}, u32[]{:S(2)}, u32[]{:S(2)}) async-start(f32[32,2,2,32,128]{4,3,2,1,0:T(8,128)} %get-tuple-element.83), calls=%async_computation.1 | async-start | bytes 4194304 | tf_op jit(solution)/shard_map/all_to_all | solution.py:398
  162.0 5.6 %collective-permute-done.20.refs_5_ = f32[33,16,128]{2,1,0:T(8,128)S(1)} collective-permute-done((f32[33,16,128]{2,1,0:T(8,128)S(1)}, f32[33,16,128]{2,1,0:T(8,128)S(1)}, u32[]{:S(2)}, u32[]{:S(2)}) %collective-permute-start.20) | collective-permute-done | bytes 270368 | tf_op jit(solution)/shard_map/ppermute | solution.py:394
  167.8 5.8 %collective-permute-done.17.refs_2_ = f32[33,16,128]{2,1,0:T(8,128)S(1)} collective-permute-done((f32[33,16,128]{2,1,0:T(8,128)S(1)}, f32[33,16,128]{2,1,0:T(8,128)S(1)}, u32[]{:S(2)}, u32[]{:S(2)}) %collective-permute-start.17) | collective-permute-done | bytes 270368 | tf_op jit(solution)/shard_map/ppermute | solution.py:394
  173.6 5.5 %collective-permute-done.19.refs_4_ = f32[33,16,128]{2,1,0:T(8,128)S(1)} collective-permute-done((f32[33,16,128]{2,1,0:T(8,128)S(1)}, f32[33,16,128]{2,1,0:T(8,128)S(1)}, u32[]{:S(2)}, u32[]{:S(2)}) %collective-permute-start.19) | collective-permute-done | bytes 270368 | tf_op jit(solution)/shard_map/ppermute | solution.py:394
  180.6 8.4 %all-to-all-start.2 = ((f32[32,4,2,16,128]{4,3,2,1,0:T(8,128)}), f32[32,4,2,16,128]{4,3,2,1,0:T(8,128)}, u32[]{:S(2)}, u32[]{:S(2)}) async-start(f32[32,4,2,16,128]{4,3,2,1,0:T(8,128)} %get-tuple-element.103), calls=%async_computation.2 | async-start | bytes 4194304 | tf_op jit(solution)/shard_map/all_to_all | solution.py:398
  191.3 2.1 collective-permute-start.12
  194.4 4.4 %collective-permute-done.11.second = f32[8,2,32,128]{3,2,1,0:T(8,128)S(1)} collective-permute-done((f32[8,2,32,128]{3,2,1,0:T(8,128)S(1)}, f32[8,2,32,128]{3,2,1,0:T(8,128)S(1)}, u32[]{:S(2)}, u32[]{:S(2)}) %collective-permute-start.11) | collective-permute-done | bytes 262176 | tf_op jit(solution)/shard_map/ppermute | solution.py:394
  198.8 6.4 %collective-permute-done.12.third = f32[8,2,32,128]{3,2,1,0:T(8,128)S(1)} collective-permute-done((f32[8,2,32,128]{3,2,1,0:T(8,128)S(1)}, f32[8,2,32,128]{3,2,1,0:T(8,128)S(1)}, u32[]{:S(2)}, u32[]{:S(2)}) %collective-permute-start.12) | collective-permute-done | bytes 262176 | tf_op jit(solution)/shard_map/ppermute | solution.py:394
  205.3 2.9 %collective-permute-start.16 = (f32[8,2,32,128]{3,2,1,0:T(8,128)S(1)}, f32[8,2,32,128]{3,2,1,0:T(8,128)S(1)}, u32[]{:S(2)}, u32[]{:S(2)}) collective-permute-start(f32[8,2,32,128]{3,2,1,0:T(8,128)S(1)} %shard_map.54.refs_0_), channel_id=1, source_target_pairs={{0,96},{32,0},{64,32},{96,64},{1,97},{33,1},{65,33},{97,65},{2,98}... | collective-permute-start | bytes 786440 | tf_op jit(solution)/shard_map/ppermute | solution.py:394
  208.9 8.9 %all-to-all-done.2.refs_4_ = f32[32,4,2,16,128]{4,3,2,1,0:T(8,128)} async-done(((f32[32,4,2,16,128]{4,3,2,1,0:T(8,128)}), f32[32,4,2,16,128]{4,3,2,1,0:T(8,128)}, u32[]{:S(2)}, u32[]{:S(2)}) %all-to-all-start.2) | async-done | bytes 2097184 | tf_op jit(solution)/shard_map/all_to_all | solution.py:398
  217.8 2.3 shard_map.58.refs_4_
  220.1 2.4 collective-permute-start.25
  223.5 3.6 %collective-permute-done.25.refs_7_ = f32[32,16,128]{2,1,0:T(8,128)S(1)} collective-permute-done((f32[32,16,128]{2,1,0:T(8,128)S(1)}, f32[32,16,128]{2,1,0:T(8,128)S(1)}, u32[]{:S(2)}, u32[]{:S(2)}) %collective-permute-start.25) | collective-permute-done | bytes 262176 | tf_op jit(solution)/shard_map/ppermute | solution.py:394
  227.1 2.9 %collective-permute-done.24.refs_6_ = f32[32,16,128]{2,1,0:T(8,128)S(1)} collective-permute-done((f32[32,16,128]{2,1,0:T(8,128)S(1)}, f32[32,16,128]{2,1,0:T(8,128)S(1)}, u32[]{:S(2)}, u32[]{:S(2)}) %collective-permute-start.24) | collective-permute-done | bytes 262176 | tf_op jit(solution)/shard_map/ppermute | solution.py:394
  230.0 7.8 %collective-permute-done.23.refs_5_ = f32[32,16,128]{2,1,0:T(8,128)S(1)} collective-permute-done((f32[32,16,128]{2,1,0:T(8,128)S(1)}, f32[32,16,128]{2,1,0:T(8,128)S(1)}, u32[]{:S(2)}, u32[]{:S(2)}) %collective-permute-start.23) | collective-permute-done | bytes 262176 | tf_op jit(solution)/shard_map/ppermute | solution.py:394
  237.8 2.8 %shard_map.59 = f32[4096,128]{1,0:T(8,128)} custom-call(s32[4]{0:T(128)S(1)} %and_select_fusion.3.place, f32[4096,128]{1,0:T(8,128)S(1)} %bitcast.20, f32[8,2,32,128]{3,2,1,0:T(8,128)S(1)} %shard_map.54.refs_0_, f32[8,2,32,128]{3,2,1,0:T(8,128)S(1)} %collective-permute-done.14.refs_1_, f32[8,2,32,128]{3,2,1,0:T(8,128)S(1)} %collective-permute-done.15.refs_2_, ...), custom_call_target="tpu_custom_call" | custom-call | bytes 6291456 | tf_op jit(solution)/shard_map/pallas_call | solution.py:40
  (125 shorter events, 47.5 us)
Async XLA Ops:
  4.0 25.9 %collective-permute-start.2 = (s32[2,32]{1,0:T(2,128)S(1)}, s32[2,32]{1,0:T(2,128)S(1)}, u32[]{:S(2)}, u32[]{:S(2)}) collective-permute-start(s32[2,32]{1,0:T(2,128)S(1)} %select_reduce_fusion.2.table.refs_0_), channel_id=1, source_target_pairs={{0,96},{32,0},{64,32},{96,64},{1,97},{33,1},{65,33},{97,65},{2,98}... | collective-permute-start | bytes 776 | tf_op jit(solution)/shard_map/ppermute | solution.py:394
  8.7 21.2 %collective-permute-start.1 = (s32[2,32]{1,0:T(2,128)S(1)}, s32[2,32]{1,0:T(2,128)S(1)}, u32[]{:S(2)}, u32[]{:S(2)}) collective-permute-start(s32[2,32]{1,0:T(2,128)S(1)} %select_reduce_fusion.2.table.refs_0_), channel_id=1, source_target_pairs={{0,64},{32,96},{64,0},{96,32},{1,65},{33,97},{65,1},{97,33},{2,66}... | collective-permute-start | bytes 776 | tf_op jit(solution)/shard_map/ppermute | solution.py:394
  8.7 21.2 %collective-permute-start = (s32[2,32]{1,0:T(2,128)S(1)}, s32[2,32]{1,0:T(2,128)S(1)}, u32[]{:S(2)}, u32[]{:S(2)}) collective-permute-start(s32[2,32]{1,0:T(2,128)S(1)} %select_reduce_fusion.2.table.refs_0_), channel_id=1, source_target_pairs={{0,32},{32,64},{64,96},{96,0},{1,33},{33,65},{65,97},{97,1},{2,34}... | collective-permute-start | bytes 776 | tf_op jit(solution)/shard_map/ppermute | solution.py:394
  13.7 59.4 %all-to-all-start = ((f32[32,2,4,32,128]{4,3,2,1,0:T(8,128)}), f32[32,2,4,32,128]{4,3,2,1,0:T(8,128)}, u32[]{:S(2)}, u32[]{:S(2)}) async-start(f32[32,2,4,32,128]{4,3,2,1,0:T(8,128)} %get-tuple-element.55), calls=%async_computation | async-start | bytes 8388608 | tf_op jit(solution)/shard_map/all_to_all | solution.py:398
  22.4 50.7 %copy-start.16 = (f32[1,4,32,128]{3,2,1,0:T(8,128)S(1)}, f32[1,4,32,128]{3,2,1,0:T(8,128)}, u32[]{:S(2)}) copy-start(f32[1,4,32,128]{3,2,1,0:T(8,128)} %get-tuple-element.61.kept) | copy-start | bytes 196612
  75.2 16.0 %collective-permute-start.5 = (f32[128,16,128]{2,1,0:T(8,128)S(1)}, f32[128,16,128]{2,1,0:T(8,128)S(1)}, u32[]{:S(2)}, u32[]{:S(2)}) collective-permute-start(f32[128,16,128]{2,1,0:T(8,128)S(1)} %get-tuple-element.67.high), channel_id=1, source_target_pairs={{0,1},{1,2},{2,3},{3,4},{4,5},{5,6},{6,7},{7,8},{8,9},{9,10},{10,1... | collective-permute-start | bytes 3145736 | tf_op jit(solution)/shard_map/ppermute | solution.py:394
  79.5 16.1 %collective-permute-start.6 = (f32[128,16,128]{2,1,0:T(8,128)S(1)}, f32[128,16,128]{2,1,0:T(8,128)S(1)}, u32[]{:S(2)}, u32[]{:S(2)}) collective-permute-start(f32[128,16,128]{2,1,0:T(8,128)S(1)} %get-tuple-element.62.low), channel_id=1, source_target_pairs={{1,0},{2,1},{3,2},{4,3},{5,4},{6,5},{7,6},{8,7},{9,8},{10,9},{11,1... | collective-permute-start | bytes 3145736 | tf_op jit(solution)/shard_map/ppermute | solution.py:394
  84.2 22.9 %collective-permute-start.3 = (f32[128,16,128]{2,1,0:T(8,128)S(1)}, f32[128,16,128]{2,1,0:T(8,128)S(1)}, u32[]{:S(2)}, u32[]{:S(2)}) collective-permute-start(f32[128,16,128]{2,1,0:T(8,128)S(1)} %get-tuple-element.77.high), channel_id=1, source_target_pairs={{0,1},{1,2},{2,3},{3,4},{4,5},{5,6},{6,7},{7,8},{8,9},{9,10},{10,1... | collective-permute-start | bytes 3145736 | tf_op jit(solution)/shard_map/ppermute | solution.py:394
  87.2 19.9 %collective-permute-start.4 = (f32[128,16,128]{2,1,0:T(8,128)S(1)}, f32[128,16,128]{2,1,0:T(8,128)S(1)}, u32[]{:S(2)}, u32[]{:S(2)}) collective-permute-start(f32[128,16,128]{2,1,0:T(8,128)S(1)} %get-tuple-element.76.low), channel_id=1, source_target_pairs={{1,0},{2,1},{3,2},{4,3},{5,4},{6,5},{7,6},{8,7},{9,8},{10,9},{11,1... | collective-permute-start | bytes 3145736 | tf_op jit(solution)/shard_map/ppermute | solution.py:394
  101.4 16.7 %collective-permute-start.10 = (f32[128,16,128]{2,1,0:T(8,128)S(1)}, f32[128,16,128]{2,1,0:T(8,128)S(1)}, u32[]{:S(2)}, u32[]{:S(2)}) collective-permute-start(f32[128,16,128]{2,1,0:T(8,128)S(1)} %get-tuple-element.73), channel_id=1, source_target_pairs={{1,0},{2,1},{3,2},{4,3},{5,4},{6,5},{7,6},{8,7},{9,8},{10,9},{11,1... | collective-permute-start | bytes 3145736 | tf_op jit(solution)/shard_map/ppermute | solution.py:394
  103.3 15.4 %collective-permute-start.9 = (f32[128,16,128]{2,1,0:T(8,128)S(1)}, f32[128,16,128]{2,1,0:T(8,128)S(1)}, u32[]{:S(2)}, u32[]{:S(2)}) collective-permute-start(f32[128,16,128]{2,1,0:T(8,128)S(1)} %get-tuple-element.74), channel_id=1, source_target_pairs={{0,1},{1,2},{2,3},{3,4},{4,5},{5,6},{6,7},{7,8},{8,9},{9,10},{10,1... | collective-permute-start | bytes 3145736 | tf_op jit(solution)/shard_map/ppermute | solution.py:394
  112.9 18.1 %copy-start.7 = (f32[128,16,128]{2,1,0:T(8,128)}, f32[128,16,128]{2,1,0:T(8,128)S(1)}, u32[]{:S(2)}) copy-start(f32[128,16,128]{2,1,0:T(8,128)S(1)} %get-tuple-element.80) | copy-start | bytes 3145732
  112.9 17.0 %collective-permute-start.7 = (f32[128,16,128]{2,1,0:T(8,128)S(1)}, f32[128,16,128]{2,1,0:T(8,128)S(1)}, u32[]{:S(2)}, u32[]{:S(2)}) collective-permute-start(f32[128,16,128]{2,1,0:T(8,128)S(1)} %get-tuple-element.79), channel_id=1, source_target_pairs={{0,1},{1,2},{2,3},{3,4},{4,5},{5,6},{6,7},{7,8},{8,9},{9,10},{10,1... | collective-permute-start | bytes 3145736 | tf_op jit(solution)/shard_map/ppermute | solution.py:394
  114.9 16.1 %collective-permute-start.8 = (f32[128,16,128]{2,1,0:T(8,128)S(1)}, f32[128,16,128]{2,1,0:T(8,128)S(1)}, u32[]{:S(2)}, u32[]{:S(2)}) collective-permute-start(f32[128,16,128]{2,1,0:T(8,128)S(1)} %get-tuple-element.80), channel_id=1, source_target_pairs={{1,0},{2,1},{3,2},{4,3},{5,4},{6,5},{7,6},{8,7},{9,8},{10,9},{11,1... | collective-permute-start | bytes 3145736 | tf_op jit(solution)/shard_map/ppermute | solution.py:394
  133.5 47.1 %all-to-all-start.1 = ((f32[32,2,2,32,128]{4,3,2,1,0:T(8,128)}), f32[32,2,2,32,128]{4,3,2,1,0:T(8,128)S(1)}, u32[]{:S(2)}, u32[]{:S(2)}) async-start(f32[32,2,2,32,128]{4,3,2,1,0:T(8,128)} %get-tuple-element.83), calls=%async_computation.1 | async-start | bytes 4194304 | tf_op jit(solution)/shard_map/all_to_all | solution.py:398
  152.4 9.1 %collective-permute-start.18 = (f32[33,16,128]{2,1,0:T(8,128)S(1)}, f32[33,16,128]{2,1,0:T(8,128)S(1)}, u32[]{:S(2)}, u32[]{:S(2)}) collective-permute-start(f32[33,16,128]{2,1,0:T(8,128)S(1)} %get-tuple-element.97), channel_id=1, source_target_pairs={{0,32},{32,64},{64,96},{96,0},{1,33},{33,65},{65,97},{97,1},{2,34}... | collective-permute-start | bytes 811016 | tf_op jit(solution)/shard_map/ppermute | solution.py:394
  154.4 13.1 %collective-permute-start.20 = (f32[33,16,128]{2,1,0:T(8,128)S(1)}, f32[33,16,128]{2,1,0:T(8,128)S(1)}, u32[]{:S(2)}, u32[]{:S(2)}) collective-permute-start(f32[33,16,128]{2,1,0:T(8,128)S(1)} %get-tuple-element.99), channel_id=1, source_target_pairs={{0,64},{32,96},{64,0},{96,32},{1,65},{33,97},{65,1},{97,33},{2,66}... | collective-permute-start | bytes 811016 | tf_op jit(solution)/shard_map/ppermute | solution.py:394
  155.3 12.4 %collective-permute-start.22 = (f32[33,16,128]{2,1,0:T(8,128)S(1)}, f32[33,16,128]{2,1,0:T(8,128)S(1)}, u32[]{:S(2)}, u32[]{:S(2)}) collective-permute-start(f32[33,16,128]{2,1,0:T(8,128)S(1)} %get-tuple-element.101), channel_id=1, source_target_pairs={{0,96},{32,0},{64,32},{96,64},{1,97},{33,1},{65,33},{97,65},{2,98}... | collective-permute-start | bytes 811016 | tf_op jit(solution)/shard_map/ppermute | solution.py:394
  158.5 15.1 %collective-permute-start.17 = (f32[33,16,128]{2,1,0:T(8,128)S(1)}, f32[33,16,128]{2,1,0:T(8,128)S(1)}, u32[]{:S(2)}, u32[]{:S(2)}) collective-permute-start(f32[33,16,128]{2,1,0:T(8,128)S(1)} %get-tuple-element.96), channel_id=1, source_target_pairs={{0,32},{32,64},{64,96},{96,0},{1,33},{33,65},{65,97},{97,1},{2,34}... | collective-permute-start | bytes 811016 | tf_op jit(solution)/shard_map/ppermute | solution.py:394
  158.6 20.5 %collective-permute-start.19 = (f32[33,16,128]{2,1,0:T(8,128)S(1)}, f32[33,16,128]{2,1,0:T(8,128)S(1)}, u32[]{:S(2)}, u32[]{:S(2)}) collective-permute-start(f32[33,16,128]{2,1,0:T(8,128)S(1)} %get-tuple-element.98), channel_id=1, source_target_pairs={{0,64},{32,96},{64,0},{96,32},{1,65},{33,97},{65,1},{97,33},{2,66}... | collective-permute-start | bytes 811016 | tf_op jit(solution)/shard_map/ppermute | solution.py:394
  161.5 17.8 %collective-permute-start.21 = (f32[33,16,128]{2,1,0:T(8,128)S(1)}, f32[33,16,128]{2,1,0:T(8,128)S(1)}, u32[]{:S(2)}, u32[]{:S(2)}) collective-permute-start(f32[33,16,128]{2,1,0:T(8,128)S(1)} %get-tuple-element.100), channel_id=1, source_target_pairs={{0,96},{32,0},{64,32},{96,64},{1,97},{33,1},{65,33},{97,65},{2,98}... | collective-permute-start | bytes 811016 | tf_op jit(solution)/shard_map/ppermute | solution.py:394
  180.6 37.2 %all-to-all-start.2 = ((f32[32,4,2,16,128]{4,3,2,1,0:T(8,128)}), f32[32,4,2,16,128]{4,3,2,1,0:T(8,128)}, u32[]{:S(2)}, u32[]{:S(2)}) async-start(f32[32,4,2,16,128]{4,3,2,1,0:T(8,128)} %get-tuple-element.103), calls=%async_computation.2 | async-start | bytes 4194304 | tf_op jit(solution)/shard_map/all_to_all | solution.py:398
  189.9 47.9 %copy-start = (f32[32,128,128]{2,1,0:T(8,128)S(1)}, f32[32,128,128]{2,1,0:T(8,128)}, u32[]{:S(2)}) copy-start(f32[32,128,128]{2,1,0:T(8,128)} %param.4) | copy-start | bytes 6291460
  189.9 8.9 %collective-permute-start.11 = (f32[8,2,32,128]{3,2,1,0:T(8,128)S(1)}, f32[8,2,32,128]{3,2,1,0:T(8,128)S(1)}, u32[]{:S(2)}, u32[]{:S(2)}) collective-permute-start(f32[8,2,32,128]{3,2,1,0:T(8,128)S(1)} %get-tuple-element.87), channel_id=1, source_target_pairs={{0,32},{32,64},{64,96},{96,0},{1,33},{33,65},{65,97},{97,1},{2,34}... | collective-permute-start | bytes 786440 | tf_op jit(solution)/shard_map/ppermute | solution.py:394
  191.3 13.9 %collective-permute-start.12 = (f32[8,2,32,128]{3,2,1,0:T(8,128)S(1)}, f32[8,2,32,128]{3,2,1,0:T(8,128)S(1)}, u32[]{:S(2)}, u32[]{:S(2)}) collective-permute-start(f32[8,2,32,128]{3,2,1,0:T(8,128)S(1)} %get-tuple-element.88), channel_id=1, source_target_pairs={{0,64},{32,96},{64,0},{96,32},{1,65},{33,97},{65,1},{97,33},{2,66}... | collective-permute-start | bytes 786440 | tf_op jit(solution)/shard_map/ppermute | solution.py:394
  193.4 11.8 %collective-permute-start.13 = (f32[8,2,32,128]{3,2,1,0:T(8,128)S(1)}, f32[8,2,32,128]{3,2,1,0:T(8,128)S(1)}, u32[]{:S(2)}, u32[]{:S(2)}) collective-permute-start(f32[8,2,32,128]{3,2,1,0:T(8,128)S(1)} %get-tuple-element.89), channel_id=1, source_target_pairs={{0,96},{32,0},{64,32},{96,64},{1,97},{33,1},{65,33},{97,65},{2,98}... | collective-permute-start | bytes 786440 | tf_op jit(solution)/shard_map/ppermute | solution.py:394
  205.3 18.0 %collective-permute-start.16 = (f32[8,2,32,128]{3,2,1,0:T(8,128)S(1)}, f32[8,2,32,128]{3,2,1,0:T(8,128)S(1)}, u32[]{:S(2)}, u32[]{:S(2)}) collective-permute-start(f32[8,2,32,128]{3,2,1,0:T(8,128)S(1)} %shard_map.54.refs_0_), channel_id=1, source_target_pairs={{0,96},{32,0},{64,32},{96,64},{1,97},{33,1},{65,33},{97,65},{2,98}... | collective-permute-start | bytes 786440 | tf_op jit(solution)/shard_map/ppermute | solution.py:394
  208.2 15.2 %collective-permute-start.15 = (f32[8,2,32,128]{3,2,1,0:T(8,128)S(1)}, f32[8,2,32,128]{3,2,1,0:T(8,128)S(1)}, u32[]{:S(2)}, u32[]{:S(2)}) collective-permute-start(f32[8,2,32,128]{3,2,1,0:T(8,128)S(1)} %shard_map.54.refs_0_), channel_id=1, source_target_pairs={{0,64},{32,96},{64,0},{96,32},{1,65},{33,97},{65,1},{97,33},{2,66}... | collective-permute-start | bytes 786440 | tf_op jit(solution)/shard_map/ppermute | solution.py:394
  208.8 14.8 %collective-permute-start.14 = (f32[8,2,32,128]{3,2,1,0:T(8,128)S(1)}, f32[8,2,32,128]{3,2,1,0:T(8,128)S(1)}, u32[]{:S(2)}, u32[]{:S(2)}) collective-permute-start(f32[8,2,32,128]{3,2,1,0:T(8,128)S(1)} %shard_map.54.refs_0_), channel_id=1, source_target_pairs={{0,32},{32,64},{64,96},{96,0},{1,33},{33,65},{65,97},{97,1},{2,34}... | collective-permute-start | bytes 786440 | tf_op jit(solution)/shard_map/ppermute | solution.py:394
  220.1 7.0 %collective-permute-start.25 = (f32[32,16,128]{2,1,0:T(8,128)S(1)}, f32[32,16,128]{2,1,0:T(8,128)S(1)}, u32[]{:S(2)}, u32[]{:S(2)}) collective-permute-start(f32[32,16,128]{2,1,0:T(8,128)S(1)} %shard_map.58.refs_4_), channel_id=1, source_target_pairs={{0,96},{32,0},{64,32},{96,64},{1,97},{33,1},{65,33},{97,65},{2,98}... | collective-permute-start | bytes 786440 | tf_op jit(solution)/shard_map/ppermute | solution.py:394
  222.4 7.5 %collective-permute-start.24 = (f32[32,16,128]{2,1,0:T(8,128)S(1)}, f32[32,16,128]{2,1,0:T(8,128)S(1)}, u32[]{:S(2)}, u32[]{:S(2)}) collective-permute-start(f32[32,16,128]{2,1,0:T(8,128)S(1)} %shard_map.58.refs_4_), channel_id=1, source_target_pairs={{0,64},{32,96},{64,0},{96,32},{1,65},{33,97},{65,1},{97,33},{2,66}... | collective-permute-start | bytes 786440 | tf_op jit(solution)/shard_map/ppermute | solution.py:394
  223.3 14.5 %collective-permute-start.23 = (f32[32,16,128]{2,1,0:T(8,128)S(1)}, f32[32,16,128]{2,1,0:T(8,128)S(1)}, u32[]{:S(2)}, u32[]{:S(2)}) collective-permute-start(f32[32,16,128]{2,1,0:T(8,128)S(1)} %shard_map.58.refs_4_), channel_id=1, source_target_pairs={{0,32},{32,64},{64,96},{96,0},{1,33},{33,65},{65,97},{97,1},{2,34}... | collective-permute-start | bytes 786440 | tf_op jit(solution)/shard_map/ppermute | solution.py:394
  (19 other events, 91.3 us)
